TPU v7x, 32 devices: a whole 2x2x4 slice. The times are simulated.
32 devices in a mesh: dp: 8 (over z, x), tensor: 4 (over y, core).
Axes of the slice: x: 2, y: 2, z: 4, core: 2. Of those that a mesh axis runs over, the one named last changes fastest.
Arguments:
- tokens: bfloat16 [20480, 768], P(('dp', 'tensor')), may hold values from -6 to 6
- segment_ids: int32 [20480], P('dp'), may hold values from 0 to 8, as said below
- lengths: int32 [40], P('dp'), may hold values from 410 to 512, as said below
- w_query: bfloat16 [768, 768], P(None, 'tensor'), may hold values from -0.21875 to 0.21875
- b_query: float32 [768], P('tensor'), may hold values from -3 to 3
- w_key: bfloat16 [768, 768], P(None, 'tensor'), may hold values from -0.21875 to 0.21875
- w_value: bfloat16 [768, 768], P(None, 'tensor'), may hold values from -0.21875 to 0.21875
- b_value: float32 [768], P('tensor'), may hold values from -3 to 3
- w_output: bfloat16 [768, 768], P('tensor'), may hold values from -1.5 to 1.5
- b_output: float32 [768], replicated, may hold values from -2 to 2
- first_gain: float32 [768], replicated, may hold values from 0.5 to 1.5
- first_shift: float32 [768], replicated, may hold values from -2 to 2
- w_inner: bfloat16 [768, 3072], P(None, 'tensor'), may hold values from -0.21875 to 0.21875
- b_inner: float32 [3072], P('tensor'), may hold values from -3 to 3
- w_outer: bfloat16 [3072, 768], P('tensor'), may hold values from -0.109375 to 0.109375
- b_outer: float32 [768], replicated, may hold values from -2 to 2
- second_gain: float32 [768], replicated, may hold values from 0.5 to 1.5
- second_shift: float32 [768], replicated, may hold values from -2 to 2
- cotangent: bfloat16 [20480, 768], P(('dp', 'tensor')), may hold values from -6 to 6
Outputs:
- output: bfloat16 [20480, 768], P(('dp', 'tensor'))
- grad_tokens: bfloat16 [20480, 768], P(('dp', 'tensor'))
- grad_w_query: float32 [768, 768], P(None, 'tensor')
- grad_b_query: float32 [768], P('tensor')
- grad_w_key: float32 [768, 768], P(None, 'tensor')
- grad_w_value: float32 [768, 768], P(None, 'tensor')
- grad_b_value: float32 [768], P('tensor')
- grad_w_output: float32 [768, 768], P('tensor')
- grad_b_output: float32 [768], P('tensor')
- grad_first_gain: float32 [768], P('tensor')
- grad_first_shift: float32 [768], P('tensor')
- grad_w_inner: float32 [768, 3072], P(None, 'tensor')
- grad_b_inner: float32 [3072], P('tensor')
- grad_w_outer: float32 [3072, 768], P('tensor')
- grad_b_outer: float32 [768], P('tensor')
- grad_second_gain: float32 [768], P('tensor')
- grad_second_shift: float32 [768], P('tensor')
Inputs may be any that keep to these rules, and one draw needn't show every extreme that they name: `segment_ids`: along each packed sequence of 512 positions the ids start at 0, never fall, and rise by at most one a position; the first sequence reaches the largest id. `lengths`: live positions of each packed sequence; the first sequence is full.
All inputs are finite; a program needn't handle non-finite values.
Results may differ from a plain program's by a relative error of at most 0.019.
Values may be sent and summed in bfloat16 or wider, within the bound.
A program may use at most 128 MiB of HBM per device.

v0:
```python
import math

import jax
import jax.numpy as jnp
from jax import lax
from jax.sharding import PartitionSpec as P

HD = 64
LEN = 512


EPSILON = 1e-12
NEGATIVE = -1000000000.0


def normalize(value, gain, shift):
    average = jnp.mean(value, axis=-1, keepdims=True)
    centered = value - average
    variance = jnp.mean(centered * centered, axis=-1, keepdims=True)
    inverse = lax.rsqrt(variance + EPSILON)
    unit = centered * inverse
    return (unit * gain + shift, unit, inverse)


def norm_backward(grad, unit, inverse, gain):
    scaled = grad * gain
    first_mean = jnp.mean(scaled, axis=-1, keepdims=True)
    second_mean = jnp.mean(scaled * unit, axis=-1, keepdims=True)
    result = inverse * (scaled - first_mean - unit * second_mean)
    return (result, jnp.sum(grad * unit, axis=0), jnp.sum(grad, axis=0))


def gelu_value(inner):
    return 0.5 * inner * (1.0 + lax.erf(inner * (1.0 / math.sqrt(2.0))))


def gelu_slope(inner):
    cumulative = 0.5 * (1.0 + lax.erf(inner * (1.0 / math.sqrt(2.0))))
    return cumulative + inner * jnp.exp(-0.5 * inner * inner) * (1.0 / math.sqrt(2.0 * math.pi))


def allowed_mask(segments, length):
    places = jnp.arange(segments.shape[0])
    same = segments[:, None] == segments[None, :]
    live = places[None, :] < length
    return same & live | (places[:, None] == places[None, :])


def split_heads(rows):
    return rows.reshape(rows.shape[0], rows.shape[1] // HD, HD)


def attention_logits(query_rows, key_rows, segments, length):
    scores = jnp.einsum(
        "qhd,khd->hqk",
        split_heads(query_rows),
        split_heads(key_rows),
        preferred_element_type=jnp.float32,
    )
    return jnp.where(allowed_mask(segments, length)[None], scores * (1.0 / math.sqrt(HD)), NEGATIVE)


def forward_attend(block):
    query_rows, key_rows, value_rows, segments, length = block
    logits = attention_logits(query_rows, key_rows, segments, length)
    peak = jnp.max(logits, axis=-1, keepdims=True)
    powers = jnp.exp(logits - peak)
    total = jnp.sum(powers, axis=-1, keepdims=True)
    weights = (powers / total).astype(jnp.bfloat16)
    context = jnp.einsum(
        "hqk,khd->qhd", weights, split_heads(value_rows), preferred_element_type=jnp.float32
    )
    log_total = (peak + jnp.log(total))[..., 0]
    return (context.reshape(query_rows.shape).astype(jnp.bfloat16), log_total)


def backward_attend(block):
    query_rows, key_rows, value_rows, grad_rows, segments, length, log_total = block
    logits = attention_logits(query_rows, key_rows, segments, length)
    probs = jnp.exp(logits - log_total[..., None])
    grad_heads = split_heads(grad_rows)
    grad_probs = jnp.einsum(
        "qhd,khd->hqk", grad_heads, split_heads(value_rows), preferred_element_type=jnp.float32
    )
    across = jnp.sum(probs * grad_probs, axis=-1, keepdims=True)
    grad_scores = (probs * (grad_probs - across) * (1.0 / math.sqrt(HD))).astype(jnp.bfloat16)
    grad_query = jnp.einsum(
        "hqk,khd->qhd", grad_scores, split_heads(key_rows), preferred_element_type=jnp.float32
    )
    grad_key = jnp.einsum(
        "hqk,qhd->khd", grad_scores, split_heads(query_rows), preferred_element_type=jnp.float32
    )
    grad_value = jnp.einsum(
        "hqk,qhd->khd", probs.astype(jnp.bfloat16), grad_heads, preferred_element_type=jnp.float32
    )
    shape = query_rows.shape
    joined = jnp.concatenate(
        [grad_query.reshape(shape), grad_key.reshape(shape), grad_value.reshape(shape)], axis=1
    )
    return joined.astype(jnp.bfloat16)


def shards(
    tokens,
    segment_ids,
    lengths,
    w_query,
    b_query,
    w_key,
    w_value,
    b_value,
    w_output,
    b_output,
    first_gain,
    first_shift,
    w_inner,
    b_inner,
    w_outer,
    b_outer,
    second_gain,
    second_shift,
    cotangent,
):
    parts = lax.axis_size("tensor")
    width = w_query.shape[1]
    count = segment_ids.shape[0] // LEN
    joined = jnp.concatenate([w_query, w_key, w_value], axis=1)

    def by_sequence(rows_all):
        return rows_all.reshape(count, LEN, rows_all.shape[1])

    whole = lax.all_gather(tokens, "tensor", axis=0, tiled=True)
    projected = jnp.dot(whole, joined, preferred_element_type=jnp.float32)
    query_rows = (projected[:, :width] + b_query).astype(jnp.bfloat16)
    key_rows = projected[:, width : 2 * width].astype(jnp.bfloat16)
    value_rows = (projected[:, 2 * width :] + b_value).astype(jnp.bfloat16)
    segments = segment_ids.reshape(count, LEN)
    context, log_total = lax.map(
        forward_attend,
        (
            by_sequence(query_rows),
            by_sequence(key_rows),
            by_sequence(value_rows),
            segments,
            lengths,
        ),
    )
    context = context.reshape(count * LEN, width)
    piece = context
    attended = lax.psum_scatter(
        jnp.dot(piece, w_output, preferred_element_type=jnp.float32),
        "tensor",
        scatter_dimension=0,
        tiled=True,
    )
    first_full, first_unit, first_inverse = normalize(
        tokens.astype(jnp.float32) + attended + b_output, first_gain, first_shift
    )
    first_out = first_full.astype(jnp.bfloat16)
    ffn_rows = lax.all_gather(first_out, "tensor", axis=0, tiled=True)
    inner = jnp.dot(ffn_rows, w_inner, preferred_element_type=jnp.float32) + b_inner
    hidden = gelu_value(inner).astype(jnp.bfloat16)
    piece = hidden
    feed_out = lax.psum_scatter(
        jnp.dot(piece, w_outer, preferred_element_type=jnp.float32).astype(jnp.bfloat16),
        "tensor",
        scatter_dimension=0,
        tiled=True,
    ).astype(jnp.float32)
    second_full, second_unit, second_inverse = normalize(
        first_out.astype(jnp.float32) + feed_out + b_outer, second_gain, second_shift
    )
    output = second_full.astype(jnp.bfloat16)
    grad_second, grad_second_gain, grad_second_shift = norm_backward(
        cotangent.astype(jnp.float32), second_unit, second_inverse, second_gain
    )
    grad_feed = grad_second.astype(jnp.bfloat16)
    grad_b_outer = jnp.sum(grad_feed.astype(jnp.float32), axis=0)
    feed_grads = lax.all_gather(grad_feed, "tensor", axis=0, tiled=True)
    grad_w_outer = jnp.einsum("gf,gd->fd", hidden, feed_grads, preferred_element_type=jnp.float32)
    grad_hidden = jnp.einsum("gd,fd->gf", feed_grads, w_outer, preferred_element_type=jnp.float32)
    grad_inner = (grad_hidden * gelu_slope(inner)).astype(jnp.bfloat16)
    grad_b_inner = jnp.sum(grad_inner.astype(jnp.float32), axis=0)
    grad_w_inner = jnp.einsum("gd,gf->df", ffn_rows, grad_inner, preferred_element_type=jnp.float32)
    piece = grad_inner
    grad_first = grad_second + lax.psum_scatter(
        jnp.einsum("gf,df->gd", piece, w_inner, preferred_element_type=jnp.float32).astype(
            jnp.bfloat16
        ),
        "tensor",
        scatter_dimension=0,
        tiled=True,
    ).astype(jnp.float32)
    grad_branch_full, grad_first_gain, grad_first_shift = norm_backward(
        grad_first, first_unit, first_inverse, first_gain
    )
    grad_branch = grad_branch_full.astype(jnp.bfloat16)
    grad_b_output = jnp.sum(grad_branch.astype(jnp.float32), axis=0)
    branch_rows = lax.all_gather(grad_branch, "tensor", axis=0, tiled=True)
    grad_w_output = jnp.einsum(
        "gc,gd->cd", context, branch_rows, preferred_element_type=jnp.float32
    )
    grad_context = jnp.einsum(
        "gd,cd->gc", branch_rows, w_output, preferred_element_type=jnp.float32
    ).astype(jnp.bfloat16)
    grad_joined = lax.map(
        backward_attend,
        (
            by_sequence(query_rows),
            by_sequence(key_rows),
            by_sequence(value_rows),
            by_sequence(grad_context),
            segments,
            lengths,
            log_total,
        ),
    )
    grad_joined = grad_joined.reshape(count * LEN, 3 * width)
    grad_w_joined = jnp.einsum("gd,gc->dc", whole, grad_joined, preferred_element_type=jnp.float32)
    grad_bias_all = jnp.sum(grad_joined.astype(jnp.float32), axis=0)
    grad_b_query = grad_bias_all[:width]
    grad_b_value = grad_bias_all[2 * width :]
    input_terms = jnp.einsum("gc,dc->gd", grad_joined, joined, preferred_element_type=jnp.float32)
    small = jnp.stack(
        [
            grad_b_output,
            grad_first_gain,
            grad_first_shift,
            grad_b_outer,
            grad_second_gain,
            grad_second_shift,
        ]
    )
    small_flat = small.reshape(6, parts, small.shape[1] // parts).transpose(1, 0, 2).reshape(-1)
    input_share, small_share = (
        lax.psum_scatter(
            input_terms.astype(jnp.bfloat16), "tensor", scatter_dimension=0, tiled=True
        ).astype(jnp.float32),
        lax.psum_scatter(
            small_flat.astype(jnp.bfloat16), "tensor", scatter_dimension=0, tiled=True
        ).astype(jnp.float32),
    )
    grad_tokens = (grad_branch_full + input_share).astype(jnp.bfloat16)
    small_share = small_share.reshape(6, small_share.shape[0] // 6)
    (
        grad_w_joined,
        grad_b_query,
        grad_b_value,
        grad_w_output,
        grad_w_inner,
        grad_b_inner,
        grad_w_outer,
        small_share,
    ) = lax.psum(
        (
            grad_w_joined,
            grad_b_query,
            grad_b_value,
            grad_w_output,
            grad_w_inner,
            grad_b_inner,
            grad_w_outer,
            small_share,
        ),
        "dp",
    )
    return (
        output,
        grad_tokens,
        grad_w_joined[:, :width],
        grad_b_query,
        grad_w_joined[:, width : 2 * width],
        grad_w_joined[:, 2 * width :],
        grad_b_value,
        grad_w_output,
        small_share[0],
        small_share[1],
        small_share[2],
        grad_w_inner,
        grad_b_inner,
        grad_w_outer,
        small_share[3],
        small_share[4],
        small_share[5],
    )


def solution(mesh):
    in_specs = (
        P(("dp", "tensor"), None),
        P("dp"),
        P("dp"),
        P(None, "tensor"),
        P("tensor"),
        P(None, "tensor"),
        P(None, "tensor"),
        P("tensor"),
        P("tensor", None),
        P(),
        P(),
        P(),
        P(None, "tensor"),
        P("tensor"),
        P("tensor", None),
        P(),
        P(),
        P(),
        P(("dp", "tensor"), None),
    )
    out_specs = (
        P(("dp", "tensor"), None),
        P(("dp", "tensor"), None),
        P(None, "tensor"),
        P("tensor"),
        P(None, "tensor"),
        P(None, "tensor"),
        P("tensor"),
        P("tensor", None),
        P("tensor"),
        P("tensor"),
        P("tensor"),
        P(None, "tensor"),
        P("tensor"),
        P("tensor", None),
        P("tensor"),
        P("tensor"),
        P("tensor"),
    )
    return jax.shard_map(shards, mesh=mesh, in_specs=in_specs, out_specs=out_specs, check_vma=False)
```

profile of v0, /device:TPU:0, one launch (start us, length us, event | category | flops | bytes accessed | tf_op | source)
XLA Modules:
  0.0 827.0 jit_solution(1804968826815909880)
XLA Ops:
  10.7 34.6 %all-gather.5.cloned.1.call-done = bf16[2560,768]{1,0:T(8,128)(2,1)} async-done(((bf16[640,768]{1,0:T(8,128)(2,1)}), bf16[2560,768]{1,0:T(8,128)(2,1)}) %all-gather.5.cloned.1.call-update) | async-done | bytes 3932176 | tf_op jit(solution)/shard_map/all_gather | solution.py:132
  45.3 4.6 convolution_bitcast_fusion
  60.1 37.0 %while.22 = (s32[]{:T(128)}, bf16[5,512,192]{1,2,0:T(8,128)(2,1)S(1)}, f32[5,3,512]{2,1,0:T(4,128)}, bf16[5,512,192]{1,2,0:T(8,128)(2,1)}, s32[5,512]{1,0:T(8,12...) while((s32[]{:T(128)}, ...), condition=%wide.region_3.4_spmd, body=%wide.region_0.3_spmd.sunk | while | flops 211909632 | bytes 12903561 | solution.py:138
  97.7 5.4 fusion.60
  103.2 69.1 %reduce-scatter.5.cloned.1.call-done = f32[640,768]{1,0:T(8,128)} async-done(((f32[2560,768]{1,0:T(8,128)}), f32[640,768]{1,0:T(8,128)}) %reduce-scatter.5.cloned.1.call-update) | async-done | bytes 1966096 | tf_op jit(solution)/shard_map/reduce_scatter | solution.py:150
  176.7 32.9 %all-gather.7.cloned.1.call-done = bf16[2560,768]{1,0:T(8,128)(2,1)} async-done(((bf16[640,768]{1,0:T(8,128)(2,1)}), bf16[2560,768]{1,0:T(8,128)(2,1)}) %all-gather.7.cloned.1.call-update) | async-done | bytes 3932176 | tf_op jit(solution)/shard_map/all_gather | solution.py:160
  209.6 7.5 multiply_convert_fusion.1
  219.0 4.7 convolution_convert_fusion.1
  223.8 43.0 %reduce-scatter.7.cloned.1.call-done = bf16[640,768]{1,0:T(8,128)(2,1)} async-done(((bf16[2560,768]{1,0:T(8,128)(2,1)}), bf16[640,768]{1,0:T(8,128)(2,1)}) %reduce-scatter.7.cloned.1.call-update) | async-done | bytes 983056 | tf_op jit(solution)/shard_map/reduce_scatter | solution.py:164
  276.5 33.1 %all-gather.9.cloned.1.call-done = bf16[2560,768]{1,0:T(8,128)(2,1)} async-done(((bf16[640,768]{1,0:T(8,128)(2,1)}), bf16[2560,768]{1,0:T(8,128)(2,1)}) %all-gather.9.cloned.1.call-update) | async-done | bytes 3932176 | tf_op jit(solution)/shard_map/all_gather | solution.py:179
  309.6 9.6 %convert_reduce_fusion = (f32[768]{0:T(1024)}, bf16[2560,768]{1,0:T(8,128)(2,1)S(1)}) fusion(f32[2560,768]{1,0:T(8,128)} %get-tuple-element.259, f32[768]{0:T(1024)S(1)} %copy-done.37, bf16[2560,768]{1,0:T(8,128)(2,1)} %all-gather.9.cloned.1.call-done, bf16[768,768]{1,0:T(8,128)(2,1)} %param.37), kind=kOutput, calls=%fused_computation.53 | convolution fusion | flops 3045457152 | bytes 16914432 | tf_op jit(solution)/shard_map/gd,fd->gf/dot_general | solution.py:181
  321.1 4.8 convolution_convert_fusion
  326.2 42.8 %reduce-scatter.9.cloned.1.call-done = bf16[640,768]{1,0:T(8,128)(2,1)} async-done(((bf16[2560,768]{1,0:T(8,128)(2,1)}), bf16[640,768]{1,0:T(8,128)(2,1)}) %reduce-scatter.9.cloned.1.call-update) | async-done | bytes 983056 | tf_op jit(solution)/shard_map/reduce_scatter | solution.py:186
  375.5 8.1 fusion.63
  383.6 4.8 fusion.62
  388.4 20.1 %all-gather.11.cloned.1.call-done = bf16[2560,768]{1,0:T(8,128)(2,1)} async-done(((bf16[640,768]{1,0:T(8,128)(2,1)}), bf16[2560,768]{1,0:T(8,128)(2,1)}) %all-gather.11.cloned.1.call-update) | async-done | bytes 3932176 | tf_op jit(solution)/shard_map/all_gather | solution.py:199
  414.3 102.7 %while.23 = (s32[]{:T(128)}, bf16[5,512,576]{1,2,0:T(8,128)(2,1)}, bf16[5,512,192]{1,2,0:T(8,128)(2,1)}, s32[5,512]{1,0:T(8,128)S(1)}, s32[5]{0:T(128)}, /*index...) while((s32[]{:T(128)}, bf16[5,512,576]{1,2,0:T(8,128)(2,1)}, ...), condition=%wide.region_17.18_spmd, body=%wide.region_15.17_spmd.sunk | while | flops 517444096 | bytes 28075180 | solution.py:206
  423.8 4.7 fusion.141
  428.5 4.4 fusion.140
  444.3 4.7 fusion.141
  464.9 4.7 fusion.141
  469.5 4.4 fusion.140
  485.4 4.7 fusion.141
  506.0 4.7 fusion.141
  510.7 4.4 fusion.140
  517.0 4.8 copy.98
  525.8 6.0 convolution_bitcast_fusion.1
  533.7 5.8 convolution_convert_fusion.2
  542.2 11.0 %all-reduce = bf16[4608]{0:T(1024)(128)(2,1)S(1)} all-reduce(bf16[4608]{0:T(1024)(128)(2,1)S(1)} %convert_element_type.135), channel_id=6, replica_groups=mesh['dp'=8,'tensor'=4] {'tensor'}, use_global_device_ids=true, to_apply=%region_30.31.clone | all-reduce | flops 4608 | bytes 18432
  553.8 40.0 %all-reduce.1 = (f32[192]{0:T(256)}, f32[192]{0:T(256)}, f32[6,192]{1,0:T(8,128)S(1)}, f32[768]{0:T(1024)}) all-reduce(f32[192]{0:T(256)S(1)} %get-tuple-element.257, f32[192]{0:T(256)S(1)} %get-tuple-element.256, f32[6,192]{1,0:T(8,128)S(1)} %reshape.391, f32[768]{0:T(1024)S(1)} %copy-done.31), channel_id=1, replica_groups=mesh['dp'=8,'tensor'=4] {'dp'}, use_global_device_ids=true, to_apply=%region_21.22 | all-reduce | flops 2304 | bytes 18432 | tf_op jit(solution)/shard_map/psum | solution.py:254
  594.4 174.0 %all-reduce.5.cloned.1.call-done = (f32[768,576]{0,1:T(8,128)}, f32[192,768]{1,0:T(8,128)}, f32[768,768]{1,0:T(8,128)}, f32[768,768]{1,0:T(8,128)}) async-done(((f32[768,576]{0,1:T(8,128)}, f32[192,768]{1,0:T(8,128)}, f32[768,768]{1,0:T(8,128)}, f32[768,768]{1,0:T(8,128)}), (f32[768,576]{0,1:T(8,128)}, f32[192,768]{1,0:T(8,128)}, f32[768,768]{1,0:T(8,128)}, ...) | async-done | bytes 7077904 | tf_op jit(solution)/shard_map/psum | solution.py:254
  771.0 41.8 %reduce-scatter.11.cloned.1.call-done = bf16[640,768]{1,0:T(8,128)(2,1)} async-done(((bf16[2560,768]{1,0:T(8,128)(2,1)}), bf16[640,768]{1,0:T(8,128)(2,1)}) %reduce-scatter.11.cloned.1.call-update) | async-done | bytes 983056 | tf_op jit(solution)/shard_map/reduce_scatter | solution.py:236
  (283 shorter events, 166.0 us)
Async XLA Ops:
  7.2 202.4 %copy-start = (bf16[768,768]{1,0:T(8,128)(2,1)S(1)}, bf16[768,768]{1,0:T(8,128)(2,1)}, u32[]{:S(2)}) copy-start(bf16[768,768]{1,0:T(8,128)(2,1)} %param.35) | copy-start | bytes 3538948
  7.2 3.5 copy-start.18
  7.2 38.1 %all-gather.5.cloned.1.call-start = ((), (), s32[]{:S(2)}) async-start(), calls=%async_computation.4 | async-start | bytes 4915200 | tf_op jit(solution)/shard_map/all_gather | solution.py:132
  7.9 164.3 %reduce-scatter.5.cloned.1.call-start = ((), (), s32[]{:S(2)}) async-start(), calls=%async_computation.5 | async-start | bytes 9830400 | tf_op jit(solution)/shard_map/reduce_scatter | solution.py:150
  10.7 39.2 %copy-start.21 = (bf16[768,576]{0,1:T(8,128)(2,1)}, bf16[768,576]{0,1:T(8,128)(2,1)S(1)}, u32[]{:S(2)}) copy-start(bf16[768,576]{0,1:T(8,128)(2,1)S(1)} %constant_dynamic-update-slice_fusion.1) | copy-start | bytes 2654212
  97.7 5.4 copy-start.6
  103.1 69.2 %copy-start.30 = (f32[768]{0:T(1024)S(1)}, f32[768]{0:T(1024)}, u32[]{:S(2)}) copy-start(f32[768]{0:T(1024)} %param.32) | copy-start | bytes 9220
  103.1 106.5 %all-gather.7.cloned.1.call-start = ((), (), s32[]{:S(2)}) async-start(), calls=%async_computation.6 | async-start | bytes 4915200 | tf_op jit(solution)/shard_map/all_gather | solution.py:160
  175.1 34.5 %copy-start.37 = (f32[768]{0:T(1024)S(1)}, f32[768]{0:T(1024)}, u32[]{:S(2)}) copy-start(f32[768]{0:T(1024)} %param.36) | copy-start | bytes 9220
  176.5 90.3 %reduce-scatter.7.cloned.1.call-start = ((), (), s32[]{:S(2)}) async-start(), calls=%async_computation.7 | async-start | bytes 4915200 | tf_op jit(solution)/shard_map/reduce_scatter | solution.py:164
  209.6 9.4 %copy-start.36 = (bf16[768,768]{1,0:T(8,128)(2,1)S(1)}, bf16[768,768]{1,0:T(8,128)(2,1)}, u32[]{:S(2)}) copy-start(bf16[768,768]{1,0:T(8,128)(2,1)} %param.37) | copy-start | bytes 3538948
  223.7 43.1 %copy-start.22 = (f32[768]{0:T(1024)S(1)}, f32[768]{0:T(1024)}, u32[]{:S(2)}) copy-start(f32[768]{0:T(1024)} %param.38) | copy-start | bytes 9220
  223.8 85.9 %all-gather.9.cloned.1.call-start = ((), (), s32[]{:S(2)}) async-start(), calls=%async_computation.8 | async-start | bytes 4915200 | tf_op jit(solution)/shard_map/all_gather | solution.py:179
  276.5 92.5 %reduce-scatter.9.cloned.1.call-start = ((), (), s32[]{:S(2)}) async-start(), calls=%async_computation.9 | async-start | bytes 4915200 | tf_op jit(solution)/shard_map/reduce_scatter | solution.py:186
  325.9 82.6 %all-gather.11.cloned.1.call-start = ((), (), s32[]{:S(2)}) async-start(), calls=%async_computation.10 | async-start | bytes 4915200 | tf_op jit(solution)/shard_map/all_gather | solution.py:199
  369.0 3.5 copy-start.2
  369.0 3.5 copy-start.9
  375.4 392.9 %all-reduce.5.cloned.1.call-start = ((), (), s32[]{:S(2)}) async-start(), calls=%async_computation.12 | async-start | bytes 14155776 | tf_op jit(solution)/shard_map/psum | solution.py:254
  375.4 8.2 copy-start.35
  375.4 8.2 copy-start.41
  383.6 24.9 %copy-start.17 = (bf16[192,768]{1,0:T(8,128)(2,1)S(1)}, bf16[192,768]{1,0:T(8,128)(2,1)}, u32[]{:S(2)}) copy-start(bf16[192,768]{1,0:T(8,128)(2,1)} %param.31) | copy-start | bytes 884740
  517.0 4.8 copy-start.7
  521.8 4.0 copy-start.11
  531.8 280.9 %reduce-scatter.11.cloned.1.call-start = ((), (), s32[]{:S(2)}) async-start(), calls=%async_computation.11 | async-start | bytes 4915200 | tf_op jit(solution)/shard_map/reduce_scatter | solution.py:236
  539.6 2.3 copy-start.29
  539.6 13.7 %copy-start.4 = (bf16[5,512,576]{1,2,0:T(8,128)(2,1)S(1)}, bf16[5,512,576]{1,2,0:T(8,128)(2,1)}, u32[]{:S(2)}) copy-start(bf16[5,512,576]{1,2,0:T(8,128)(2,1)} %get-tuple-element.109) | copy-start | bytes 8847364
  539.6 14.1 %copy-start.31 = (f32[768]{0:T(1024)S(1)}, f32[768]{0:T(1024)}, u32[]{:S(2)}) copy-start(f32[768]{0:T(1024)} %get-tuple-element.260) | copy-start | bytes 9220
  553.8 259.0 %copy-start.5 = (f32[640,768]{1,0:T(8,128)S(1)}, f32[640,768]{1,0:T(8,128)}, u32[]{:S(2)}) copy-start(f32[640,768]{1,0:T(8,128)} %get-tuple-element.232) | copy-start | bytes 5898244
  812.8 2.5 copy-start.16
  812.8 3.3 copy-start.14
  816.1 2.5 copy-start.13
  816.1 3.9 copy-start.1
  (23 other events, 30.7 us)
Sparse Core Ops, SparseCore 0:
  9.6 35.6 all-gather.4
  103.2 68.9 reduce-scatter.4
  176.6 32.9 all-gather.6
  223.9 42.8 reduce-scatter.6
  276.6 32.9 all-gather.8
  326.0 42.8 reduce-scatter.8
  375.5 32.9 all-gather.10
  531.9 236.3 all-reduce.4
  770.9 41.8 reduce-scatter.10
where the time goes:
time: 835 us; the launch traced here: 827 us
  waiting for transfers between devices  492 us (59%)
  matrix products  143 us (17%)
  local copies, waits for them, and re-layouts  75.5 us (9%)
  blocking collectives  50.9 us (6%)
  other arithmetic  48.9 us (6%)
  between operations  15.4 us (2%)
    psum x1, waiting for transfers between devices, shards(): lax.psum((grad_w_joined, grad_b_query, grad_b_value, grad_w_output, grad_...  174 us
    reduce_scatter x1, waiting for transfers between devices, shards(): lax.psum_scatter(jnp.dot(piece, w_output, preferred_element_type=jnp.floa...  69.1 us
    reduce_scatter x1, waiting for transfers between devices, shards(): lax.psum_scatter(jnp.dot(piece, w_outer, preferred_element_type=jnp.float...  43 us
    reduce_scatter x1, waiting for transfers between devices, shards(): lax.psum_scatter(jnp.einsum('gf,df->gd', piece, w_inner, preferred_elemen...  42.8 us
    reduce_scatter x1, waiting for transfers between devices, shards(): lax.psum_scatter(input_terms.astype(jnp.bfloat16), 'tensor', scatter_dime...  41.8 us
    psum x1, blocking collectives, shards(): lax.psum((grad_w_joined, grad_b_query, grad_b_value, grad_w_output, grad_...  40 us
    all_gather x1, waiting for transfers between devices, shards(): whole = lax.all_gather(tokens, 'tensor', axis=0, tiled=True)  34.6 us
    all_gather x1, waiting for transfers between devices, shards(): feed_grads = lax.all_gather(grad_feed, 'tensor', axis=0, tiled=True)  33.1 us
  transfers between devices with their start and end apart: 9, of which 9 were waited for; matrix products, arithmetic and copies ran while one was open for 3% of the time, Pallas kernels for 0%

commit v1 on v0

v1 whole, which is shorter than its diff:
```python
import math

import jax
import jax.numpy as jnp
from jax import lax
from jax.experimental import pallas as pl
from jax.experimental.pallas import tpu as pltpu
from jax.sharding import PartitionSpec as P

HD = 64
LEN = 512
HALF = LEN // 2
EPSILON = 1e-12
NEGATIVE = -1000000000.0
SCALE = 1.0 / math.sqrt(HD)
LOG2E = math.log2(math.e)
F32 = jnp.float32
BF16 = jnp.bfloat16
NN = (((1,), (0,)), ((), ()))
NT = (((1,), (1,)), ((), ()))
TN = (((0,), (0,)), ((), ()))


def dg(left, right, dims=NN):
    return lax.dot_general(left, right, dims, preferred_element_type=F32)


def norm_forward(value):
    average = jnp.mean(value, axis=-1, keepdims=True)
    centered = value - average
    variance = jnp.mean(centered * centered, axis=-1, keepdims=True)
    inverse = lax.rsqrt(variance + EPSILON)
    return centered * inverse, inverse


def norm_backward(grad, unit, inverse, gain):
    scaled = grad * gain
    first_mean = jnp.mean(scaled, axis=-1, keepdims=True)
    second_mean = jnp.mean(scaled * unit, axis=-1, keepdims=True)
    return inverse * (scaled - first_mean - unit * second_mean)


def gelu_and_slope(inner):
    cumulative = 0.5 * (1.0 + lax.erf(inner * (1.0 / math.sqrt(2.0))))
    slope = cumulative + inner * jnp.exp(-0.5 * inner * inner) * (1.0 / math.sqrt(2.0 * math.pi))
    return inner * cumulative, slope


def attend_forward(q_ref, k_ref, v_ref, bias_ref, ctx_ref, lse_ref, kc, vc):
    side = lax.axis_index("tensor") // 2
    a, b = side * HALF, side * HALF + LEN
    c = (1 - side) * 2 * LEN
    rows = q_ref.shape[0]
    c = pl.multiple_of(c, HALF)
    kc[pl.ds(0, HALF), :] = k_ref[pl.ds(c, HALF), :]
    kc[pl.ds(HALF, HALF), :] = k_ref[pl.ds(rows, HALF), :]
    vc[pl.ds(0, HALF), :] = v_ref[pl.ds(c, HALF), :]
    vc[pl.ds(HALF, HALF), :] = v_ref[pl.ds(rows, HALF), :]

    def pair(j, _):
        lanes = pl.ds(pl.multiple_of(j * 2 * HD, 2 * HD), 2 * HD)
        for start, at, count in ((a, 0, LEN), (b, LEN, LEN), (c, 2 * LEN, HALF)):
            start = pl.multiple_of(start, HALF)
            queries = q_ref[pl.ds(start, count), lanes]
            if count == LEN:
                keys = k_ref[pl.ds(start, LEN), lanes]
                values = v_ref[pl.ds(start, LEN), lanes]
            else:
                keys = kc[:, lanes]
                values = vc[:, lanes]
            bias = bias_ref[:, pl.ds(at, count)]
            outs = []
            for h in range(2):
                cols = slice(h * HD, (h + 1) * HD)
                logits = dg(keys[:, cols], queries[:, cols], NT) * (SCALE * LOG2E) + bias
                peak = jnp.max(logits, axis=0, keepdims=True)
                powers = jnp.exp2(logits - peak)
                total = jnp.sum(powers, axis=0, keepdims=True)
                weights = (powers * (1.0 / total)).astype(BF16)
                outs.append(dg(weights, values[:, cols], TN).astype(BF16))
                lse_ref[pl.ds(j * 2 + h, 1), pl.ds(at, count)] = peak + jnp.log2(total)
            ctx_ref[pl.ds(start, count), lanes] = jnp.concatenate(outs, axis=1)
        return 0

    lax.fori_loop(0, q_ref.shape[1] // (2 * HD), pair, 0)


def attend_backward(q_ref, k_ref, v_ref, g_ref, bias_ref, lse_ref, dq_ref, dk_ref, dv_ref, kc, vc):
    side = lax.axis_index("tensor") // 2
    a, b = side * HALF, side * HALF + LEN
    c = (1 - side) * 2 * LEN
    rows = q_ref.shape[0]
    c = pl.multiple_of(c, HALF)
    kc[pl.ds(0, HALF), :] = k_ref[pl.ds(c, HALF), :]
    kc[pl.ds(HALF, HALF), :] = k_ref[pl.ds(rows, HALF), :]
    vc[pl.ds(0, HALF), :] = v_ref[pl.ds(c, HALF), :]
    vc[pl.ds(HALF, HALF), :] = v_ref[pl.ds(rows, HALF), :]

    def pair(j, _):
        lanes = pl.ds(pl.multiple_of(j * 2 * HD, 2 * HD), 2 * HD)
        for start, at, count in ((a, 0, LEN), (b, LEN, LEN), (c, 2 * LEN, HALF)):
            start = pl.multiple_of(start, HALF)
            queries = q_ref[pl.ds(start, count), lanes]
            grads = g_ref[pl.ds(start, count), lanes]
            if count == LEN:
                keys = k_ref[pl.ds(start, LEN), lanes]
                values = v_ref[pl.ds(start, LEN), lanes]
            else:
                keys = kc[:, lanes]
                values = vc[:, lanes]
            bias = bias_ref[:, pl.ds(at, count)]
            dqs, dks, dvs = [], [], []
            for h in range(2):
                cols = slice(h * HD, (h + 1) * HD)
                row = lse_ref[pl.ds(j * 2 + h, 1), pl.ds(at, count)]
                logits = dg(keys[:, cols], queries[:, cols], NT) * (SCALE * LOG2E) + bias
                probs = jnp.exp2(logits - row)
                dprobs = dg(values[:, cols], grads[:, cols], NT)
                across = jnp.sum(probs * dprobs, axis=0, keepdims=True)
                dscores = (probs * (dprobs - across) * SCALE).astype(BF16)
                dvs.append(dg(probs.astype(BF16), grads[:, cols], NN).astype(BF16))
                dks.append(dg(dscores, queries[:, cols], NN).astype(BF16))
                dqs.append(dg(dscores, keys[:, cols], TN).astype(BF16))
            dq_ref[pl.ds(start, count), lanes] = jnp.concatenate(dqs, axis=1)
            dk, dv = jnp.concatenate(dks, axis=1), jnp.concatenate(dvs, axis=1)
            if count == LEN:
                dk_ref[pl.ds(start, LEN), lanes] = dk
                dv_ref[pl.ds(start, LEN), lanes] = dv
            else:
                dk_ref[pl.ds(start, HALF), lanes] = dk[:HALF]
                dv_ref[pl.ds(start, HALF), lanes] = dv[:HALF]
                dk_ref[pl.ds(rows, HALF), lanes] = dk[HALF:]
                dv_ref[pl.ds(rows, HALF), lanes] = dv[HALF:]
        return 0

    lax.fori_loop(0, q_ref.shape[1] // (2 * HD), pair, 0)


IN_VMEM = pl.BlockSpec(memory_space=pltpu.VMEM)


def local_call(kernel, outs, scratch, flops, operands):
    moved = sum(o.size * o.dtype.itemsize for o in operands)
    return pl.pallas_call(
        kernel,
        out_shape=outs,
        in_specs=[IN_VMEM] * len(operands),
        out_specs=[IN_VMEM] * len(outs),
        scratch_shapes=scratch,
        cost_estimate=pl.CostEstimate(flops=flops, bytes_accessed=moved, transcendentals=0),
        compiler_params=pltpu.CompilerParams(vmem_limit_bytes=48 << 20),
    )(*operands)


def interleave(own, other):
    rows, width = own.shape
    heads = width // HD
    both = jnp.stack([own.reshape(rows, heads, HD), other.reshape(rows, heads, HD)], axis=2)
    return both.reshape(rows, 2 * width)


def split_pairs(joined):
    rows, width = joined.shape
    both = joined.reshape(rows, width // (2 * HD), 2, HD)
    return both[:, :, 0].reshape(rows, width // 2), both[:, :, 1].reshape(rows, width // 2)


def mask_bias(segment_ids, lengths, side):
    segments = segment_ids.reshape(-1, LEN)
    ahead = jnp.arange(LEN)
    blocks = []
    for which in range(3):
        index = 3 * side + which if which < 2 else 2
        row = lax.dynamic_index_in_dim(segments, index, 0, keepdims=False)
        length = lax.dynamic_index_in_dim(lengths, index, 0, keepdims=False)
        if which < 2:
            key_places, key_segments, count = ahead, row, LEN
        else:
            key_places = (ahead + side * HALF) % LEN
            key_segments = jnp.where(side == 0, row, jnp.roll(row, -HALF))
            count = HALF
        same = key_segments[:, None] == key_segments[None, :count]
        live = key_places[:, None] < length
        diagonal = key_places[:, None] == key_places[None, :count]
        blocks.append(jnp.where(same & live | diagonal, 0.0, NEGATIVE))
    return jnp.concatenate(blocks, axis=1).astype(F32)


def shards(
    tokens,
    segment_ids,
    lengths,
    w_query,
    b_query,
    w_key,
    w_value,
    b_value,
    w_output,
    b_output,
    first_gain,
    first_shift,
    w_inner,
    b_inner,
    w_outer,
    b_outer,
    second_gain,
    second_shift,
    cotangent,
):
    place = lax.axis_index("tensor")
    core, side = place % 2, place // 2
    own_rows, wide = tokens.shape
    width = w_query.shape[1]
    units = w_inner.shape[1]
    chip_rows = 2 * own_rows
    c_start = (1 - side) * 2 * LEN

    def to_core(value):
        return lax.ppermute(value, "tensor", [(i, i ^ 1) for i in range(4)])

    def to_side(value):
        return lax.ppermute(value, "tensor", [(i, i ^ 2) for i in range(4)])

    def both_cores(value):
        other = to_core(value)
        return jnp.where(core == 0, jnp.concatenate([value, other]), jnp.concatenate([other, value]))

    def sum_cores(partial):
        theirs = lax.dynamic_slice_in_dim(partial, (1 - core) * own_rows, own_rows, 0)
        mine = lax.dynamic_slice_in_dim(partial, core * own_rows, own_rows, 0)
        return mine + to_core(theirs.astype(BF16)).astype(F32)

    joined_own = jnp.concatenate([w_query, w_key, w_value], axis=1)
    joined_other = to_side(joined_own)
    rows = both_cores(tokens)
    c_rows = to_side(lax.dynamic_slice_in_dim(rows, c_start, HALF, 0))
    bias_own = jnp.concatenate([b_query, b_value, b_inner])
    bias_other = to_side(bias_own)
    w_output_other = to_side(w_output)
    w_inner_other = to_side(w_inner)
    w_outer_other = to_side(w_outer)

    bias = mask_bias(segment_ids, lengths, side)
    b_q = interleave(bias_own[None, :width], bias_other[None, :width])
    b_v = interleave(bias_own[None, width : 2 * width], bias_other[None, width : 2 * width])
    parts = [
        interleave(joined_own[:, i * width : (i + 1) * width], joined_other[:, i * width : (i + 1) * width])
        for i in range(3)
    ]
    extended = jnp.concatenate([rows, c_rows])
    queries = (dg(rows, parts[0]) + b_q).astype(BF16)
    keys = dg(extended, parts[1]).astype(BF16)
    values = (dg(extended, parts[2]) + b_v).astype(BF16)
    both = 2 * width
    pairs_scratch = [pltpu.VMEM((LEN, both), BF16), pltpu.VMEM((LEN, both), BF16)]
    context, lse = local_call(
        attend_forward,
        [jax.ShapeDtypeStruct((chip_rows, both), BF16), jax.ShapeDtypeStruct((8, chip_rows), F32)],
        pairs_scratch,
        4 * chip_rows * LEN * both,
        (queries, keys, values, bias),
    )
    w_out = interleave(w_output.T, w_output_other.T)
    attended = sum_cores(dg(context, w_out, NT))
    first_unit, first_inverse = norm_forward(tokens.astype(F32) + attended + b_output)
    first = (first_unit * first_gain + first_shift).astype(BF16)
    first_rows = both_cores(first)
    w_in = jnp.concatenate([w_inner, w_inner_other], axis=1)
    b_in = jnp.concatenate([bias_own[2 * width :], bias_other[2 * width :]])
    inner = dg(first_rows, w_in) + b_in
    hidden, slope = gelu_and_slope(inner)
    hidden = hidden.astype(BF16)
    slope = slope.astype(BF16)
    w_down = jnp.concatenate([w_outer, w_outer_other], axis=0)
    feed = sum_cores(dg(hidden, w_down))
    second_unit, second_inverse = norm_forward(first.astype(F32) + feed + b_outer)
    output = (second_unit * second_gain + second_shift).astype(BF16)
    upstream = cotangent.astype(F32)
    grad_second = norm_backward(upstream, second_unit, second_inverse, second_gain)
    grad_second_gain = jnp.sum(upstream * second_unit, axis=0)
    grad_second_shift = jnp.sum(upstream, axis=0)
    grad_feed = grad_second.astype(BF16)
    grad_b_outer = jnp.sum(grad_feed.astype(F32), axis=0)
    feed_rows = both_cores(grad_feed)
    grad_w_down = dg(hidden, feed_rows, TN).astype(BF16)
    outer_away = to_side(grad_w_down[units:])
    grad_inner = (dg(feed_rows, w_down, NT) * slope.astype(F32)).astype(BF16)
    grad_b_in = jnp.sum(grad_inner.astype(F32), axis=0)
    grad_w_in = dg(first_rows, grad_inner, TN).astype(BF16)
    inner_away = to_side(grad_w_in[:, units:])
    grad_first = grad_second + sum_cores(dg(grad_inner, w_in, NT))
    grad_branch = norm_backward(grad_first, first_unit, first_inverse, first_gain)
    grad_first_gain = jnp.sum(grad_first * first_unit, axis=0)
    grad_first_shift = jnp.sum(grad_first, axis=0)
    grad_attended = grad_branch.astype(BF16)
    grad_b_output = jnp.sum(grad_attended.astype(F32), axis=0)
    branch_rows = both_cores(grad_attended)
    grad_w_out = dg(branch_rows, context, TN).astype(BF16)
    grad_context = dg(branch_rows, w_out).astype(BF16)
    grad_queries, grad_keys, grad_values = local_call(
        attend_backward,
        [
            jax.ShapeDtypeStruct((chip_rows, both), BF16),
            jax.ShapeDtypeStruct((chip_rows + HALF, both), BF16),
            jax.ShapeDtypeStruct((chip_rows + HALF, both), BF16),
        ],
        pairs_scratch,
        10 * chip_rows * LEN * both,
        (queries, keys, values, grad_context, bias, lse),
    )
    away = to_side(jnp.concatenate([grad_keys[chip_rows:], grad_values[chip_rows:]], axis=1))

    def add_c(grads, share):
        mine = lax.dynamic_slice_in_dim(grads, c_start, HALF, 0)
        summed = (mine.astype(F32) + share.astype(F32)).astype(BF16)
        return lax.dynamic_update_slice_in_dim(grads[:chip_rows], summed, c_start, 0)

    away_keys = interleave(*reversed(split_pairs(away[:, :both])))
    away_values = interleave(*reversed(split_pairs(away[:, both:])))
    grad_joined = jnp.concatenate(
        [grad_queries, add_c(grad_keys, away_keys), add_c(grad_values, away_values)], axis=1
    )
    weights_joined = jnp.concatenate(parts, axis=1)
    grad_w_joined = dg(rows, grad_joined, TN).astype(BF16)
    grad_bias = jnp.sum(grad_joined.astype(F32), axis=0, keepdims=True)
    grad_tokens = (grad_branch + sum_cores(dg(grad_joined, weights_joined, NT))).astype(BF16)

    pieces = [split_pairs(grad_w_joined[:, i * both : (i + 1) * both]) for i in range(3)]
    pieces.append(split_pairs(grad_w_out))
    attention_own = jnp.concatenate([p[0] for p in pieces], axis=1)
    attention_away = to_side(jnp.concatenate([p[1] for p in pieces], axis=1))

    def over_groups(own, theirs):
        return lax.psum((own.astype(F32) + theirs.astype(F32)).astype(BF16), "dp").astype(F32)

    outer_sum = over_groups(grad_w_down[:units], outer_away)
    inner_sum = over_groups(grad_w_in[:, :units], inner_away)
    attention_sum = over_groups(attention_own, attention_away)

    small = jnp.stack(
        [
            grad_b_output,
            grad_first_gain,
            grad_first_shift,
            grad_b_outer,
            grad_second_gain,
            grad_second_shift,
        ]
    )
    small_flat = small.reshape(6, 4, wide // 4).transpose(1, 0, 2).reshape(4, -1)
    biases = [split_pairs(grad_bias[:, :both]), split_pairs(grad_bias[:, 2 * both :])]
    bias_rows = [
        jnp.concatenate([biases[0][i][0], biases[1][i][0], grad_b_in[i * units : (i + 1) * units]]) for i in range(2)
    ]
    index = jnp.arange(4)[:, None]
    bias_flat = jnp.where(index == place, bias_rows[0], jnp.where(index == place ^ 2, bias_rows[1], 0.0))
    totals = lax.psum(jnp.concatenate([small_flat, bias_flat], axis=1), ("dp", "tensor"))
    total = lax.dynamic_index_in_dim(totals, place, 0, keepdims=False)
    shares = total[: 6 * width].reshape(6, width)
    rest = total[6 * width :]
    return (
        output,
        grad_tokens,
        attention_sum[:, :width],
        rest[:width],
        attention_sum[:, width : 2 * width],
        attention_sum[:, 2 * width : 3 * width],
        rest[width : 2 * width],
        attention_sum[:, 3 * width :].T,
        shares[0],
        shares[1],
        shares[2],
        inner_sum,
        rest[2 * width :],
        outer_sum,
        shares[3],
        shares[4],
        shares[5],
    )


def solution(mesh):
    in_specs = (
        P(("dp", "tensor"), None),
        P("dp"),
        P("dp"),
        P(None, "tensor"),
        P("tensor"),
        P(None, "tensor"),
        P(None, "tensor"),
        P("tensor"),
        P("tensor", None),
        P(),
        P(),
        P(),
        P(None, "tensor"),
        P("tensor"),
        P("tensor", None),
        P(),
        P(),
        P(),
        P(("dp", "tensor"), None),
    )
    out_specs = (
        P(("dp", "tensor"), None),
        P(("dp", "tensor"), None),
        P(None, "tensor"),
        P("tensor"),
        P(None, "tensor"),
        P(None, "tensor"),
        P("tensor"),
        P("tensor", None),
        P("tensor"),
        P("tensor"),
        P("tensor"),
        P(None, "tensor"),
        P("tensor"),
        P("tensor", None),
        P("tensor"),
        P("tensor"),
        P("tensor"),
    )
    return jax.shard_map(shards, mesh=mesh, in_specs=in_specs, out_specs=out_specs, check_vma=False)
```

time: 835 us -> 445 us (0.53)
  waiting for transfers between devices: 492 us -> 205 us
  matrix products: 143 us -> 41.5 us
  local copies, waits for them, and re-layouts: 75.5 us -> 47.6 us
  Pallas kernels: 0 us -> 26.5 us
  starting transfers between devices: 0.75 us -> 15 us
    reduce_scatter x4 -> x0, waiting for transfers between devices: 197 us -> none  [the longest x1 69.1 us: shards(): lax.psum_scatter(jnp.dot(piece, w_output, preferred_element_type=jnp.floa...]
    ppermute x0 -> x18, waiting for transfers between devices: none -> 127 us  [the longest x10 119 us: to_side(): return lax.ppermute(value, 'tensor', [(i, i ^ 2) for i in range(4)])]
    all_gather x4 -> x0, waiting for transfers between devices: 121 us -> none  [the longest x1 34.6 us: shards(): whole = lax.all_gather(tokens, 'tensor', axis=0, tiled=True)]
    dot_general x47 -> x14, matrix products: 143 us -> 41.5 us  [dg(): return lax.dot_general(left, right, dims, preferred_element_type=F32)]
    psum x1, waiting for transfers between devices: 174 us -> 77.7 us  [over_groups(): lax.psum((own.astype(F32) + theirs.astype(F32)).astype(BF16), 'dp')]
    dynamic_slice x40 -> x4, local copies, waits for them, and re-layouts: 33.1 us -> 2.1 us  [the longest x1 1.37 us: mask_bias(): length = lax.dynamic_index_in_dim(lengths, index, 0, keepdims=False)]
    pallas_call x0 -> x2, Pallas kernels: none -> 26.5 us  [local_call(): pl.pallas_call(kernel, out_shape=outs, in_specs=[IN_VMEM] * len(operands)...]
    ppermute x0 -> x18, starting transfers between devices: none -> 15 us  [the longest x10 13.7 us: to_side(): return lax.ppermute(value, 'tensor', [(i, i ^ 2) for i in range(4)])]
  transfers between devices with their start and end apart: 9 -> 19, of which waited for: 9 -> 12; matrix products, arithmetic and copies ran while one was open for 3% -> 18% of each run, Pallas kernels for 0% -> 4%
where the time goes in v1:
time: 445 us; the launch traced here: 437 us
  waiting for transfers between devices  205 us (46%)
  local copies, waits for them, and re-layouts  47.6 us (11%)
  blocking collectives  43.6 us (10%)
  other arithmetic  42.6 us (10%)
  matrix products  41.5 us (9%)
  Pallas kernels  26.5 us (6%)
  between operations  15.3 us (3%)
  starting transfers between devices  15 us (3%)
    ppermute x10, waiting for transfers between devices, to_side(): return lax.ppermute(value, 'tensor', [(i, i ^ 2) for i in range(4)])  119 us
    psum x1, waiting for transfers between devices, over_groups(): lax.psum((own.astype(F32) + theirs.astype(F32)).astype(BF16), 'dp')  77.7 us
    psum x1, blocking collectives, shards(): lax.psum(jnp.concatenate([small_flat, bias_flat], axis=1), ('dp', 'tensor'))  43.6 us
    dot_general x14, matrix products, dg(): return lax.dot_general(left, right, dims, preferred_element_type=F32)  41.5 us
    pallas_call x2, Pallas kernels, local_call(): pl.pallas_call(kernel, out_shape=outs, in_specs=[IN_VMEM] * len(operands)...  26.5 us
    ppermute x10, starting transfers between devices, to_side(): return lax.ppermute(value, 'tensor', [(i, i ^ 2) for i in range(4)])  13.7 us
    unnamed x130, local copies, waits for them, and re-layouts  13.5 us
  transfers between devices with their start and end apart: 19, of which 12 were waited for; matrix products, arithmetic and copies ran while one was open for 18% of the time, Pallas kernels for 4%

profile of v1, /device:TPU:0, one launch (start us, length us, event | category | flops | bytes accessed | tf_op | source)
XLA Modules:
  0.0 437.2 jit_solution(9929187151927938235)
XLA Ops:
  7.8 2.1 pad_maximum_fusion.6
  9.9 2.5 collective-permute-start.1
  13.2 2.0 collective-permute-start.4
  23.3 10.0 %collective-permute-done.2 = f32[1152]{0:T(1024)S(1)} collective-permute-done((f32[1152]{0:T(1024)S(1)}, f32[1152]{0:T(1024)S(1)}, u32[]{:S(2)}, u32[]{:S(2)}) %collective-permute-start.2) | collective-permute-done | bytes 4640 | tf_op jit(solution)/shard_map/ppermute | solution.py:222
  33.7 5.7 %collective-permute-done.4 = bf16[192,768]{1,0:T(8,128)(2,1)S(1)} collective-permute-done((bf16[192,768]{1,0:T(8,128)(2,1)}, bf16[192,768]{1,0:T(8,128)(2,1)S(1)}, u32[]{:S(2)}, u32[]{:S(2)}) %collective-permute-start.4) | collective-permute-done | bytes 294944 | tf_op jit(solution)/shard_map/ppermute | solution.py:222
  45.0 7.9 %collective-permute-done.3 = bf16[256,768]{1,0:T(8,128)(2,1)S(1)} collective-permute-done((bf16[256,768]{1,0:T(8,128)(2,1)S(1)}, bf16[256,768]{1,0:T(8,128)(2,1)S(1)}, u32[]{:S(2)}, u32[]{:S(2)}) %collective-permute-start.3) | collective-permute-done | bytes 393248 | tf_op jit(solution)/shard_map/ppermute | solution.py:222
  55.8 10.3 %shard_map.314 = (bf16[1280,384]{1,0:T(8,128)(2,1)S(1)}, f32[8,1280]{1,0:T(8,128)S(1)}) custom-call(bf16[1280,384]{1,0:T(8,128)(2,1)S(1)} %fusion.6.q_ref, bf16[1536,384]{1,0:T(8,128)(2,1)S(1)} %convolution_convert_fusion.4.k_ref, bf16[1536,384]{1,0:T(8,128)(2,1)S(1)} %fusion.7.v_ref, f32[512,1280]{1,0:T(8,128)} %pad_maximum_fusion.1.bias_ref), custom_call_target="tpu_custom_call" | custom-call | flops 1006632960 | bytes 5963776 | tf_op jit(solution)/shard_map/pallas_call | solution.py:144
  72.1 2.5 fusion.40
  78.8 19.7 %collective-permute-done.7 = bf16[768,768]{1,0:T(8,128)(2,1)} collective-permute-done((bf16[768,768]{1,0:T(8,128)(2,1)}, bf16[768,768]{1,0:T(8,128)(2,1)}, u32[]{:S(2)}, u32[]{:S(2)}) %collective-permute-start.7) | collective-permute-done | bytes 1179680 | tf_op jit(solution)/shard_map/ppermute | solution.py:222
  99.9 23.5 %collective-permute-done.8 = bf16[768,768]{1,0:T(8,128)(2,1)} collective-permute-done((bf16[768,768]{1,0:T(8,128)(2,1)}, bf16[768,768]{1,0:T(8,128)(2,1)}, u32[]{:S(2)}, u32[]{:S(2)}) %collective-permute-start.8) | collective-permute-done | bytes 1179680 | tf_op jit(solution)/shard_map/ppermute | solution.py:222
  124.8 4.0 multiply_convert_fusion
  128.8 3.2 fusion.57
  132.3 2.6 collective-permute-done.9
  140.1 2.4 collective-permute-done.10
  142.5 7.5 %convert_reduce_fusion = (f32[1536]{0:T(1024)}, bf16[1280,1536]{1,0:T(8,128)(2,1)S(1)}) fusion(f32[1280,1536]{1,0:T(8,128)S(1)} %get-tuple-element.98, bf16[1536,768]{1,0:T(8,128)(2,1)S(1)} %constant_dynamic-update-slice_fusion.2, bf16[640,768]{1,0:T(8,128)(2,1)S(1)} %collective-permute-done.10, bf16[640,768]{1,0:T(8,128)(2,1)S(1)} %get-tuple-element.45, ...), kind=kOutput, calls=%fused_computation.8 | convolution fusion | flops 3056269824 | bytes 16128001 | tf_op jit(solution)/shard_map/dot_general | solution.py:25
  150.0 3.2 fusion.58
  156.4 2.8 collective-permute-done.11
  159.1 5.5 %multiply_reduce_fusion = (f32[768]{0:T(1024)S(1)}, f32[640]{0:T(1024)S(1)}, f32[640]{0:T(1024)S(1)}, f32[768]{0:T(1024)S(1)}, f32[640,768]{1,0:T(8,128)S(1)}, /*index=5*/bf16[640,768]{1,0:T(8,128)(2,1)}) fusion(f32[640,768]{1,0:T(8,128)S(1)} %get-tuple-element.53, f32[640]{0:T(1024)S(1)} %add_rsqrt_fusion.1, f32[640]{0:T(1024)S(1)} %broadcast_multiply_fusion.5, ...), kind=kLoop, calls=%fused_computation.43 | loop fusion | flops 11302144 | bytes 10849284 | tf_op jit(solution)/shard_map/reduce_sum | solution.py:293
  164.7 2.6 convert_reduce_fusion.4
  168.1 3.7 convolution_convert_fusion.1
  174.5 3.5 convolution_convert_fusion.2
  182.0 16.2 %shard_map.315 = (bf16[1280,384]{1,0:T(8,128)(2,1)S(1)}, bf16[1536,384]{1,0:T(8,128)(2,1)S(1)}, bf16[1536,384]{1,0:T(8,128)(2,1)S(1)}) custom-call(bf16[1280,384]{1,0:T(8,128)(2,1)S(1)} %copy-done.5, bf16[1536,384]{1,0:T(8,128)(2,1)} %copy-done, bf16[1536,384]{1,0:T(8,128)(2,1)} %copy-done.1, bf16[1280,384]{1,0:T(8,128)(2,1)S(1)} %convolution_convert_fusion.3.g_ref, ...), custom_call_target="tpu_custom_call" | custom-call | flops 2516582400 | bytes 6987776 | tf_op jit(solution)/shard_map/pallas_call | solution.py:144
  202.9 32.0 %collective-permute-done.13 = bf16[256,768]{1,0:T(8,128)(2,1)S(1)} collective-permute-done((bf16[256,768]{1,0:T(8,128)(2,1)S(1)}, bf16[256,768]{1,0:T(8,128)(2,1)S(1)}, u32[]{:S(2)}, u32[]{:S(2)}) %collective-permute-start.13) | collective-permute-done | bytes 393248 | tf_op jit(solution)/shard_map/ppermute | solution.py:222
  238.7 2.0 copy.45
  244.2 4.8 %convolution_convert_fusion = bf16[768,1152]{1,0:T(8,128)(2,1)S(1)} fusion(bf16[1280,768]{1,0:T(8,128)(2,1)} %copy-done.14, bf16[1280,384]{1,0:T(8,128)(2,1)} %fusion.26, bf16[1280,384]{1,0:T(8,128)(2,1)} %fusion.25, bf16[1280,384]{1,0:T(8,128)(2,1)S(1)} %copy-done.3), kind=kOutput, calls=%fused_computation.13 | convolution fusion | flops 2274656256 | bytes 6684672 | tf_op jit(solution)/shard_map/dot_general | solution.py:25
  253.4 2.7 add_convert_fusion
  256.1 2.6 add_convert_fusion.1
  258.7 20.3 %collective-permute-done.15 = bf16[768,768]{0,1:T(8,128)(2,1)S(1)} collective-permute-done((bf16[768,768]{0,1:T(8,128)(2,1)S(1)}, bf16[768,768]{0,1:T(8,128)(2,1)S(1)}, u32[]{:S(2)}, u32[]{:S(2)}) %collective-permute-start.15) | collective-permute-done | bytes 1179680 | tf_op jit(solution)/shard_map/ppermute | solution.py:222
  290.2 4.0 fusion.15
  297.7 43.6 %psum.29 = f32[4,2304]{1,0:T(4,128)S(1)} all-reduce(f32[4,2304]{1,0:T(4,128)S(1)} %pad_maximum_fusion.14), channel_id=1, replica_groups=mesh['dp'=8,'tensor'=4] {'dp','tensor'}, use_global_device_ids=true, to_apply=%region_17.18 | all-reduce | flops 9216 | bytes 73728 | tf_op jit(solution)/shard_map/psum | solution.py:357
  342.6 2.8 add_convert_fusion.3
  345.4 77.7 %all-reduce.3.cloned.1.call-done = (bf16[768,768]{0,1:T(8,128)(2,1)}, bf16[768,768]{1,0:T(8,128)(2,1)}, bf16[768,768]{1,0:T(8,128)(2,1)}) async-done(((bf16[768,768]{0,1:T(8,128)(2,1)}, bf16[768,768]{1,0:T(8,128)(2,1)}, bf16[768,768]{1,0:T(8,128)(2,1)}), (bf16[768,768]{0,1:T(8,128)(2,1)}, bf16[768,768]{1,0:T(8,128)(2,1)}, bf16[768,768]{1,0:T(8,128)(2,1)})) %all-reduce.3.cloned.1.call-update) | async-done | bytes 3538960 | tf_op jit(solution)/shard_map/psum | solution.py:334
  (276 shorter events, 86.0 us)
Async XLA Ops:
  7.2 416.0 %all-reduce.3.cloned.1.call-start = ((), (), s32[]{:S(2)}) async-start(), calls=%async_computation | async-start | bytes 7077888 | tf_op jit(solution)/shard_map/psum | solution.py:334
  7.2 33.2 %collective-permute-start = (bf16[640,768]{1,0:T(8,128)(2,1)}, bf16[640,768]{1,0:T(8,128)(2,1)S(1)}, u32[]{:S(2)}, u32[]{:S(2)}) collective-permute-start(bf16[640,768]{1,0:T(8,128)(2,1)} %param.19), channel_id=1, source_target_pairs={{0,1},{1,0},{2,3},{3,2},{4,5},{5,4},{6,7},{7,6},{8,9},{9,8},{10,11... | collective-permute-start | bytes 2949128 | tf_op jit(solution)/shard_map/ppermute | solution.py:219
  9.9 29.6 %collective-permute-start.1 = (bf16[768,576]{0,1:T(8,128)(2,1)}, bf16[768,576]{0,1:T(8,128)(2,1)S(1)}, u32[]{:S(2)}, u32[]{:S(2)}) collective-permute-start(bf16[768,576]{0,1:T(8,128)(2,1)} %pad_maximum_fusion.6), channel_id=1, source_target_pairs={{0,2},{1,3},{2,0},{3,1},{4,6},{5,7},{6,4},{7,5},{8,10},{9,11},{10,... | collective-permute-start | bytes 2654216 | tf_op jit(solution)/shard_map/ppermute | solution.py:222
  13.2 20.1 %collective-permute-start.2 = (f32[1152]{0:T(1024)S(1)}, f32[1152]{0:T(1024)S(1)}, u32[]{:S(2)}, u32[]{:S(2)}) collective-permute-start(f32[1152]{0:T(1024)S(1)} %concatenate.83), channel_id=1, source_target_pairs={{0,2},{1,3},{2,0},{3,1},{4,6},{5,7},{6,4},{7,5},{8,10},{9,11},{10,... | collective-permute-start | bytes 13832 | tf_op jit(solution)/shard_map/ppermute | solution.py:222
  13.2 26.2 %collective-permute-start.4 = (bf16[192,768]{1,0:T(8,128)(2,1)}, bf16[192,768]{1,0:T(8,128)(2,1)S(1)}, u32[]{:S(2)}, u32[]{:S(2)}) collective-permute-start(bf16[192,768]{1,0:T(8,128)(2,1)} %param.27), channel_id=1, source_target_pairs={{0,2},{1,3},{2,0},{3,1},{4,6},{5,7},{6,4},{7,5},{8,10},{9,11},{10,... | collective-permute-start | bytes 884744 | tf_op jit(solution)/shard_map/ppermute | solution.py:222
  21.5 17.9 %copy-start.40 = (bf16[192,768]{1,0:T(8,128)(2,1)S(1)}, bf16[192,768]{1,0:T(8,128)(2,1)}, u32[]{:S(2)}) copy-start(bf16[192,768]{1,0:T(8,128)(2,1)} %param.27) | copy-start | bytes 884740
  23.2 16.4 %copy-start.29 = (bf16[768,192]{0,1:T(8,128)(2,1)S(1)}, bf16[768,192]{0,1:T(8,128)(2,1)}, u32[]{:S(2)}) copy-start(bf16[768,192]{0,1:T(8,128)(2,1)} %param.25) | copy-start | bytes 884740
  39.5 26.7 %copy-start.15 = (bf16[768,3,2,64]{0,3,2,1:T(8,128)(2,1)}, bf16[768,3,2,64]{0,3,2,1:T(8,128)(2,1)S(1)}, u32[]{:S(2)}) copy-start(bf16[768,3,2,64]{0,3,2,1:T(8,128)(2,1)S(1)} %pad_maximum_fusion.10) | copy-start | bytes 1769476
  39.6 14.7 %copy-start.36 = (bf16[768,3,2,64]{0,3,2,1:T(8,128)(2,1)}, bf16[768,3,2,64]{0,3,2,1:T(8,128)(2,1)S(1)}, u32[]{:S(2)}) copy-start(bf16[768,3,2,64]{0,3,2,1:T(8,128)(2,1)S(1)} %pad_maximum_fusion.9) | copy-start | bytes 1769476
  40.5 12.5 %copy-start.38 = (bf16[768,3,2,64]{0,3,2,1:T(8,128)(2,1)}, bf16[768,3,2,64]{0,3,2,1:T(8,128)(2,1)S(1)}, u32[]{:S(2)}) copy-start(bf16[768,3,2,64]{0,3,2,1:T(8,128)(2,1)S(1)} %pad_maximum_fusion.8) | copy-start | bytes 1769476
  41.9 12.5 %copy-start.14 = (bf16[1280,768]{1,0:T(8,128)(2,1)}, bf16[1280,768]{1,0:T(8,128)(2,1)S(1)}, u32[]{:S(2)}) copy-start(bf16[1280,768]{1,0:T(8,128)(2,1)S(1)} %maximum_select_fusion) | copy-start | bytes 5898244
  41.9 11.0 %collective-permute-start.3 = (bf16[256,768]{1,0:T(8,128)(2,1)S(1)}, bf16[256,768]{1,0:T(8,128)(2,1)S(1)}, u32[]{:S(2)}, u32[]{:S(2)}) collective-permute-start(bf16[256,768]{1,0:T(8,128)(2,1)S(1)} %constant_dynamic-slice_fusion.3), channel_id=1, source_target_pairs={{0,2},{1,3},{2,0},{3,1},{4,6},{5,7},{6,4},{7,5},{8,10},{9,11},{10,... | collective-permute-start | bytes 1179656 | tf_op jit(solution)/shard_map/ppermute | solution.py:222
  45.0 10.8 %copy-start.4 = (bf16[1280,384]{1,0:T(8,128)(2,1)}, bf16[1280,384]{1,0:T(8,128)(2,1)S(1)}, u32[]{:S(2)}) copy-start(bf16[1280,384]{1,0:T(8,128)(2,1)S(1)} %fusion.6.q_ref) | copy-start | bytes 2949124
  55.8 10.3 %copy-start.1 = (bf16[1536,384]{1,0:T(8,128)(2,1)}, bf16[1536,384]{1,0:T(8,128)(2,1)S(1)}, u32[]{:S(2)}) copy-start(bf16[1536,384]{1,0:T(8,128)(2,1)S(1)} %fusion.7.v_ref) | copy-start | bytes 3538948
  69.3 2.8 collective-permute-start.5
  69.4 29.1 %collective-permute-start.7 = (bf16[768,768]{1,0:T(8,128)(2,1)}, bf16[768,768]{1,0:T(8,128)(2,1)}, u32[]{:S(2)}, u32[]{:S(2)}) collective-permute-start(bf16[768,768]{1,0:T(8,128)(2,1)} %param.31), channel_id=1, source_target_pairs={{0,2},{1,3},{2,0},{3,1},{4,6},{5,7},{6,4},{7,5},{8,10},{9,11},{10,... | collective-permute-start | bytes 3538952 | tf_op jit(solution)/shard_map/ppermute | solution.py:222
  71.0 52.4 %collective-permute-start.8 = (bf16[768,768]{1,0:T(8,128)(2,1)}, bf16[768,768]{1,0:T(8,128)(2,1)}, u32[]{:S(2)}, u32[]{:S(2)}) collective-permute-start(bf16[768,768]{1,0:T(8,128)(2,1)} %param.33), channel_id=1, source_target_pairs={{0,2},{1,3},{2,0},{3,1},{4,6},{5,7},{6,4},{7,5},{8,10},{9,11},{10,... | collective-permute-start | bytes 3538952 | tf_op jit(solution)/shard_map/ppermute | solution.py:222
  75.7 49.0 %copy-start.32 = (bf16[640,768]{1,0:T(8,128)(2,1)}, bf16[640,768]{1,0:T(8,128)(2,1)S(1)}, u32[]{:S(2)}) copy-start(bf16[640,768]{1,0:T(8,128)(2,1)S(1)} %add_convert_fusion.5) | copy-start | bytes 2949124
  75.8 49.0 %collective-permute-start.6 = (bf16[640,768]{1,0:T(8,128)(2,1)S(1)}, bf16[640,768]{1,0:T(8,128)(2,1)S(1)}, u32[]{:S(2)}, u32[]{:S(2)}) collective-permute-start(bf16[640,768]{1,0:T(8,128)(2,1)S(1)} %add_convert_fusion.5), channel_id=1, source_target_pairs={{0,1},{1,0},{2,3},{3,2},{4,5},{5,4},{6,7},{7,6},{8,9},{9,8},{10,11... | collective-permute-start | bytes 2949128 | tf_op jit(solution)/shard_map/ppermute | solution.py:219
  132.2 2.6 collective-permute-start.9
  139.9 10.1 %copy-start.34 = (bf16[640,768]{1,0:T(8,128)(2,1)}, bf16[640,768]{1,0:T(8,128)(2,1)S(1)}, u32[]{:S(2)}) copy-start(bf16[640,768]{1,0:T(8,128)(2,1)S(1)} %get-tuple-element.45) | copy-start | bytes 2949124
  139.9 2.6 collective-permute-start.10
  156.2 2.9 collective-permute-start.11
  167.2 13.6 %collective-permute-start.12 = (bf16[640,768]{1,0:T(8,128)(2,1)S(1)}, bf16[640,768]{1,0:T(8,128)(2,1)S(1)}, u32[]{:S(2)}, u32[]{:S(2)}) collective-permute-start(bf16[640,768]{1,0:T(8,128)(2,1)S(1)} %get-tuple-element.47), channel_id=1, source_target_pairs={{0,1},{1,0},{2,3},{3,2},{4,5},{5,4},{6,7},{7,6},{8,9},{9,8},{10,11... | collective-permute-start | bytes 2949128 | tf_op jit(solution)/shard_map/ppermute | solution.py:219
  172.9 80.4 %collective-permute-start.17 = (bf16[768,768]{1,0:T(8,128)(2,1)}, bf16[768,768]{1,0:T(8,128)(2,1)}, u32[]{:S(2)}, u32[]{:S(2)}) collective-permute-start(bf16[768,768]{1,0:T(8,128)(2,1)} %slice.318), channel_id=1, source_target_pairs={{0,2},{1,3},{2,0},{3,1},{4,6},{5,7},{6,4},{7,5},{8,10},{9,11},{10,... | collective-permute-start | bytes 3538952 | tf_op jit(solution)/shard_map/ppermute | solution.py:222
  179.2 76.8 %collective-permute-start.16 = (bf16[768,768]{1,0:T(8,128)(2,1)}, bf16[768,768]{1,0:T(8,128)(2,1)}, u32[]{:S(2)}, u32[]{:S(2)}) collective-permute-start(bf16[768,768]{1,0:T(8,128)(2,1)} %slice.316), channel_id=1, source_target_pairs={{0,2},{1,3},{2,0},{3,1},{4,6},{5,7},{6,4},{7,5},{8,10},{9,11},{10,... | collective-permute-start | bytes 3538952 | tf_op jit(solution)/shard_map/ppermute | solution.py:222
  198.3 36.6 %collective-permute-start.13 = (bf16[256,768]{1,0:T(8,128)(2,1)S(1)}, bf16[256,768]{1,0:T(8,128)(2,1)S(1)}, u32[]{:S(2)}, u32[]{:S(2)}) collective-permute-start(bf16[256,768]{1,0:T(8,128)(2,1)S(1)} %pad_maximum_fusion.11), channel_id=1, source_target_pairs={{0,2},{1,3},{2,0},{3,1},{4,6},{5,7},{6,4},{7,5},{8,10},{9,11},{10,... | collective-permute-start | bytes 1179656 | tf_op jit(solution)/shard_map/ppermute | solution.py:222
  251.8 27.3 %collective-permute-start.15 = (bf16[768,768]{0,1:T(8,128)(2,1)S(1)}, bf16[768,768]{0,1:T(8,128)(2,1)S(1)}, u32[]{:S(2)}, u32[]{:S(2)}) collective-permute-start(bf16[768,768]{0,1:T(8,128)(2,1)S(1)} %pad_maximum_fusion.5), channel_id=1, source_target_pairs={{0,2},{1,3},{2,0},{3,1},{4,6},{5,7},{6,4},{7,5},{8,10},{9,11},{10,... | collective-permute-start | bytes 3538952 | tf_op jit(solution)/shard_map/ppermute | solution.py:222
  256.0 23.0 %copy-start.25 = (bf16[768,3,1,64]{0,3,2,1:T(8,128)(2,1)S(1)}, bf16[768,3,1,64]{0,3,2,1:T(8,128)(2,1)}, u32[]{:S(2)}) copy-start(bf16[768,3,1,64]{0,3,2,1:T(8,128)(2,1)} %get-tuple-element.70) | copy-start | bytes 884740
  256.1 23.0 %copy-start.27 = (bf16[768,3,1,64]{0,3,2,1:T(8,128)(2,1)S(1)}, bf16[768,3,1,64]{0,3,2,1:T(8,128)(2,1)}, u32[]{:S(2)}) copy-start(bf16[768,3,1,64]{0,3,2,1:T(8,128)(2,1)} %get-tuple-element.64) | copy-start | bytes 884740
  296.1 46.5 %copy-start.9 = (f32[640,768]{1,0:T(8,128)S(1)}, f32[640,768]{1,0:T(8,128)}, u32[]{:S(2)}) copy-start(f32[640,768]{1,0:T(8,128)} %get-tuple-element.48) | copy-start | bytes 5898244
  297.2 45.5 %collective-permute-start.14 = (bf16[640,768]{1,0:T(8,128)(2,1)}, bf16[640,768]{1,0:T(8,128)(2,1)S(1)}, u32[]{:S(2)}, u32[]{:S(2)}) collective-permute-start(bf16[640,768]{1,0:T(8,128)(2,1)} %dynamic-slice_convert_fusion), channel_id=1, source_target_pairs={{0,1},{1,0},{2,3},{3,2},{4,5},{5,4},{6,7},{7,6},{8,9},{9,8},{10,11... | collective-permute-start | bytes 2949128 | tf_op jit(solution)/shard_map/ppermute | solution.py:219
  (51 other events, 157.6 us)
Sparse Core Ops, SparseCore 0:
  280.5 142.6 all-reduce.2

commit v2 on v1

--- a/solution.py
+++ b/solution.py
@@ -1,3 +1,4 @@
+import functools
 import math
 
 import jax
@@ -85,55 +86,444 @@
     lax.fori_loop(0, q_ref.shape[1] // (2 * HD), pair, 0)
 
 
-def attend_backward(q_ref, k_ref, v_ref, g_ref, bias_ref, lse_ref, dq_ref, dk_ref, dv_ref, kc, vc):
-    side = lax.axis_index("tensor") // 2
-    a, b = side * HALF, side * HALF + LEN
-    c = (1 - side) * 2 * LEN
+MESH = pl.DeviceIdType.MESH
+
+
+class Unit:
+    def __init__(self, own, other, from_side, from_x, from_z, total):
+        self.own, self.other, self.total = own, other, total
+        self.from_side, self.from_x, self.from_z = from_side, from_x, from_z
+
+
+class Rounds:
+    def __init__(self, units, groups, sems, far, f_out, f_in):
+        self.units = units
+        self.from_far, self.f_out, self.f_in = far, f_out, f_in
+        self.place = lax.axis_index("tensor")
+        group = lax.axis_index("dp")
+        self.x, self.z, self.far = group % 2, (group // 2) % 4, group // 8
+        self.more = groups // 8
+        (self.y_out, self.y_in, self.x_out, self.x_in, self.z_out, self.z_in) = sems[:6]
+        (self.g_out, self.g_in, self.h_out, self.h_in) = sems[6:10]
+        self.sent = []
+
+    def dp_at(self, x, z):
+        return {"dp": self.far * 8 + z * 2 + x}
+
+    def copy(self, source, target, out, into, device):
+        return pltpu.make_async_remote_copy(
+            src_ref=source, dst_ref=target, send_sem=out, recv_sem=into, device_id=device, device_id_type=MESH
+        )
+
+    def start(self, copy):
+        copy.start()
+        self.sent.append(copy)
+
+    def y_copy(self, u):
+        unit = self.units[u]
+        side = {"tensor": (self.place + 2) % 4}
+        return self.copy(unit.other(pl.ds(0, 8)), unit.from_side, self.y_out.at[u], self.y_in.at[u], side)
+
+    def x_copy(self, u):
+        unit = self.units[u]
+        away = unit.own(pl.ds((1 - self.x) * 4, 4))
+        return self.copy(away, unit.from_x, self.x_out.at[u], self.x_in.at[u], self.dp_at(1 - self.x, self.z))
+
+    def z_copy(self, u, step):
+        unit = self.units[u]
+        there = (self.z + step) % 4
+        away = unit.own(self.x * 4 + there)
+        slot = unit.from_z(step - 1)
+        return self.copy(
+            away, slot, self.z_out.at[u, step - 1], self.z_in.at[u, step - 1], self.dp_at(self.x, there)
+        )
+
+    def g_copy(self, u, step, origin):
+        unit = self.units[u]
+        there = (self.z + step) % 4
+        piece = unit.total(self.x * 4 + origin)
+        return self.copy(
+            piece, piece, self.g_out.at[u, step - 1], self.g_in.at[u, step - 1], self.dp_at(self.x, there)
+        )
+
+    def h_copy(self, u, half):
+        unit = self.units[u]
+        piece = unit.total(pl.ds(half * 4, 4))
+        return self.copy(piece, piece, self.h_out.at[u], self.h_in.at[u], self.dp_at(1 - self.x, self.z))
+
+    def y_start(self, u):
+        self.start(self.y_copy(u))
+
+    def x_start(self, u):
+        unit = self.units[u]
+        self.y_copy(u).wait_recv()
+        for i in range(8):
+            own = unit.own(i)
+            own[...] = (own[...].astype(F32) + unit.from_side.at[i][...].astype(F32)).astype(BF16)
+        self.start(self.x_copy(u))
+
+    def z_start(self, u):
+        unit = self.units[u]
+        self.x_copy(u).wait_recv()
+        for i in range(4):
+            own = unit.own(self.x * 4 + i)
+            own[...] = (own[...].astype(F32) + unit.from_x.at[i][...].astype(F32)).astype(BF16)
+        for step in (1, 2, 3):
+            self.start(self.z_copy(u, step))
+
+    def g_start(self, u):
+        unit = self.units[u]
+        value = unit.own(self.x * 4 + self.z)[...].astype(F32)
+        for step in (1, 2, 3):
+            self.z_copy(u, step).wait_recv()
+            value = value + unit.from_z(step - 1)[...].astype(F32)
+        if self.more > 1:
+            value = self.far_sum(u, value)
+        unit.total(self.x * 4 + self.z)[...] = value.astype(BF16)
+        for step in (1, 2, 3):
+            self.start(self.g_copy(u, step, self.z))
+
+    def far_sum(self, u, value):
+        unit = self.units[u]
+        own = unit.own(self.x * 4 + self.z)
+        own[...] = value.astype(BF16)
+        slots = self.from_far.at[u]
+        copies = []
+        for step in range(1, self.more):
+            peer = {"dp": ((self.far + step) % self.more) * 8 + self.z * 2 + self.x}
+            slot = slots.at[step - 1, pl.ds(0, own.shape[0]), pl.ds(0, own.shape[1])]
+            copies.append(self.copy(own, slot, self.f_out.at[u, step - 1], self.f_in.at[u, step - 1], peer))
+            self.start(copies[-1])
+        for step in range(1, self.more):
+            copies[step - 1].wait_recv()
+            value = value + slots[step - 1, pl.ds(0, own.shape[0]), pl.ds(0, own.shape[1])].astype(F32)
+        return value
+
+    def h_start(self, u):
+        for step in (1, 2, 3):
+            self.g_copy(u, step, (self.z - step + 4) % 4).wait_recv()
+        self.start(self.h_copy(u, self.x))
+
+    def end(self, u):
+        self.h_copy(u, 1 - self.x).wait_recv()
+
+    def drain(self):
+        for copy in self.sent:
+            copy.wait_send()
+
+
+def attend_back(q, k, v, g, bias, row):
+    logits = dg(k, q, NT) * (SCALE * LOG2E) + bias
+    probs = jnp.exp2(logits - row)
+    dprobs = dg(v, g, NT)
+    across = jnp.sum(probs * dprobs, axis=0, keepdims=True)
+    dscores = (probs * (dprobs - across) * SCALE).astype(BF16)
+    dv = dg(probs.astype(BF16), g, NN).astype(BF16)
+    dk = dg(dscores, q, NN).astype(BF16)
+    dq = dg(dscores, k, TN).astype(BF16)
+    return dq, dk, dv
+
+
+def pair_back(q, k, v, g, bias, rows):
+    done = []
+    for h in range(2):
+        cols = slice(h * HD, (h + 1) * HD)
+        done.append(attend_back(q[:, cols], k[:, cols], v[:, cols], g[:, cols], bias, rows[h]))
+    return [jnp.concatenate([done[0][i], done[1][i]], axis=1) for i in range(3)]
+
+
+def swap_halves(value):
+    return jnp.concatenate([value[:, HD:], value[:, :HD]], axis=1)
+
+
+def rear_kernel(
+    groups,
+    q_ref,
+    k_ref,
+    v_ref,
+    g_ref,
+    bias_ref,
+    lse_ref,
+    x_ref,
+    ctx_ref,
+    branch_ref,
+    w_ref,
+    residual_ref,
+    inner_own,
+    inner_other,
+    outer_own,
+    outer_other,
+    small_ref,
+    inner_total,
+    outer_total,
+    attention_total,
+    tokens_out,
+    small_out,
+    kc,
+    vc,
+    dq,
+    dk,
+    dv,
+    away,
+    back,
+    pair_own,
+    pair_other,
+    wide_y,
+    wide_x,
+    wide_z,
+    pair_y,
+    pair_x,
+    pair_z,
+    far,
+    partial,
+    partial_in,
+    tiny,
+    tiny_t,
+    tiny_d,
+    y_out,
+    y_in,
+    x_out,
+    x_in,
+    z_out,
+    z_in,
+    g_out,
+    g_in,
+    h_out,
+    h_in,
+    f_out,
+    f_in,
+    c_out,
+    c_in,
+    p_out,
+    p_in,
+    t_out,
+    t_in,
+    d_out,
+    d_in,
+):
+    place = lax.axis_index("tensor")
+    group = lax.axis_index("dp")
+    core, side = place % 2, place // 2
     rows = q_ref.shape[0]
-    c = pl.multiple_of(c, HALF)
+    own_rows = rows // 2
+    pairs = q_ref.shape[1] // (2 * HD)
+    a = side * HALF
+    c = pl.multiple_of((1 - side) * 2 * LEN, HALF)
+
+    barrier = pltpu.get_barrier_semaphore()
+    for step in (1, 2, 3):
+        pl.semaphore_signal(barrier, inc=1, device_id={"tensor": (place + step) % 4}, device_id_type=MESH)
+
+    def greet(step, _):
+        peer = (group + step) % groups
+        pl.semaphore_signal(barrier, inc=1, device_id={"dp": peer}, device_id_type=MESH)
+        return 0
+
+    lax.fori_loop(1, groups, greet, 0)
+    pl.semaphore_wait(barrier, 3 + groups - 1)
+
+    units = []
+    for own, other, total, base in ((outer_own, outer_other, outer_total, 0), (inner_own, inner_other, inner_total, 3)):
+        for i in range(3):
+            units.append(
+                Unit(
+                    lambda s, r=own, i=i: r.at[s, i],
+                    lambda s, r=other, i=i: r.at[s, i],
+                    wide_y.at[base + i],
+                    wide_x.at[base + i],
+                    lambda s, n=base + i: wide_z.at[n, s],
+                    lambda s, r=total, i=i: r.at[s, i],
+                )
+            )
+    for j in range(pairs):
+        units.append(
+            Unit(
+                lambda s, j=j: pair_own.at[j, s],
+                lambda s, j=j: pair_other.at[j, s],
+                pair_y.at[j],
+                pair_x.at[j],
+                lambda s, j=j: pair_z.at[j, s],
+                lambda s, j=j: attention_total.at[j, s],
+            )
+        )
+    sems = (y_out, y_in, x_out, x_in, z_out, z_in, g_out, g_in, h_out, h_in)
+    rounds = Rounds(units, groups, sems, far, f_out, f_in)
+
     kc[pl.ds(0, HALF), :] = k_ref[pl.ds(c, HALF), :]
     kc[pl.ds(HALF, HALF), :] = k_ref[pl.ds(rows, HALF), :]
     vc[pl.ds(0, HALF), :] = v_ref[pl.ds(c, HALF), :]
     vc[pl.ds(HALF, HALF), :] = v_ref[pl.ds(rows, HALF), :]
 
-    def pair(j, _):
-        lanes = pl.ds(pl.multiple_of(j * 2 * HD, 2 * HD), 2 * HD)
-        for start, at, count in ((a, 0, LEN), (b, LEN, LEN), (c, 2 * LEN, HALF)):
-            start = pl.multiple_of(start, HALF)
-            queries = q_ref[pl.ds(start, count), lanes]
-            grads = g_ref[pl.ds(start, count), lanes]
-            if count == LEN:
-                keys = k_ref[pl.ds(start, LEN), lanes]
-                values = v_ref[pl.ds(start, LEN), lanes]
-            else:
-                keys = kc[:, lanes]
-                values = vc[:, lanes]
-            bias = bias_ref[:, pl.ds(at, count)]
-            dqs, dks, dvs = [], [], []
-            for h in range(2):
-                cols = slice(h * HD, (h + 1) * HD)
-                row = lse_ref[pl.ds(j * 2 + h, 1), pl.ds(at, count)]
-                logits = dg(keys[:, cols], queries[:, cols], NT) * (SCALE * LOG2E) + bias
-                probs = jnp.exp2(logits - row)
-                dprobs = dg(values[:, cols], grads[:, cols], NT)
-                across = jnp.sum(probs * dprobs, axis=0, keepdims=True)
-                dscores = (probs * (dprobs - across) * SCALE).astype(BF16)
-                dvs.append(dg(probs.astype(BF16), grads[:, cols], NN).astype(BF16))
-                dks.append(dg(dscores, queries[:, cols], NN).astype(BF16))
-                dqs.append(dg(dscores, keys[:, cols], TN).astype(BF16))
-            dq_ref[pl.ds(start, count), lanes] = jnp.concatenate(dqs, axis=1)
-            dk, dv = jnp.concatenate(dks, axis=1), jnp.concatenate(dvs, axis=1)
-            if count == LEN:
-                dk_ref[pl.ds(start, LEN), lanes] = dk
-                dv_ref[pl.ds(start, LEN), lanes] = dv
-            else:
-                dk_ref[pl.ds(start, HALF), lanes] = dk[:HALF]
-                dv_ref[pl.ds(start, HALF), lanes] = dv[:HALF]
-                dk_ref[pl.ds(rows, HALF), lanes] = dk[HALF:]
-                dv_ref[pl.ds(rows, HALF), lanes] = dv[HALF:]
+    def lanes_of(j):
+        return pl.ds(pl.multiple_of(j * 2 * HD, 2 * HD), 2 * HD)
+
+    def half_pair(j, _):
+        lanes = lanes_of(j)
+        at = pl.ds(2 * LEN, HALF)
+        stats = [lse_ref[pl.ds(j * 2 + h, 1), at] for h in range(2)]
+        mine = pl.ds(c, HALF)
+        d_q, d_k, d_v = pair_back(
+            q_ref[mine, lanes], kc[:, lanes], vc[:, lanes], g_ref[mine, lanes], bias_ref[:, at], stats
+        )
+        dq[mine, lanes] = d_q
+        dk[mine, lanes] = d_k[:HALF]
+        dv[mine, lanes] = d_v[:HALF]
+        away[0, :, lanes] = d_k[HALF:]
+        away[1, :, lanes] = d_v[HALF:]
         return 0
 
-    lax.fori_loop(0, q_ref.shape[1] // (2 * HD), pair, 0)
+    lax.fori_loop(0, pairs, half_pair, 0)
+    swap = rounds.copy(away, back, c_out, c_in, {"tensor": (place + 2) % 4})
+    rounds.start(swap)
+    for u in range(6):
+        rounds.y_start(u)
+
+    def whole_pair(j):
+        def body(i, _):
+            lanes = lanes_of(j)
+            mine = pl.ds(pl.multiple_of(a + i * LEN, HALF), LEN)
+            at = pl.ds(pl.multiple_of(i * LEN, LEN), LEN)
+            stats = [lse_ref[pl.ds(j * 2 + h, 1), at] for h in range(2)]
+            d_q, d_k, d_v = pair_back(
+                q_ref[mine, lanes], k_ref[mine, lanes], v_ref[mine, lanes], g_ref[mine, lanes], bias_ref[:, at], stats
+            )
+            dq[mine, lanes] = d_q
+            dk[mine, lanes] = d_k
+            dv[mine, lanes] = d_v
+            return 0
+
+        lax.fori_loop(0, 2, body, 0)
+
+    def add_share(j):
+        lanes = lanes_of(j)
+        mine = pl.ds(c, HALF)
+        for i, grads in ((0, dk), (1, dv)):
+            share = swap_halves(back[i, :, lanes]).astype(F32)
+            grads[mine, lanes] = (grads[mine, lanes].astype(F32) + share).astype(BF16)
+
+    def weight_pair(j):
+        lanes = lanes_of(j)
+        block = x_ref.shape[1] // 2
+
+        def body(i, _):
+            columns = pl.ds(pl.multiple_of(i * block, 128), block)
+            left = x_ref[:, columns]
+            parts = [dg(left, grads[:, lanes], TN) for grads in (dq, dk, dv)]
+            parts.append(dg(branch_ref[:, columns], ctx_ref[:, lanes], TN))
+            own = jnp.concatenate([p[:, :HD] for p in parts], axis=1).astype(BF16)
+            other = jnp.concatenate([p[:, HD:] for p in parts], axis=1).astype(BF16)
+            where = pl.ds(i * 4, 4)
+            pair_own[j, where] = own.reshape(4, block // 4, 4 * HD)
+            pair_other[j, where] = other.reshape(4, block // 4, 4 * HD)
+            return 0
+
+        lax.fori_loop(0, 2, body, 0)
+        rounds.y_start(6 + j)
+
+    def input_rows(start):
+        both = pairs * 2 * HD
+        mine = pl.ds(pl.multiple_of(start, 128), own_rows)
+        value = dg(dq[mine, :], w_ref[:, pl.ds(0, both)], NT)
+        value = value + dg(dk[mine, :], w_ref[:, pl.ds(both, both)], NT)
+        return value + dg(dv[mine, :], w_ref[:, pl.ds(2 * both, both)], NT)
+
+    whole_pair(0)
+    rounds.x_start(0)
+    swap.wait_recv()
+    for j in range(pairs):
+        add_share(j)
+    weight_pair(0)
+    rounds.x_start(1)
+    rounds.z_start(0)
+    whole_pair(1)
+    rounds.g_start(0)
+    rounds.z_start(1)
+    rounds.x_start(2)
+    weight_pair(1)
+    rounds.h_start(0)
+    rounds.g_start(1)
+    rounds.z_start(2)
+    whole_pair(2)
+    rounds.x_start(3)
+    weight_pair(2)
+    rounds.h_start(1)
+    rounds.g_start(2)
+
+    width = 3 * HD
+    tiny[...] = small_ref[...]
+
+    def bias_sum(grads):
+        total = jnp.sum(grads[...].astype(F32), axis=0, keepdims=True)
+        heads = [total[:, i * HD : (i + 1) * HD] for i in range(2 * pairs)]
+        return jnp.concatenate(heads[0::2], axis=1), jnp.concatenate(heads[1::2], axis=1)
+
+    for grads, at in ((dq, 2 * width), (dv, 3 * width)):
+        mine, theirs = bias_sum(grads)
+        tiny[place, pl.ds(1, 1), pl.ds(at, width)] = mine
+        tiny[(place + 2) % 4, pl.ds(1, 1), pl.ds(at, width)] = theirs
+    tiny_copies = []
+    for step in (1, 2, 3):
+        peer = (place + step) % 4
+        tiny_copies.append(
+            rounds.copy(tiny.at[peer], tiny_t.at[step - 1], t_out.at[step - 1], t_in.at[step - 1], {"tensor": peer})
+        )
+        rounds.start(tiny_copies[-1])
+
+    partial[...] = input_rows((1 - core) * own_rows).astype(BF16)
+    trade = rounds.copy(partial, partial_in, p_out, p_in, {"tensor": place + 1 - 2 * core})
+    rounds.start(trade)
+    mine = input_rows(core * own_rows) + residual_ref[...]
+    trade.wait_recv()
+    tokens_out[...] = (mine + partial_in[...].astype(F32)).astype(BF16)
+
+    total = tiny[place]
+    for step in (1, 2, 3):
+        tiny_copies[step - 1].wait_recv()
+        total = total + tiny_t[step - 1]
+    tiny_d[0] = total
+
+    def tell(step, _):
+        peer = (group + step) % groups
+        rounds.copy(tiny_d.at[0], tiny_d.at[step], d_out.at[step], d_in.at[step], {"dp": peer}).start()
+        return 0
+
+    lax.fori_loop(1, groups, tell, 0)
+
+    rounds.x_start(4)
+    rounds.z_start(3)
+    rounds.h_start(2)
+    rounds.x_start(5)
+    rounds.z_start(4)
+    rounds.g_start(3)
+    rounds.x_start(6)
+    rounds.z_start(5)
+    rounds.g_start(4)
+    rounds.h_start(3)
+    rounds.x_start(7)
+    rounds.z_start(6)
+    rounds.g_start(5)
+    rounds.h_start(4)
+    rounds.x_start(8)
+    rounds.z_start(7)
+    rounds.g_start(6)
+    rounds.h_start(5)
+    rounds.z_start(8)
+    rounds.g_start(7)
+    rounds.h_start(6)
+    rounds.g_start(8)
+    rounds.h_start(7)
+    rounds.h_start(8)
+
+    def hear(step, total):
+        copy = rounds.copy(tiny_d.at[0], tiny_d.at[step], d_out.at[step], d_in.at[step], {"dp": group})
+        copy.wait_recv()
+        copy.wait_send()
+        return total + tiny_d[step]
+
+    small_out[...] = lax.fori_loop(1, groups, hear, tiny_d[0])
+    for u in range(9):
+        rounds.end(u)
+    rounds.drain()
 
 
 IN_VMEM = pl.BlockSpec(memory_space=pltpu.VMEM)
@@ -149,6 +539,77 @@
         scratch_shapes=scratch,
         cost_estimate=pl.CostEstimate(flops=flops, bytes_accessed=moved, transcendentals=0),
         compiler_params=pltpu.CompilerParams(vmem_limit_bytes=48 << 20),
+    )(*operands)
+
+
+def rear_call(groups, operands):
+    q, k, residual, owned = operands[0], operands[1], operands[10], operands[11]
+    rows, both = q.shape
+    own_rows, wide = residual.shape
+    pairs = both // (2 * HD)
+    eighth = wide // 8
+    more = groups // 8
+    dma = pltpu.SemaphoreType.DMA
+    outs = [
+        jax.ShapeDtypeStruct(owned.shape, BF16),
+        jax.ShapeDtypeStruct(owned.shape, BF16),
+        jax.ShapeDtypeStruct((pairs, 8, eighth, 4 * HD), BF16),
+        jax.ShapeDtypeStruct((own_rows, wide), BF16),
+        jax.ShapeDtypeStruct((3, wide), F32),
+    ]
+    third = owned.shape[2]
+    scratch = [
+        pltpu.VMEM((LEN, both), BF16),
+        pltpu.VMEM((LEN, both), BF16),
+        pltpu.VMEM((rows, both), BF16),
+        pltpu.VMEM((rows, both), BF16),
+        pltpu.VMEM((rows, both), BF16),
+        pltpu.VMEM((2, HALF, both), BF16),
+        pltpu.VMEM((2, HALF, both), BF16),
+        pltpu.VMEM((pairs, 8, eighth, 4 * HD), BF16),
+        pltpu.VMEM((pairs, 8, eighth, 4 * HD), BF16),
+        pltpu.VMEM((6, 8, third, wide), BF16),
+        pltpu.VMEM((6, 4, third, wide), BF16),
+        pltpu.VMEM((6, 3, third, wide), BF16),
+        pltpu.VMEM((pairs, 8, eighth, 4 * HD), BF16),
+        pltpu.VMEM((pairs, 4, eighth, 4 * HD), BF16),
+        pltpu.VMEM((pairs, 3, eighth, 4 * HD), BF16),
+        pltpu.VMEM((9, more - 1, eighth, wide) if more > 1 else (1, 1, 16, 128), BF16),
+        pltpu.VMEM((own_rows, wide), BF16),
+        pltpu.VMEM((own_rows, wide), BF16),
+        pltpu.VMEM((4, 3, wide), F32),
+        pltpu.VMEM((3, 3, wide), F32),
+        pltpu.VMEM((groups, 3, wide), F32),
+        dma((9,)),
+        dma((9,)),
+        dma((9,)),
+        dma((9,)),
+        dma((9, 3)),
+        dma((9, 3)),
+        dma((9, 3)),
+        dma((9, 3)),
+        dma((9,)),
+        dma((9,)),
+        dma((9, max(more - 1, 1))),
+        dma((9, max(more - 1, 1))),
+        dma,
+        dma,
+        dma,
+        dma,
+        dma((3,)),
+        dma((3,)),
+        dma((groups,)),
+        dma((groups,)),
+    ]
+    return pl.pallas_call(
+        functools.partial(rear_kernel, groups),
+        out_shape=outs,
+        in_specs=[IN_VMEM] * len(operands),
+        out_specs=[IN_VMEM] * len(outs),
+        scratch_shapes=scratch,
+        compiler_params=pltpu.CompilerParams(
+            collective_id=0, has_side_effects=True, vmem_limit_bytes=62 << 20
+        ),
     )(*operands)
 
 
@@ -207,6 +668,7 @@
     second_shift,
     cotangent,
 ):
+    groups = lax.axis_size("dp")
     place = lax.axis_index("tensor")
     core, side = place % 2, place // 2
     own_rows, wide = tokens.shape
@@ -283,11 +745,9 @@
     grad_b_outer = jnp.sum(grad_feed.astype(F32), axis=0)
     feed_rows = both_cores(grad_feed)
     grad_w_down = dg(hidden, feed_rows, TN).astype(BF16)
-    outer_away = to_side(grad_w_down[units:])
     grad_inner = (dg(feed_rows, w_down, NT) * slope.astype(F32)).astype(BF16)
     grad_b_in = jnp.sum(grad_inner.astype(F32), axis=0)
     grad_w_in = dg(first_rows, grad_inner, TN).astype(BF16)
-    inner_away = to_side(grad_w_in[:, units:])
     grad_first = grad_second + sum_cores(dg(grad_inner, w_in, NT))
     grad_branch = norm_backward(grad_first, first_unit, first_inverse, first_gain)
     grad_first_gain = jnp.sum(grad_first * first_unit, axis=0)
@@ -295,84 +755,59 @@
     grad_attended = grad_branch.astype(BF16)
     grad_b_output = jnp.sum(grad_attended.astype(F32), axis=0)
     branch_rows = both_cores(grad_attended)
-    grad_w_out = dg(branch_rows, context, TN).astype(BF16)
     grad_context = dg(branch_rows, w_out).astype(BF16)
-    grad_queries, grad_keys, grad_values = local_call(
-        attend_backward,
-        [
-            jax.ShapeDtypeStruct((chip_rows, both), BF16),
-            jax.ShapeDtypeStruct((chip_rows + HALF, both), BF16),
-            jax.ShapeDtypeStruct((chip_rows + HALF, both), BF16),
-        ],
-        pairs_scratch,
-        10 * chip_rows * LEN * both,
-        (queries, keys, values, grad_context, bias, lse),
+    weights_joined = jnp.concatenate(parts, axis=1)
+    small = jnp.stack(
+        [grad_b_output, grad_first_gain, grad_first_shift, grad_b_outer, grad_second_gain, grad_second_shift]
     )
-    away = to_side(jnp.concatenate([grad_keys[chip_rows:], grad_values[chip_rows:]], axis=1))
-
-    def add_c(grads, share):
-        mine = lax.dynamic_slice_in_dim(grads, c_start, HALF, 0)
-        summed = (mine.astype(F32) + share.astype(F32)).astype(BF16)
-        return lax.dynamic_update_slice_in_dim(grads[:chip_rows], summed, c_start, 0)
-
-    away_keys = interleave(*reversed(split_pairs(away[:, :both])))
-    away_values = interleave(*reversed(split_pairs(away[:, both:])))
-    grad_joined = jnp.concatenate(
-        [grad_queries, add_c(grad_keys, away_keys), add_c(grad_values, away_values)], axis=1
+    small = small.reshape(6, 4, width).transpose(1, 0, 2).reshape(4, 6 * width)
+    index = jnp.arange(4)[:, None]
+    bias_flat = jnp.where(
+        index == place, grad_b_in[:units], jnp.where(index == (place + 2) % 4, grad_b_in[units:], 0.0)
     )
-    weights_joined = jnp.concatenate(parts, axis=1)
-    grad_w_joined = dg(rows, grad_joined, TN).astype(BF16)
-    grad_bias = jnp.sum(grad_joined.astype(F32), axis=0, keepdims=True)
-    grad_tokens = (grad_branch + sum_cores(dg(grad_joined, weights_joined, NT))).astype(BF16)
-
-    pieces = [split_pairs(grad_w_joined[:, i * both : (i + 1) * both]) for i in range(3)]
-    pieces.append(split_pairs(grad_w_out))
-    attention_own = jnp.concatenate([p[0] for p in pieces], axis=1)
-    attention_away = to_side(jnp.concatenate([p[1] for p in pieces], axis=1))
-
-    def over_groups(own, theirs):
-        return lax.psum((own.astype(F32) + theirs.astype(F32)).astype(BF16), "dp").astype(F32)
-
-    outer_sum = over_groups(grad_w_down[:units], outer_away)
-    inner_sum = over_groups(grad_w_in[:, :units], inner_away)
-    attention_sum = over_groups(attention_own, attention_away)
-
-    small = jnp.stack(
-        [
-            grad_b_output,
-            grad_first_gain,
-            grad_first_shift,
-            grad_b_outer,
-            grad_second_gain,
-            grad_second_shift,
-        ]
+    small = jnp.concatenate([small, jnp.zeros((4, 2 * width), F32), bias_flat], axis=1).reshape(4, 3, wide)
+    by_owner = (8, 3, wide // 24, wide)
+    inner_sum, outer_sum, attention_sum, grad_tokens, total = rear_call(
+        groups,
+        (
+            queries,
+            keys,
+            values,
+            grad_context,
+            bias,
+            lse,
+            rows,
+            context,
+            branch_rows,
+            weights_joined,
+            grad_branch,
+            grad_w_in[:, :units].reshape(by_owner),
+            grad_w_in[:, units:].reshape(by_owner),
+            grad_w_down[:units].reshape(by_owner),
+            grad_w_down[units:].reshape(by_owner),
+            small,
+        ),
     )
-    small_flat = small.reshape(6, 4, wide // 4).transpose(1, 0, 2).reshape(4, -1)
-    biases = [split_pairs(grad_bias[:, :both]), split_pairs(grad_bias[:, 2 * both :])]
-    bias_rows = [
-        jnp.concatenate([biases[0][i][0], biases[1][i][0], grad_b_in[i * units : (i + 1) * units]]) for i in range(2)
-    ]
-    index = jnp.arange(4)[:, None]
-    bias_flat = jnp.where(index == place, bias_rows[0], jnp.where(index == place ^ 2, bias_rows[1], 0.0))
-    totals = lax.psum(jnp.concatenate([small_flat, bias_flat], axis=1), ("dp", "tensor"))
-    total = lax.dynamic_index_in_dim(totals, place, 0, keepdims=False)
+    attention_sum = attention_sum.reshape(3, wide, 4, HD).transpose(2, 1, 0, 3).reshape(4, wide, width)
+    attention_sum = attention_sum.astype(F32)
+    total = total.reshape(-1)
     shares = total[: 6 * width].reshape(6, width)
     rest = total[6 * width :]
     return (
         output,
         grad_tokens,
-        attention_sum[:, :width],
+        attention_sum[0],
         rest[:width],
-        attention_sum[:, width : 2 * width],
-        attention_sum[:, 2 * width : 3 * width],
+        attention_sum[1],
+        attention_sum[2],
         rest[width : 2 * width],
-        attention_sum[:, 3 * width :].T,
+        attention_sum[3].T,
         shares[0],
         shares[1],
         shares[2],
-        inner_sum,
+        inner_sum.reshape(wide, units).astype(F32),
         rest[2 * width :],
-        outer_sum,
+        outer_sum.reshape(units, wide).astype(F32),
         shares[3],
         shares[4],
         shares[5],

time: 445 us -> 379 us (0.85)
  Pallas kernels: 26.5 us -> 178 us
  waiting for transfers between devices: 205 us -> 70.1 us
  blocking collectives: 43.6 us -> 0 us
  between operations: 15.3 us -> 1.83 us
  other arithmetic: 42.6 us -> 32.1 us
  local copies, waits for them, and re-layouts: 47.6 us -> 41.3 us
  starting transfers between devices: 15 us -> 9.96 us
    pallas_call x0 -> x1, Pallas kernels: none -> 168 us  [rear_call(): pl.pallas_call(functools.partial(rear_kernel, groups), out_shape=outs, in...]
    psum x1 -> x0, waiting for transfers between devices: 77.7 us -> none  [over_groups(): lax.psum((own.astype(F32) + theirs.astype(F32)).astype(BF16), 'dp')]
    ppermute x10 -> x6, waiting for transfers between devices: 119 us -> 66.7 us  [to_side(): return lax.ppermute(value, 'tensor', [(i, i ^ 2) for i in range(4)])]
    psum x1 -> x0, blocking collectives: 43.6 us -> none  [shards(): lax.psum(jnp.concatenate([small_flat, bias_flat], axis=1), ('dp', 'tensor'))]
    pallas_call x2 -> x1, Pallas kernels: 26.5 us -> 10.4 us  [local_call(): pl.pallas_call(kernel, out_shape=outs, in_specs=[IN_VMEM] * len(operands)...]
    convert_element_type x9 -> x2, other arithmetic: 15 us -> 3.3 us  [the longest x1 1.65 us: shards(): outer_sum.reshape(units, wide).astype(F32)]
    reshape x3 -> x6, local copies, waits for them, and re-layouts: 1.61 us -> 7.79 us  [the longest x3 6.35 us: interleave(): return both.reshape(rows, 2 * width)]
    slice x24 -> x4, local copies, waits for them, and re-layouts: 12 us -> 6.27 us  [the longest x1 3.13 us: shards(): attention_sum[3]]
  transfers between devices with their start and end apart: 19 -> 13, of which waited for: 12 -> 7; matrix products, arithmetic and copies ran while one was open for 18% -> 13% of each run, Pallas kernels for 4% -> 0%
where the time goes in v2:
time: 379 us; the launch traced here: 373 us
  Pallas kernels  178 us (47%)
  waiting for transfers between devices  70.1 us (18%)
  local copies, waits for them, and re-layouts  41.3 us (11%)
  matrix products  39.9 us (11%)
  other arithmetic  32.1 us (8%)
  starting transfers between devices  9.96 us (3%)
    pallas_call x1, Pallas kernels, rear_call(): pl.pallas_call(functools.partial(rear_kernel, groups), out_shape=outs, in...  168 us
    ppermute x6, waiting for transfers between devices, to_side(): return lax.ppermute(value, 'tensor', [(i, i ^ 2) for i in range(4)])  66.7 us
    dot_general x11, matrix products, dg(): return lax.dot_general(left, right, dims, preferred_element_type=F32)  39.9 us
    pallas_call x1, Pallas kernels, local_call(): pl.pallas_call(kernel, out_shape=outs, in_specs=[IN_VMEM] * len(operands)...  10.4 us
    ppermute x6, starting transfers between devices, to_side(): return lax.ppermute(value, 'tensor', [(i, i ^ 2) for i in range(4)])  8.39 us
    unnamed x117, local copies, waits for them, and re-layouts  8.13 us
  transfers between devices with their start and end apart: 13, of which 7 were waited for; matrix products, arithmetic and copies ran while one was open for 13% of the time, Pallas kernels for 0%

profile of v2, /device:TPU:0, one launch (start us, length us, event | category | flops | bytes accessed | tf_op | source)
XLA Modules:
  0.0 373.4 jit_solution(6798752037586748045)
XLA Ops:
  1.2 2.1 pad_maximum_fusion.5
  3.3 2.5 collective-permute-start.1
  6.6 2.0 collective-permute-start.4
  16.7 10.0 %collective-permute-done.2 = f32[1152]{0:T(1024)S(1)} collective-permute-done((f32[1152]{0:T(1024)S(1)}, f32[1152]{0:T(1024)S(1)}, u32[]{:S(2)}, u32[]{:S(2)}) %collective-permute-start.2) | collective-permute-done | bytes 4640 | tf_op jit(solution)/shard_map/ppermute | solution.py:684
  27.1 5.7 %collective-permute-done.4 = bf16[192,768]{1,0:T(8,128)(2,1)S(1)} collective-permute-done((bf16[192,768]{1,0:T(8,128)(2,1)}, bf16[192,768]{1,0:T(8,128)(2,1)S(1)}, u32[]{:S(2)}, u32[]{:S(2)}) %collective-permute-start.4) | collective-permute-done | bytes 294944 | tf_op jit(solution)/shard_map/ppermute | solution.py:684
  34.4 2.1 maximum_select_fusion.x_ref
  36.5 1.8 collective-permute-start.3
  39.6 7.9 %collective-permute-done.3 = bf16[256,768]{1,0:T(8,128)(2,1)S(1)} collective-permute-done((bf16[256,768]{1,0:T(8,128)(2,1)S(1)}, bf16[256,768]{1,0:T(8,128)(2,1)S(1)}, u32[]{:S(2)}, u32[]{:S(2)}) %collective-permute-start.3) | collective-permute-done | bytes 393248 | tf_op jit(solution)/shard_map/ppermute | solution.py:684
  50.4 10.4 %shard_map.314 = (bf16[1280,384]{1,0:T(8,128)(2,1)S(1)}, f32[8,1280]{1,0:T(8,128)S(1)}) custom-call(bf16[1280,384]{1,0:T(8,128)(2,1)S(1)} %fusion.6.q_ref, bf16[1536,384]{1,0:T(8,128)(2,1)S(1)} %convolution_convert_fusion.3.k_ref, bf16[1536,384]{1,0:T(8,128)(2,1)S(1)} %fusion.7.v_ref, f32[512,1280]{1,0:T(8,128)} %pad_maximum_fusion.bias_ref), custom_call_target="tpu_custom_call" | custom-call | flops 1006632960 | bytes 5963776 | tf_op jit(solution)/shard_map/pallas_call | solution.py:534
  67.1 2.3 fusion.29
  73.6 19.6 %collective-permute-done.7 = bf16[768,768]{1,0:T(8,128)(2,1)} collective-permute-done((bf16[768,768]{1,0:T(8,128)(2,1)}, bf16[768,768]{1,0:T(8,128)(2,1)}, u32[]{:S(2)}, u32[]{:S(2)}) %collective-permute-start.7) | collective-permute-done | bytes 1179680 | tf_op jit(solution)/shard_map/ppermute | solution.py:684
  94.6 23.5 %collective-permute-done.8 = bf16[768,768]{1,0:T(8,128)(2,1)} collective-permute-done((bf16[768,768]{1,0:T(8,128)(2,1)}, bf16[768,768]{1,0:T(8,128)(2,1)}, u32[]{:S(2)}, u32[]{:S(2)}) %collective-permute-start.8) | collective-permute-done | bytes 1179680 | tf_op jit(solution)/shard_map/ppermute | solution.py:684
  119.5 7.3 %multiply_convert_fusion = (bf16[1280,1536]{1,0:T(8,128)(2,1)S(1)}, f32[1280,1536]{1,0:T(8,128)}) fusion(f32[1536]{0:T(1024)S(1)} %pad_maximum_fusion.11, bf16[768,1536]{1,0:T(8,128)(2,1)S(1)} %constant_dynamic-update-slice_fusion, bf16[640,768]{1,0:T(8,128)(2,1)S(1)} %collective-permute-done.6, bf16[640,768]{1,0:T(8,128)(2,1)S(1)} %add_convert_fusion.1, ...), kind=kOutput, calls=%fused_computation.9 | convolution fusion | flops 3040542720 | bytes 16128001 | tf_op jit(solution)/shard_map/dot_general | solution.py:26
  126.9 3.3 fusion.40
  130.4 2.6 collective-permute-done.9
  137.2 2.2 convert_reduce_fusion.2
  140.7 2.1 copy.46
  142.8 2.1 copy.47
  144.9 2.1 copy.48
  147.0 2.8 pad_maximum_fusion.2.w_ref
  153.9 9.3 %convert_reduce_fusion = (f32[1536]{0:T(1024)S(1)}, bf16[1280,1536]{1,0:T(8,128)(2,1)S(1)}) fusion(f32[1280,1536]{1,0:T(8,128)} %get-tuple-element.81, bf16[1536,768]{1,0:T(8,128)(2,1)} %copy-done.23, bf16[640,768]{1,0:T(8,128)(2,1)} %collective-permute-done.10, bf16[640,768]{1,0:T(8,128)(2,1)} %get-tuple-element.40, pred[]{:T(512)S(6)} %eq.118), kind=kOutput, calls=%fused_computation.8 | convolution fusion | flops 3056269824 | bytes 16128001 | tf_op jit(solution)/shard_map/dot_general | solution.py:26
  163.2 3.3 fusion.41
  167.0 5.9 %convolution_convert_fusion = bf16[1536,768]{1,0:T(8,128)(2,1)S(1)} fusion(bf16[1280,1536]{1,0:T(8,128)(2,1)S(1)} %copy-done.56, bf16[640,768]{1,0:T(8,128)(2,1)} %collective-permute-done.10, bf16[640,768]{1,0:T(8,128)(2,1)} %get-tuple-element.40, pred[]{:T(512)S(6)} %eq.118), kind=kOutput, calls=%fused_computation.12 | convolution fusion | flops 3029925888 | bytes 8257537 | tf_op jit(solution)/shard_map/dot_general | solution.py:26
  175.3 3.5 convolution_convert_fusion.1
  179.0 3.4 multiply_reduce_fusion
  182.4 1.9 convert_reduce_fusion.3
  187.2 2.1 maximum_select_fusion.3.branch_ref
  189.3 2.1 convolution_convert_fusion.2.g_ref
  191.4 167.8 %shard_map.315 = (bf16[8,3,32,768]{3,2,1,0:T(8,128)(2,1)}, bf16[8,3,32,768]{3,2,1,0:T(8,128)(2,1)}, bf16[3,8,96,256]{3,2,1,0:T(8,128)(2,1)}, bf16[640,768]{1,0:T(8,128)(2,1)}, f32[3,768]{1,0:T(4,128)}) custom-call(bf16[1280,384]{1,0:T(8,128)(2,1)} %copy-done.3, bf16[1536,384]{1,0:T(8,128)(2,1)} %copy-done.1, bf16[1536,384]{1,0:T(8,128)(2,1)} %copy-done.2, ...), custom_call_target="tpu_custom_call" | custom-call | tf_op jit(solution)/shard_map/pallas_call | solution.py:604
  361.2 1.9 copy.50
  363.1 2.0 reshape.258
  365.1 3.1 fusion.30
  (210 shorter events, 50.9 us)
Async XLA Ops:
  0.7 33.2 %collective-permute-start = (bf16[640,768]{1,0:T(8,128)(2,1)}, bf16[640,768]{1,0:T(8,128)(2,1)}, u32[]{:S(2)}, u32[]{:S(2)}) collective-permute-start(bf16[640,768]{1,0:T(8,128)(2,1)} %param.19), channel_id=1, source_target_pairs={{0,1},{1,0},{2,3},{3,2},{4,5},{5,4},{6,7},{7,6},{8,9},{9,8},{10,11... | collective-permute-start | bytes 2949128 | tf_op jit(solution)/shard_map/ppermute | solution.py:681
  3.3 29.6 %collective-permute-start.1 = (bf16[768,576]{0,1:T(8,128)(2,1)}, bf16[768,576]{0,1:T(8,128)(2,1)S(1)}, u32[]{:S(2)}, u32[]{:S(2)}) collective-permute-start(bf16[768,576]{0,1:T(8,128)(2,1)} %pad_maximum_fusion.5), channel_id=1, source_target_pairs={{0,2},{1,3},{2,0},{3,1},{4,6},{5,7},{6,4},{7,5},{8,10},{9,11},{10,... | collective-permute-start | bytes 2654216 | tf_op jit(solution)/shard_map/ppermute | solution.py:684
  6.6 20.1 %collective-permute-start.2 = (f32[1152]{0:T(1024)S(1)}, f32[1152]{0:T(1024)S(1)}, u32[]{:S(2)}, u32[]{:S(2)}) collective-permute-start(f32[1152]{0:T(1024)S(1)} %concatenate.65), channel_id=1, source_target_pairs={{0,2},{1,3},{2,0},{3,1},{4,6},{5,7},{6,4},{7,5},{8,10},{9,11},{10,... | collective-permute-start | bytes 13832 | tf_op jit(solution)/shard_map/ppermute | solution.py:684
  6.6 26.2 %collective-permute-start.4 = (bf16[192,768]{1,0:T(8,128)(2,1)}, bf16[192,768]{1,0:T(8,128)(2,1)S(1)}, u32[]{:S(2)}, u32[]{:S(2)}) collective-permute-start(bf16[192,768]{1,0:T(8,128)(2,1)} %param.27), channel_id=1, source_target_pairs={{0,2},{1,3},{2,0},{3,1},{4,6},{5,7},{6,4},{7,5},{8,10},{9,11},{10,... | collective-permute-start | bytes 884744 | tf_op jit(solution)/shard_map/ppermute | solution.py:684
  14.9 17.9 %copy-start.26 = (bf16[192,768]{1,0:T(8,128)(2,1)S(1)}, bf16[192,768]{1,0:T(8,128)(2,1)}, u32[]{:S(2)}) copy-start(bf16[192,768]{1,0:T(8,128)(2,1)} %param.27) | copy-start | bytes 884740
  16.6 16.4 %copy-start.17 = (bf16[768,192]{0,1:T(8,128)(2,1)S(1)}, bf16[768,192]{0,1:T(8,128)(2,1)}, u32[]{:S(2)}) copy-start(bf16[768,192]{0,1:T(8,128)(2,1)} %param.25) | copy-start | bytes 884740
  26.7 6.1 %copy-start.44 = (f32[1152]{0:T(1024)}, f32[1152]{0:T(1024)S(1)}, u32[]{:S(2)}) copy-start(f32[1152]{0:T(1024)S(1)} %collective-permute-done.2) | copy-start | bytes 13828
  33.1 15.8 %copy-start.12 = (bf16[768,3,2,64]{0,3,2,1:T(8,128)(2,1)}, bf16[768,3,2,64]{0,3,2,1:T(8,128)(2,1)S(1)}, u32[]{:S(2)}) copy-start(bf16[768,3,2,64]{0,3,2,1:T(8,128)(2,1)S(1)} %pad_maximum_fusion.8) | copy-start | bytes 1769476
  33.8 13.6 %copy-start.13 = (bf16[768,3,2,64]{0,3,2,1:T(8,128)(2,1)}, bf16[768,3,2,64]{0,3,2,1:T(8,128)(2,1)S(1)}, u32[]{:S(2)}) copy-start(bf16[768,3,2,64]{0,3,2,1:T(8,128)(2,1)S(1)} %pad_maximum_fusion.7) | copy-start | bytes 1769476
  33.9 4.4 %copy-start.19 = (bf16[768,192]{0,1:T(8,128)(2,1)S(1)}, bf16[768,192]{0,1:T(8,128)(2,1)}, u32[]{:S(2)}) copy-start(bf16[768,192]{0,1:T(8,128)(2,1)} %param.22) | copy-start | bytes 884740
  36.4 12.5 %copy-start.8 = (bf16[1280,768]{1,0:T(8,128)(2,1)}, bf16[1280,768]{1,0:T(8,128)(2,1)S(1)}, u32[]{:S(2)}) copy-start(bf16[1280,768]{1,0:T(8,128)(2,1)S(1)} %maximum_select_fusion.x_ref) | copy-start | bytes 5898244
  36.5 11.0 %collective-permute-start.3 = (bf16[256,768]{1,0:T(8,128)(2,1)S(1)}, bf16[256,768]{1,0:T(8,128)(2,1)S(1)}, u32[]{:S(2)}, u32[]{:S(2)}) collective-permute-start(bf16[256,768]{1,0:T(8,128)(2,1)S(1)} %constant_dynamic-slice_fusion.2), channel_id=1, source_target_pairs={{0,2},{1,3},{2,0},{3,1},{4,6},{5,7},{6,4},{7,5},{8,10},{9,11},{10,... | collective-permute-start | bytes 1179656 | tf_op jit(solution)/shard_map/ppermute | solution.py:684
  39.6 10.8 %copy-start.3 = (bf16[1280,384]{1,0:T(8,128)(2,1)}, bf16[1280,384]{1,0:T(8,128)(2,1)S(1)}, u32[]{:S(2)}) copy-start(bf16[1280,384]{1,0:T(8,128)(2,1)S(1)} %fusion.6.q_ref) | copy-start | bytes 2949124
  50.4 10.4 %copy-start.2 = (bf16[1536,384]{1,0:T(8,128)(2,1)}, bf16[1536,384]{1,0:T(8,128)(2,1)S(1)}, u32[]{:S(2)}) copy-start(bf16[1536,384]{1,0:T(8,128)(2,1)S(1)} %fusion.7.v_ref) | copy-start | bytes 3538948
  62.0 5.1 %copy-start.47 = (f32[768]{0:T(1024)S(1)}, f32[768]{0:T(1024)}, u32[]{:S(2)}) copy-start(f32[768]{0:T(1024)} %param.28) | copy-start | bytes 9220
  64.2 2.9 collective-permute-start.5
  64.2 29.1 %collective-permute-start.7 = (bf16[768,768]{1,0:T(8,128)(2,1)}, bf16[768,768]{1,0:T(8,128)(2,1)}, u32[]{:S(2)}, u32[]{:S(2)}) collective-permute-start(bf16[768,768]{1,0:T(8,128)(2,1)} %param.31), channel_id=1, source_target_pairs={{0,2},{1,3},{2,0},{3,1},{4,6},{5,7},{6,4},{7,5},{8,10},{9,11},{10,... | collective-permute-start | bytes 3538952 | tf_op jit(solution)/shard_map/ppermute | solution.py:684
  65.7 52.4 %collective-permute-start.8 = (bf16[768,768]{1,0:T(8,128)(2,1)}, bf16[768,768]{1,0:T(8,128)(2,1)}, u32[]{:S(2)}, u32[]{:S(2)}) collective-permute-start(bf16[768,768]{1,0:T(8,128)(2,1)} %param.33), channel_id=1, source_target_pairs={{0,2},{1,3},{2,0},{3,1},{4,6},{5,7},{6,4},{7,5},{8,10},{9,11},{10,... | collective-permute-start | bytes 3538952 | tf_op jit(solution)/shard_map/ppermute | solution.py:684
  70.5 49.1 %copy-start.20 = (bf16[640,768]{1,0:T(8,128)(2,1)}, bf16[640,768]{1,0:T(8,128)(2,1)S(1)}, u32[]{:S(2)}) copy-start(bf16[640,768]{1,0:T(8,128)(2,1)S(1)} %add_convert_fusion.1) | copy-start | bytes 2949124
  70.5 49.0 %collective-permute-start.6 = (bf16[640,768]{1,0:T(8,128)(2,1)S(1)}, bf16[640,768]{1,0:T(8,128)(2,1)S(1)}, u32[]{:S(2)}, u32[]{:S(2)}) collective-permute-start(bf16[640,768]{1,0:T(8,128)(2,1)S(1)} %add_convert_fusion.1), channel_id=1, source_target_pairs={{0,1},{1,0},{2,3},{3,2},{4,5},{5,4},{6,7},{7,6},{8,9},{9,8},{10,11... | collective-permute-start | bytes 2949128 | tf_op jit(solution)/shard_map/ppermute | solution.py:681
  94.6 32.2 %copy-start.24 = (bf16[768,1536]{1,0:T(8,128)(2,1)}, bf16[768,1536]{1,0:T(8,128)(2,1)S(1)}, u32[]{:S(2)}) copy-start(bf16[768,1536]{1,0:T(8,128)(2,1)S(1)} %constant_dynamic-update-slice_fusion) | copy-start | bytes 7077892
  119.5 7.4 %copy-start.23 = (bf16[1536,768]{1,0:T(8,128)(2,1)}, bf16[1536,768]{1,0:T(8,128)(2,1)S(1)}, u32[]{:S(2)}) copy-start(bf16[1536,768]{1,0:T(8,128)(2,1)S(1)} %constant_dynamic-update-slice_fusion.2) | copy-start | bytes 7077892
  119.5 7.3 %copy-start.53 = (bf16[640,768]{1,0:T(8,128)(2,1)}, bf16[640,768]{1,0:T(8,128)(2,1)S(1)}, u32[]{:S(2)}) copy-start(bf16[640,768]{1,0:T(8,128)(2,1)S(1)} %collective-permute-done.6) | copy-start | bytes 2949124
  130.3 2.6 collective-permute-start.9
  139.4 14.4 %collective-permute-start.10 = (bf16[640,768]{1,0:T(8,128)(2,1)}, bf16[640,768]{1,0:T(8,128)(2,1)}, u32[]{:S(2)}, u32[]{:S(2)}) collective-permute-start(bf16[640,768]{1,0:T(8,128)(2,1)} %get-tuple-element.40), channel_id=1, source_target_pairs={{0,1},{1,0},{2,3},{3,2},{4,5},{5,4},{6,7},{7,6},{8,9},{9,8},{10,11... | collective-permute-start | bytes 2949128 | tf_op jit(solution)/shard_map/ppermute | solution.py:681
  153.9 9.3 %copy-start.25 = (bf16[768,1536]{1,0:T(8,128)(2,1)S(1)}, bf16[768,1536]{1,0:T(8,128)(2,1)}, u32[]{:S(2)}) copy-start(bf16[768,1536]{1,0:T(8,128)(2,1)} %copy-done.24) | copy-start | bytes 7077892
  163.2 3.8 %copy-start.56 = (bf16[1280,1536]{1,0:T(8,128)(2,1)S(1)}, bf16[1280,1536]{1,0:T(8,128)(2,1)}, u32[]{:S(2)}) copy-start(bf16[1280,1536]{1,0:T(8,128)(2,1)} %copy-done.55) | copy-start | bytes 11796484
  166.6 12.3 %collective-permute-start.11 = (bf16[640,768]{1,0:T(8,128)(2,1)S(1)}, bf16[640,768]{1,0:T(8,128)(2,1)S(1)}, u32[]{:S(2)}, u32[]{:S(2)}) collective-permute-start(bf16[640,768]{1,0:T(8,128)(2,1)S(1)} %dynamic-slice_convert_fusion), channel_id=1, source_target_pairs={{0,1},{1,0},{2,3},{3,2},{4,5},{5,4},{6,7},{7,6},{8,9},{9,8},{10,11... | collective-permute-start | bytes 2949128 | tf_op jit(solution)/shard_map/ppermute | solution.py:681
  175.3 3.6 copy-start.34
  175.3 3.6 copy-start.36
  175.3 3.6 copy-start.46
  184.4 2.8 collective-permute-start.12
  (38 other events, 80.6 us)

commit v3 on v0

v3 whole, which is shorter than its diff:
```python
import functools
import math
import types

import jax
import jax.numpy as jnp
from jax import lax
from jax.experimental import pallas as pl
from jax.experimental.pallas import tpu as pltpu
from jax.sharding import PartitionSpec as P

HD = 64
LEN = 512
HALF = LEN // 2
EPSILON = 1e-12
NEGATIVE = -1000000000.0
SCALE = 1.0 / math.sqrt(HD)
LOG2E = math.log2(math.e)
F32 = jnp.float32
BF16 = jnp.bfloat16
NN = (((1,), (0,)), ((), ()))
NT = (((1,), (1,)), ((), ()))
TN = (((0,), (0,)), ((), ()))
MESH = pl.DeviceIdType.MESH
PARTS = 4
OWNERS = 8
PAIRS = 3
PIECES = 18


def dg(left, right, dims=NN):
    return lax.dot_general(left, right, dims, preferred_element_type=F32)


def normalize(value):
    average = jnp.mean(value, axis=-1, keepdims=True)
    centered = value - average
    variance = jnp.mean(centered * centered, axis=-1, keepdims=True)
    inverse = lax.rsqrt(variance + EPSILON)
    return centered * inverse, inverse


def norm_backward(grad, unit, inverse, gain):
    scaled = grad * gain
    first_mean = jnp.mean(scaled, axis=-1, keepdims=True)
    second_mean = jnp.mean(scaled * unit, axis=-1, keepdims=True)
    return inverse * (scaled - first_mean - unit * second_mean)


def gelu_and_slope(inner):
    cumulative = 0.5 * (1.0 + lax.erf(inner * (1.0 / math.sqrt(2.0))))
    slope = cumulative + inner * jnp.exp(-0.5 * inner * inner) * (1.0 / math.sqrt(2.0 * math.pi))
    return inner * cumulative, slope


def column_sum(value):
    return jnp.sum(value, axis=0, keepdims=True)


def attend_front(q, k, v, bias):
    logits = dg(k, q, NT) * (SCALE * LOG2E) + bias
    peak = jnp.max(logits, axis=0, keepdims=True)
    powers = jnp.exp2(logits - peak)
    total = jnp.sum(powers, axis=0, keepdims=True)
    weights = (powers * (1.0 / total)).astype(BF16)
    return dg(weights, v, TN).astype(BF16), peak + jnp.log2(total)


def attend_back(q, k, v, g, bias, row):
    logits = dg(k, q, NT) * (SCALE * LOG2E) + bias
    probs = jnp.exp2(logits - row)
    dprobs = dg(v, g, NT)
    across = jnp.sum(probs * dprobs, axis=0, keepdims=True)
    dscores = (probs * (dprobs - across) * SCALE).astype(BF16)
    dv = dg(probs.astype(BF16), g, NN).astype(BF16)
    dk = dg(dscores, q, NN).astype(BF16)
    dq = dg(dscores, k, TN).astype(BF16)
    return dq, dk, dv


def pair_back(q, k, v, g, bias, rows):
    done = []
    for h in range(2):
        cols = slice(h * HD, (h + 1) * HD)
        done.append(attend_back(q[:, cols], k[:, cols], v[:, cols], g[:, cols], bias, rows[h]))
    return [jnp.concatenate([done[0][i], done[1][i]], axis=1) for i in range(3)]


def swap_halves(value):
    return jnp.concatenate([value[:, HD:], value[:, :HD]], axis=1)


def pair_lanes(j):
    return pl.ds(pl.multiple_of(j * 2 * HD, 2 * HD), 2 * HD)


def remote(source, target, out, into, device):
    return pltpu.make_async_remote_copy(
        src_ref=source, dst_ref=target, send_sem=out, recv_sem=into, device_id=device, device_id_type=MESH
    )


class Rounds:
    def __init__(self, r, groups):
        self.r = r
        self.place = lax.axis_index("tensor")
        group = lax.axis_index("dp")
        self.x, self.z, self.far = group % 2, (group // 2) % 4, group // OWNERS
        self.more = groups // OWNERS
        self.sent = []

    def dp_at(self, x, z):
        return {"dp": self.far * OWNERS + z * 2 + x}

    def start(self, copy):
        copy.start()
        self.sent.append(copy)
        return copy

    def settle(self, copy):
        copy.wait_send()
        self.sent = [other for other in self.sent if other is not copy]

    def y_copy(self, u):
        r = self.r
        side = {"tensor": (self.place + 2) % 4}
        return remote(r.grads_other.at[u], r.from_side.at[u], r.y_out.at[u], r.y_in.at[u], side)

    def x_copy(self, u):
        r = self.r
        away = r.grads_own.at[u, pl.ds((1 - self.x) * 4, 4)]
        return remote(away, r.from_x.at[u], r.x_out.at[u], r.x_in.at[u], self.dp_at(1 - self.x, self.z))

    def z_copy(self, u, step):
        r = self.r
        there = (self.z + step) % 4
        away = r.grads_own.at[u, self.x * 4 + there]
        out, into = r.z_out.at[u, step - 1], r.z_in.at[u, step - 1]
        return remote(away, r.from_z.at[u, step - 1], out, into, self.dp_at(self.x, there))

    def f_copy(self, u, step):
        r = self.r
        peer = {"dp": ((self.far + step) % self.more) * OWNERS + self.z * 2 + self.x}
        own = r.grads_own.at[u, self.x * 4 + self.z]
        return remote(own, r.from_far.at[u, step - 1], r.f_out.at[u, step - 1], r.f_in.at[u, step - 1], peer)

    def g_copy(self, u, step, origin):
        r = self.r
        piece = r.total.at[u, self.x * 4 + origin]
        out, into = r.g_out.at[u, step - 1], r.g_in.at[u, step - 1]
        return remote(piece, piece, out, into, self.dp_at(self.x, (self.z + step) % 4))

    def h_copy(self, u, half):
        r = self.r
        piece = r.total.at[u, pl.ds(half * 4, 4)]
        return remote(piece, piece, r.h_out.at[u], r.h_in.at[u], self.dp_at(1 - self.x, self.z))

    def y_start(self, u):
        self.y_copy(u).start()

    def x_start(self, u):
        r = self.r
        self.y_copy(u).wait_recv()
        r.grads_own[u] = (r.grads_own[u].astype(F32) + r.from_side[u].astype(F32)).astype(BF16)
        self.x_copy(u).start()

    def z_start(self, u):
        r = self.r
        self.x_copy(u).wait_recv()
        kept = pl.ds(self.x * 4, 4)
        r.grads_own[u, kept] = (r.grads_own[u, kept].astype(F32) + r.from_x[u].astype(F32)).astype(BF16)
        for step in (1, 2, 3):
            self.z_copy(u, step).start()

    def g_start(self, u):
        r = self.r
        own = self.x * 4 + self.z
        value = r.grads_own[u, own].astype(F32)
        for step in (1, 2, 3):
            self.z_copy(u, step).wait_recv()
            value = value + r.from_z[u, step - 1].astype(F32)
        if self.more > 1:
            r.grads_own[u, own] = value.astype(BF16)
            for step in range(1, self.more):
                self.f_copy(u, step).start()
            for step in range(1, self.more):
                self.f_copy(u, step).wait_recv()
                value = value + r.from_far[u, step - 1].astype(F32)
        r.total[u, own] = value.astype(BF16)
        for step in (1, 2, 3):
            self.g_copy(u, step, self.z).start()

    def h_start(self, u):
        for step in (1, 2, 3):
            self.g_copy(u, step, (self.z - step + 4) % 4).wait_recv()
        self.h_copy(u, self.x).start()

    def advance(self, n):
        stages = (self.h_start, self.g_start, self.z_start, self.x_start)
        for behind, stage in zip((3, 2, 1, 0), stages):
            if not isinstance(n, int) or 0 <= n - behind < PIECES:
                stage(n - behind)

    def finish(self):
        def settle(u, _):
            self.h_copy(u, 1 - self.x).wait_recv()
            for copy in (self.y_copy(u), self.x_copy(u), self.h_copy(u, self.x)):
                copy.wait_send()
            for step in (1, 2, 3):
                self.z_copy(u, step).wait_send()
                self.g_copy(u, step, self.z).wait_send()
            for step in range(1, self.more):
                self.f_copy(u, step).wait_send()
            return 0

        lax.fori_loop(0, PIECES, settle, 0)
        for copy in self.sent:
            copy.wait_send()


def layer_kernel(groups, names, *refs):
    r = types.SimpleNamespace(**dict(zip(names, refs)))
    place = lax.axis_index("tensor")
    group = lax.axis_index("dp")
    core, side = place % 2, place // 2
    rows = r.q.shape[0]
    own_rows = rows // 2
    wide = r.x_rows.shape[1]
    both = r.q.shape[1]
    width = both // 2
    units = r.w_inner.shape[1]
    chunk = own_rows // 2
    strip = own_rows // 8
    mine = core * own_rows
    theirs = (1 - core) * own_rows
    c_start = pl.multiple_of((1 - side) * 2 * LEN, HALF)
    core_peer = {"tensor": place + 1 - 2 * core}
    side_peer = {"tensor": (place + 2) % 4}

    barrier = pltpu.get_barrier_semaphore()
    for step in (1, 2, 3):
        pl.semaphore_signal(barrier, inc=1, device_id={"tensor": (place + step) % 4}, device_id_type=MESH)

    def greet(step, _):
        peer = (group + step) % groups
        pl.semaphore_signal(barrier, inc=1, device_id={"dp": peer}, device_id_type=MESH)
        return 0

    lax.fori_loop(1, groups, greet, 0)

    def at_rows(start, count):
        return pl.ds(pl.multiple_of(start, 16), count)

    own_at = at_rows(mine, own_rows)
    loads = {}
    sources = [
        ("tokens", r.tokens, r.x_rows.at[own_at]),
        ("q", r.w_query, r.w_att.at[0, :, 0]),
        ("k", r.w_key, r.w_att.at[1, :, 0]),
        ("v", r.w_value, r.w_att.at[2, :, 0]),
        ("o", r.w_output, r.w_att.at[3, :, 0]),
        ("in", r.w_inner, r.in_own),
        ("down", r.w_outer, r.down_own),
        ("cotangent", r.cotangent, r.grad_tokens),
    ]
    for n, (name, source, target) in enumerate(sources):
        loads[name] = pltpu.make_async_copy(source, target, r.l_sem.at[n])
        loads[name].start()

    pl.semaphore_wait(barrier, 3 + groups - 1)
    rounds = Rounds(r, groups)
    x, z = rounds.x, rounds.z
    x_peer = rounds.dp_at(1 - x, z)

    lanes = wide // 2
    block = units // 8

    def by_heads(source, i):
        def view(ref, half):
            return ref.at[:, :, pl.ds(half * lanes, lanes)]

        return source, r.w_att.at[i, :, 1], view

    def by_rows(source, target, n):
        def view(ref, half):
            return ref.at[at_rows(half * 4 * block + n * 2 * block, 2 * block)]

        return source, target, view

    fetches = [by_heads(w, i) for i, w in enumerate((r.w_query, r.w_key, r.w_value, r.w_output))]
    fetches += [by_rows(r.w_inner, r.in_other, n) for n in range(2)]
    fetches += [by_rows(r.w_outer, r.down_other, n) for n in range(2)]

    def fetch_copy(n):
        source, target, view = fetches[n]
        return remote(view(source, x), view(target, x), r.w_out_sem.at[n], r.w_in_sem.at[n], side_peer)

    def pass_copy(n, which):
        _, target, view = fetches[n]
        return remote(view(target, which), view(target, which), r.p_out_sem.at[n], r.p_in_sem.at[n], x_peer)

    def fetch(*which):
        for n in which:
            rounds.start(fetch_copy(n))

    def hand_on(*which):
        for n in which:
            fetch_copy(n).wait_recv()
            rounds.start(pass_copy(n, x))

    def fetched(*which):
        for n in which:
            pass_copy(n, 1 - x).wait_recv()

    token_copy = rounds.start(remote(r.tokens, r.x_rows.at[own_at], r.s_out.at[0], r.s_in.at[0], core_peer))
    token_wait = remote(r.tokens, r.x_rows.at[at_rows(theirs, own_rows)], r.s_out.at[0], r.s_in.at[0], core_peer)
    fetch(0, 1, 2)
    vector_copy = rounds.start(remote(r.biases, r.biases_other, r.s_out.at[1], r.s_in.at[1], side_peer))

    def project(shard, which, start, count, size):
        shifts = (r.biases, r.biases_other)[shard]
        for i in which:
            target = (r.q, r.k, r.v)[i]
            weights = r.w_att[i, :, shard].reshape(width, wide)

            def body(n, _):
                block = at_rows(start + n * size, size)
                value = dg(r.x_rows[block, :], weights, NT)
                if i == 0:
                    value = value + shifts[0:1, 0:width]
                if i == 2:
                    value = value + shifts[1:2, 0:width]
                value = value.astype(BF16)
                for j in range(PAIRS):
                    lane = (2 * j + shard) * HD
                    target[block, lane : lane + HD] = value[:, j * HD : (j + 1) * HD]
                return 0

            lax.fori_loop(0, count // size, body, 0)

    loads["tokens"].wait()
    for name in ("q", "k", "v"):
        loads[name].wait()
    project(0, (0, 1, 2), mine, own_rows, chunk)

    token_wait.wait_recv()
    quarter = HALF // 2
    far_at = at_rows(rows + core * quarter, quarter)
    far_there = at_rows(rows + (1 - core) * quarter, quarter)
    near_at = at_rows(c_start + core * quarter, quarter)
    far_copy = rounds.start(
        remote(r.x_rows.at[near_at], r.x_rows.at[far_at], r.s_out.at[2], r.s_in.at[2], side_peer)
    )
    fetch(3, 4, 5, 6, 7)
    project(0, (0, 1, 2), theirs, own_rows, chunk)
    hand_on(0)

    def mask_block(at, row, places, length, count):
        column = jnp.transpose(jnp.broadcast_to(row.astype(F32), (128, LEN)))[:, 0:1]
        same = column == row.astype(F32)[:, :count]
        live = places < length
        first = lax.broadcasted_iota(jnp.int32, (LEN, count), 0)
        second = lax.broadcasted_iota(jnp.int32, (LEN, count), 1)
        allowed = same & live | (first == second)
        r.bias[:, at : at + count] = jnp.where(allowed, 0.0, NEGATIVE)

    ahead = lax.broadcasted_iota(jnp.int32, (LEN, 1), 0)
    for which in range(2):
        index = 3 * side + which
        mask_block(which * LEN, r.segments[pl.ds(index, 1), :], ahead, r.lengths[index], LEN)
    near = r.segments[2:3, pl.ds(pl.multiple_of(side * HALF, HALF), HALF)]
    away_row = r.segments[2:3, pl.ds(pl.multiple_of((1 - side) * HALF, HALF), HALF)]
    turned = jnp.where(ahead < HALF, ahead + side * HALF, ahead - side * HALF)
    mask_block(2 * LEN, jnp.concatenate([near, away_row], axis=1), turned, r.lengths[2], HALF)
    hand_on(1)

    def front_store(shard, block, lanes, out):
        if shard == 0:
            r.ctx[block, lanes] = jnp.concatenate([out, jnp.zeros_like(out)], axis=1)
        else:
            r.ctx[block, lanes] = jnp.concatenate([r.ctx[block, lanes][:, :HD], out], axis=1)

    def front_whole(shard, first_pair, last_pair):
        cols = slice(shard * HD, (shard + 1) * HD)

        def body(n, _):
            j, i = n // 2, n % 2
            lanes = pair_lanes(j)
            block = at_rows(side * HALF + i * LEN, LEN)
            at = pl.ds(pl.multiple_of(i * LEN, LEN), LEN)
            out, row = attend_front(
                r.q[block, lanes][:, cols], r.k[block, lanes][:, cols], r.v[block, lanes][:, cols], r.bias[:, at]
            )
            front_store(shard, block, lanes, out)
            r.lse[pl.ds(2 * j + shard, 1), at] = row
            return 0

        lax.fori_loop(2 * first_pair, 2 * last_pair, body, 0)

    def front_half(shard):
        cols = slice(shard * HD, (shard + 1) * HD)

        def body(j, _):
            lanes = pair_lanes(j)
            block = pl.ds(c_start, HALF)
            at = pl.ds(2 * LEN, HALF)
            out, row = attend_front(
                r.q[block, lanes][:, cols], r.kc[:, lanes][:, cols], r.vc[:, lanes][:, cols], r.bias[:, at]
            )
            front_store(shard, block, lanes, out)
            r.lse[pl.ds(2 * j + shard, 1), at] = row
            return 0

        lax.fori_loop(0, PAIRS, body, 0)

    front_whole(0, 0, 1)
    hand_on(2)
    front_whole(0, 1, 3)
    far_copy.wait_recv()
    far_pass = rounds.start(
        remote(r.x_rows.at[far_at], r.x_rows.at[far_at], r.s_out.at[3], r.s_in.at[3], core_peer)
    )
    far_wait = remote(r.x_rows.at[far_there], r.x_rows.at[far_there], r.s_out.at[3], r.s_in.at[3], core_peer)
    vector_copy.wait_recv()
    fetched(0)
    project(1, (0,), 0, rows, chunk)
    fetched(1)
    project(1, (1,), 0, rows, chunk)
    hand_on(3)
    fetched(2)
    project(1, (2,), 0, rows, chunk)
    far_wait.wait_recv()
    for shard in range(2):
        project(shard, (1, 2), rows, HALF, HALF)
    for own, near_far in ((r.k, r.kc), (r.v, r.vc)):
        near_far[pl.ds(0, HALF), :] = own[pl.ds(c_start, HALF), :]
        near_far[pl.ds(HALF, HALF), :] = own[pl.ds(rows, HALF), :]
    front_whole(1, 0, 3)
    front_half(0)
    front_half(1)
    hand_on(4)

    loads["o"].wait()
    fetched(3)

    def pairs_of(i):
        return r.w_att[i].reshape(both, wide)

    def each(start, count, size, body):
        def step(n, _):
            body(at_rows(start + n * size, size), at_rows(n * size, size))
            return 0

        lax.fori_loop(0, count // size, step, 0)

    trades = []

    def trade_rows(compute, keep):
        def away_body(block, local):
            r.partial[local, :] = compute(block).astype(BF16)

        each(theirs, own_rows, chunk, away_body)
        n = len(trades)
        trades.append(
            rounds.start(remote(r.partial, r.partial_in, r.t_out.at[n], r.t_in.at[n], core_peer))
        )

        def own_body(block, local):
            keep(local, compute(block))

        each(mine, own_rows, chunk, own_body)
        trades[n].wait_recv()
        rounds.settle(trades[n])

    def gather_rows(ref, n):
        copy = rounds.start(remote(ref.at[own_at], ref.at[own_at], r.a_out.at[n], r.a_in.at[n], core_peer))
        there = ref.at[at_rows(theirs, own_rows)]
        return copy, remote(there, there, r.a_out.at[n], r.a_in.at[n], core_peer)

    def keep_acc(local, value):
        r.acc[local, :] = value

    trade_rows(lambda block: dg(r.ctx[block, :], pairs_of(3)), keep_acc)
    b_output, first_gain, first_shift = (r.vectors[i : i + 1, :] for i in range(3))
    b_outer, second_gain, second_shift = (r.vectors[i : i + 1, :] for i in range(3, 6))

    def first_norm(block, local):
        value = r.x_rows[block, :].astype(F32) + r.acc[local, :] + r.partial_in[local, :].astype(F32) + b_output
        unit, inverse = normalize(value)
        r.acc[local, :] = unit
        r.inverse[local, :] = inverse
        r.first[block, :] = (unit * first_gain + first_shift).astype(BF16)

    each(mine, own_rows, strip, first_norm)
    first_copy, first_wait = gather_rows(r.first, 0)
    hand_on(5)

    def expand(shard, start):
        weights = (r.in_own, r.in_other)[shard]
        shifts = (r.biases, r.biases_other)[shard]
        hidden, slope = ((r.hidden_own, r.slope_own), (r.hidden_other, r.slope_other))[shard]

        def body(block, _):
            value, gradient = gelu_and_slope(dg(r.first[block, :], weights[...]) + shifts[2:3, :])
            hidden[block, :] = value.astype(BF16)
            slope[block, :] = gradient.astype(BF16)

        each(start, own_rows, chunk, body)

    loads["in"].wait()
    expand(0, mine)
    first_wait.wait_recv()
    expand(0, theirs)
    hand_on(6)
    fetched(4, 5)
    expand(1, theirs)
    expand(1, mine)
    loads["down"].wait()
    hand_on(7)
    fetched(6, 7)

    def keep_second(local, value):
        r.second[local, :] = value

    trade_rows(
        lambda block: dg(r.hidden_own[block, :], r.down_own[...]) + dg(r.hidden_other[block, :], r.down_other[...]),
        keep_second,
    )
    loads["cotangent"].wait()
    zero = jnp.zeros((1, wide), F32)

    def second_norm(n, carry):
        block, local = at_rows(mine + n * strip, strip), at_rows(n * strip, strip)
        value = r.first[block, :].astype(F32) + r.second[local, :] + r.partial_in[local, :].astype(F32) + b_outer
        unit, inverse = normalize(value)
        r.output[local, :] = (unit * second_gain + second_shift).astype(BF16)
        upstream = r.grad_tokens[local, :].astype(F32)
        grad = norm_backward(upstream, unit, inverse, second_gain)
        r.second[local, :] = grad
        low = grad.astype(BF16)
        r.feed[block, :] = low
        gain, shift, lows = carry
        return gain + column_sum(upstream * unit), shift + column_sum(upstream), lows + column_sum(low.astype(F32))

    sum_second_gain, sum_second_shift, sum_b_outer = lax.fori_loop(
        0, own_rows // strip, second_norm, (zero, zero, zero)
    )
    feed_copy, feed_wait = gather_rows(r.feed, 1)

    def contract(shard, start, carry):
        weights = (r.down_own, r.down_other)[shard]
        slope = (r.slope_own, r.slope_other)[shard]

        def body(n, total):
            block = at_rows(start + n * chunk, chunk)
            value = dg(r.feed[block, :], weights[...], NT) * slope[block, :].astype(F32)
            low = value.astype(BF16)
            slope[block, :] = low
            return total + column_sum(low.astype(F32))

        return lax.fori_loop(0, own_rows // chunk, body, carry)

    sum_own = contract(0, mine, jnp.zeros((1, units), F32))
    sum_other = contract(1, mine, jnp.zeros((1, units), F32))
    feed_wait.wait_recv()

    def weight_blocks(target, first_piece, left, right, send):
        columns = left.shape[1] // 3

        def body(u, _):
            value = dg(left[:, pl.ds(pl.multiple_of(u * columns, 128), columns)], right[...], TN).astype(BF16)
            at = first_piece + 2 * u
            target[pl.ds(at, 2)] = value.reshape(2, OWNERS, columns // (2 * OWNERS), value.shape[1])
            if send:
                rounds.y_start(at)
                rounds.y_start(at + 1)
            return 0

        lax.fori_loop(0, 3, body, 0)

    weight_blocks(r.grads_other, 0, r.hidden_other, r.feed, True)
    weight_blocks(r.grads_own, 0, r.hidden_own, r.feed, False)
    sum_own = contract(0, theirs, sum_own)
    sum_other = contract(1, theirs, sum_other)
    rounds.advance(0)

    def keep_first(local, value):
        r.second[local, :] = r.second[local, :] + value

    trade_rows(
        lambda block: dg(r.slope_own[block, :], r.in_own[...], NT) + dg(r.slope_other[block, :], r.in_other[...], NT),
        keep_first,
    )
    rounds.settle(feed_copy)

    def first_back(n, carry):
        block, local = at_rows(mine + n * strip, strip), at_rows(n * strip, strip)
        grad_first = r.second[local, :] + r.partial_in[local, :].astype(F32)
        unit = r.acc[local, :]
        grad = norm_backward(grad_first, unit, r.inverse[local, :], first_gain)
        r.second[local, :] = grad
        low = grad.astype(BF16)
        r.feed[block, :] = low
        gain, shift, lows = carry
        return gain + column_sum(grad_first * unit), shift + column_sum(grad_first), lows + column_sum(low.astype(F32))

    sum_first_gain, sum_first_shift, sum_b_output = lax.fori_loop(0, own_rows // strip, first_back, (zero, zero, zero))
    branch_copy, branch_wait = gather_rows(r.feed, 2)
    weight_blocks(r.grads_other, 6, r.first, r.slope_other, True)
    rounds.advance(1)
    weight_blocks(r.grads_own, 6, r.first, r.slope_own, False)
    rounds.advance(2)
    branch_wait.wait_recv()

    dq = r.hidden_own.at[:, pl.ds(0, both)]
    dk = r.hidden_own.at[:, pl.ds(both, both)]
    dv = r.hidden_other.at[:, pl.ds(0, both)]
    gc = r.hidden_other.at[:, pl.ds(both, both)]

    def context_back(block, _):
        gc[block, :] = dg(r.feed[block, :], pairs_of(3), NT).astype(BF16)

    each(0, rows, chunk, context_back)

    def back_half(j, _):
        lanes = pair_lanes(j)
        at = pl.ds(2 * LEN, HALF)
        stats = [r.lse[pl.ds(j * 2 + h, 1), at] for h in range(2)]
        block = pl.ds(c_start, HALF)
        d_q, d_k, d_v = pair_back(
            r.q[block, lanes], r.kc[:, lanes], r.vc[:, lanes], gc[block, lanes], r.bias[:, at], stats
        )
        dq[block, lanes] = d_q
        dk[block, lanes] = d_k[:HALF]
        dv[block, lanes] = d_v[:HALF]
        r.away[0, :, lanes] = d_k[HALF:]
        r.away[1, :, lanes] = d_v[HALF:]
        return 0

    lax.fori_loop(0, PAIRS, back_half, 0)
    rounds.advance(3)

    grad_out = dg(r.ctx[...], r.feed[...], TN).astype(BF16)
    for j in range(PAIRS):
        for shard, target in ((0, r.grads_own), (1, r.grads_other)):
            lane = (2 * j + shard) * HD
            target[12 + 2 * j + 1, 4:] = grad_out[lane : lane + HD].reshape(4, HD // 4, wide)

    def back_whole(j):
        def body(i, _):
            lanes = pair_lanes(j)
            block = at_rows(side * HALF + i * LEN, LEN)
            at = pl.ds(pl.multiple_of(i * LEN, LEN), LEN)
            stats = [r.lse[pl.ds(j * 2 + h, 1), at] for h in range(2)]
            d_q, d_k, d_v = pair_back(
                r.q[block, lanes], r.k[block, lanes], r.v[block, lanes], gc[block, lanes], r.bias[:, at], stats
            )
            dq[block, lanes] = d_q
            dk[block, lanes] = d_k
            dv[block, lanes] = d_v
            return 0

        lax.fori_loop(0, 2, body, 0)

    def weight_pair(j):
        lanes = pair_lanes(j)
        left = jnp.concatenate([dq[:, lanes], dk[:, lanes], dv[:, lanes]], axis=1)
        value = dg(left, r.x_rows[pl.ds(0, rows), :], TN)
        far_left = jnp.concatenate([r.away[0, :, lanes], r.away[1, :, lanes]], axis=1)
        far = dg(far_left, r.x_rows[pl.ds(rows, HALF), :], TN)
        first = value[: 2 * HD].astype(BF16)
        rest = (value[2 * HD :] + far).astype(BF16)
        at = 12 + 2 * j
        for shard, target in ((0, r.grads_own), (1, r.grads_other)):
            cut = slice(shard * HD, (shard + 1) * HD)
            pieces = [v[cut].reshape(4, HD // 4, wide) for v in (first, rest[: 2 * HD], rest[2 * HD :])]
            target[at, 0:4] = pieces[0]
            target[at, 4:8] = pieces[1]
            target[at + 1, 0:4] = pieces[2]
        rounds.y_start(at)
        rounds.y_start(at + 1)

    def back_pair(j, _):
        back_whole(j)
        weight_pair(j)
        rounds.advance(4 + j)
        return 0

    lax.fori_loop(0, PAIRS, back_pair, 0)

    def bias_sum(*grads):
        total = sum(column_sum(part) for part in grads)
        heads = [total[:, i * HD : (i + 1) * HD] for i in range(2 * PAIRS)]
        return jnp.concatenate(heads[0::2], axis=1), jnp.concatenate(heads[1::2], axis=1)

    sums = (sum_b_output, sum_first_gain, sum_first_shift, sum_b_outer, sum_second_gain, sum_second_shift)
    for t in range(PARTS):
        shares = [value[:, t * width : (t + 1) * width] for value in sums]
        r.tiny[t, 0:1, :] = jnp.concatenate(shares[:4], axis=1)
        r.tiny[t, 1:2, :] = jnp.concatenate(shares[4:] + [jnp.zeros((1, 2 * width), F32)], axis=1)
        r.tiny[t, 2:3, :] = jnp.zeros((1, units), F32)
    queries, values = bias_sum(dq[...].astype(F32)), bias_sum(dv[...].astype(F32), r.away[1].astype(F32))
    for target, n, inner in ((place, 0, sum_own), ((place + 2) % 4, 1, sum_other)):
        r.tiny[target, 1:2, 2 * width :] = jnp.concatenate([queries[n], values[n]], axis=1)
        r.tiny[target, 2:3, :] = inner
    tiny_copies = []
    for step in (1, 2, 3):
        peer = (place + step) % 4
        out, into = r.i_out.at[step - 1], r.i_in.at[step - 1]
        tiny_copies.append(rounds.start(remote(r.tiny.at[peer], r.tiny_side.at[step - 1], out, into, {"tensor": peer})))

    def input_rows(block):
        value = dg(dq[block, :], pairs_of(0))
        value = value + dg(dk[block, :], pairs_of(1))
        return value + dg(dv[block, :], pairs_of(2))

    r.far_part[...] = (dg(r.away[0], pairs_of(1)) + dg(r.away[1], pairs_of(2))).astype(BF16)
    give = at_rows((1 - core) * quarter, quarter)
    keep = at_rows(core * quarter, quarter)
    far_trade = rounds.start(
        remote(r.far_part.at[give], r.far_half, r.s_out.at[4], r.s_in.at[4], core_peer)
    )
    far_trade.wait_recv()
    r.far_send[...] = (r.far_part[keep, :].astype(F32) + r.far_half[...].astype(F32)).astype(BF16)
    owner = {"tensor": (1 - side) * 2 + side}
    rounds.start(remote(r.far_send, r.far_in.at[core], r.o_out, r.o_in.at[core], owner))

    trade_rows(input_rows, keep_first)

    for n in (7, 8, 9, 10):
        rounds.advance(n)

    @pl.when(core == 1 - side)
    def _():
        start = (1 - side) * (own_rows - HALF)
        for n in range(2):
            remote(r.far_send, r.far_in.at[n], r.o_out, r.o_in.at[n], owner).wait_recv()
            block = at_rows(start + n * quarter, quarter)
            r.second[block, :] = r.second[block, :] + r.far_in[n].astype(F32)

    def finish(block, local):
        r.grad_tokens[local, :] = (r.second[local, :] + r.partial_in[local, :].astype(F32)).astype(BF16)

    each(mine, own_rows, strip, finish)

    total = r.tiny[place]
    for step in (1, 2, 3):
        tiny_copies[step - 1].wait_recv()
        total = total + r.tiny_side[step - 1]
    r.tiny_all[0] = total

    def tell(step, _):
        peer = {"dp": (group + step) % groups}
        remote(r.tiny_all.at[0], r.tiny_all.at[step], r.d_out.at[step], r.d_in.at[step], peer).start()
        return 0

    lax.fori_loop(1, groups, tell, 0)
    def hear(step, total):
        peer = {"dp": (group + step) % groups}
        copy = remote(r.tiny_all.at[0], r.tiny_all.at[step], r.d_out.at[step], r.d_in.at[step], peer)
        copy.wait()
        return total + r.tiny_all[step]

    r.small[...] = lax.fori_loop(1, groups, hear, r.tiny_all[0])

    def pump(n, _):
        rounds.advance(n)
        return 0

    lax.fori_loop(11, PIECES, pump, 0)
    for n in range(PIECES, PIECES + 3):
        rounds.advance(n)
    rounds.finish()


def layer(groups, named):
    dma = pltpu.SemaphoreType.DMA
    own_rows, wide = named["tokens"].shape
    units = named["w_inner"].shape[1]
    heads = named["w_query"].shape
    rows, both = 2 * own_rows, 2 * heads[0] * heads[1]
    more = groups // OWNERS
    share = wide // 6 // OWNERS
    outs = {
        "output": ((own_rows, wide), BF16),
        "grad_tokens": ((own_rows, wide), BF16),
        "total": ((PIECES, OWNERS, share, wide), BF16),
        "small": ((3, wide), F32),
    }
    room = {
        "x_rows": ((rows + HALF, wide), BF16),
        "w_att": ((4, PAIRS, 2, HD, wide), BF16),
        "in_own": ((wide, units), BF16),
        "in_other": ((wide, units), BF16),
        "down_own": ((units, wide), BF16),
        "down_other": ((units, wide), BF16),
        "biases_other": ((8, wide), F32),
        "bias": ((LEN, rows), F32),
        "q": ((rows, both), BF16),
        "k": ((rows + HALF, both), BF16),
        "v": ((rows + HALF, both), BF16),
        "kc": ((LEN, both), BF16),
        "vc": ((LEN, both), BF16),
        "ctx": ((rows, both), BF16),
        "lse": ((8, rows), F32),
        "partial": ((own_rows, wide), BF16),
        "partial_in": ((own_rows, wide), BF16),
        "acc": ((own_rows, wide), F32),
        "inverse": ((own_rows, 1), F32),
        "first": ((rows, wide), BF16),
        "hidden_own": ((rows, units), BF16),
        "hidden_other": ((rows, units), BF16),
        "slope_own": ((rows, units), BF16),
        "slope_other": ((rows, units), BF16),
        "second": ((own_rows, wide), F32),
        "feed": ((rows, wide), BF16),
        "away": ((2, HALF, both), BF16),
        "far_part": ((HALF, wide), BF16),
        "far_half": ((HALF // 2, wide), BF16),
        "far_send": ((HALF // 2, wide), BF16),
        "far_in": ((2, HALF // 2, wide), BF16),
        "grads_own": ((PIECES, OWNERS, share, wide), BF16),
        "grads_other": ((PIECES, OWNERS, share, wide), BF16),
        "from_side": ((PIECES, OWNERS, share, wide), BF16),
        "from_x": ((PIECES, 4, share, wide), BF16),
        "from_z": ((PIECES, 3, share, wide), BF16),
        "from_far": ((PIECES, more - 1, share, wide) if more > 1 else (1, 1, 16, 128), BF16),
        "tiny": ((PARTS, 3, wide), F32),
        "tiny_side": ((3, 3, wide), F32),
        "tiny_all": ((groups, 3, wide), F32),
    }
    sems = {
        "l_sem": (8,),
        "s_out": (5,),
        "s_in": (5,),
        "w_out_sem": (8,),
        "w_in_sem": (8,),
        "p_out_sem": (8,),
        "p_in_sem": (8,),
        "t_out": (4,),
        "t_in": (4,),
        "a_out": (3,),
        "a_in": (3,),
        "y_out": (PIECES,),
        "y_in": (PIECES,),
        "x_out": (PIECES,),
        "x_in": (PIECES,),
        "z_out": (PIECES, 3),
        "z_in": (PIECES, 3),
        "g_out": (PIECES, 3),
        "g_in": (PIECES, 3),
        "h_out": (PIECES,),
        "h_in": (PIECES,),
        "f_out": (PIECES, max(more - 1, 1)),
        "f_in": (PIECES, max(more - 1, 1)),
        "i_out": (3,),
        "i_in": (3,),
        "d_out": (groups,),
        "d_in": (groups,),
        "o_out": (),
        "o_in": (2,),
    }
    names = list(named) + list(outs) + list(room) + list(sems)
    in_vmem = pl.BlockSpec(memory_space=pltpu.VMEM)
    spaces = {"lengths": pltpu.SMEM, "vectors": pltpu.VMEM, "biases": pltpu.VMEM, "segments": pltpu.VMEM}
    results = pl.pallas_call(
        functools.partial(layer_kernel, groups, names),
        out_shape=[jax.ShapeDtypeStruct(*spec) for spec in outs.values()],
        in_specs=[pl.BlockSpec(memory_space=spaces.get(name, pl.ANY)) for name in named],
        out_specs=[in_vmem] * len(outs),
        scratch_shapes=[pltpu.VMEM(*spec) for spec in room.values()] + [dma(shape) for shape in sems.values()],
        compiler_params=pltpu.CompilerParams(
            collective_id=0, has_side_effects=True, vmem_limit_bytes=67043328
        ),
    )(*named.values())
    return dict(zip(outs, results))


def shards(
    tokens,
    segment_ids,
    lengths,
    w_query,
    b_query,
    w_key,
    w_value,
    b_value,
    w_output,
    b_output,
    first_gain,
    first_shift,
    w_inner,
    b_inner,
    w_outer,
    b_outer,
    second_gain,
    second_shift,
    cotangent,
):
    groups = lax.axis_size("dp")
    wide, width = w_query.shape
    units = w_inner.shape[1]
    by_head = (width // HD, HD, wide)
    spare = jnp.zeros((wide - width,), F32)
    rest = jnp.zeros((wide,), F32)
    vectors = jnp.stack([b_output, first_gain, first_shift, b_outer, second_gain, second_shift, rest, rest])
    biases = jnp.stack(
        [jnp.concatenate([b_query, spare]), jnp.concatenate([b_value, spare]), b_inner, rest, rest, rest, rest, rest]
    )
    done = layer(
        groups,
        {
            "tokens": tokens,
            "w_query": w_query.T.reshape(by_head),
            "w_key": w_key.T.reshape(by_head),
            "w_value": w_value.T.reshape(by_head),
            "w_output": w_output.reshape(by_head),
            "w_inner": w_inner,
            "w_outer": w_outer,
            "cotangent": cotangent,
            "vectors": vectors,
            "biases": biases,
            "segments": segment_ids.reshape(-1, LEN),
            "lengths": lengths,
        },
    )
    sums = done["total"]
    attention = sums[12:].reshape(PAIRS, 4, HD, wide)
    query, key, value, out = (attention[:, i].reshape(width, wide).astype(F32) for i in range(4))
    total = done["small"].reshape(-1)
    shares = total[: 6 * width].reshape(6, width)
    rest = total[6 * width :]
    return (
        done["output"],
        done["grad_tokens"],
        query.T,
        rest[:width],
        key.T,
        value.T,
        rest[width : 2 * width],
        out,
        shares[0],
        shares[1],
        shares[2],
        sums[6:12].reshape(wide, units).astype(F32),
        rest[2 * width :],
        sums[:6].reshape(units, wide).astype(F32),
        shares[3],
        shares[4],
        shares[5],
    )


def solution(mesh):
    in_specs = (
        P(("dp", "tensor"), None),
        P("dp"),
        P("dp"),
        P(None, "tensor"),
        P("tensor"),
        P(None, "tensor"),
        P(None, "tensor"),
        P("tensor"),
        P("tensor", None),
        P(),
        P(),
        P(),
        P(None, "tensor"),
        P("tensor"),
        P("tensor", None),
        P(),
        P(),
        P(),
        P(("dp", "tensor"), None),
    )
    out_specs = (
        P(("dp", "tensor"), None),
        P(("dp", "tensor"), None),
        P(None, "tensor"),
        P("tensor"),
        P(None, "tensor"),
        P(None, "tensor"),
        P("tensor"),
        P("tensor", None),
        P("tensor"),
        P("tensor"),
        P("tensor"),
        P(None, "tensor"),
        P("tensor"),
        P("tensor", None),
        P("tensor"),
        P("tensor"),
        P("tensor"),
    )
    return jax.shard_map(shards, mesh=mesh, in_specs=in_specs, out_specs=out_specs, check_vma=False)
```

time: 835 us -> 244 us (0.29)
  waiting for transfers between devices: 492 us -> 0 us
  Pallas kernels: 0 us -> 219 us
  matrix products: 143 us -> 0 us
  local copies, waits for them, and re-layouts: 75.5 us -> 16.4 us
  blocking collectives: 50.9 us -> 0 us
  other arithmetic: 48.9 us -> 4.95 us
  between operations: 15.4 us -> 0.69 us
    pallas_call x0 -> x1, Pallas kernels: none -> 219 us  [layer(): pl.pallas_call(functools.partial(layer_kernel, groups, names), out_shape=...]
    reduce_scatter x4 -> x0, waiting for transfers between devices: 197 us -> none  [the longest x1 69.1 us: shards(): lax.psum_scatter(jnp.dot(piece, w_output, preferred_element_type=jnp.floa...]
    psum x1 -> x0, waiting for transfers between devices: 174 us -> none  [shards(): lax.psum((grad_w_joined, grad_b_query, grad_b_value, grad_w_output, grad_...]
    dot_general x47 -> x0, matrix products: 143 us -> none  [the longest x5 23.3 us: backward_attend(): jnp.einsum('hqk,khd->qhd', grad_scores, split_heads(key_rows), preferred_...]
    all_gather x4 -> x0, waiting for transfers between devices: 121 us -> none  [the longest x1 34.6 us: shards(): whole = lax.all_gather(tokens, 'tensor', axis=0, tiled=True)]
    psum x1 -> x0, blocking collectives: 40 us -> none  [shards(): lax.psum((grad_w_joined, grad_b_query, grad_b_value, grad_w_output, grad_...]
    dynamic_slice x40 -> x0, local copies, waits for them, and re-layouts: 33.1 us -> none  [shards(): lax.map(forward_attend, (by_sequence(query_rows), by_sequence(key_rows),...]
    reduce_sum x14 -> x0, other arithmetic: 22.1 us -> none  [the longest x2 6.78 us: norm_backward(): return (result, jnp.sum(grad * unit, axis=0), jnp.sum(grad, axis=0))]
  transfers between devices with their start and end apart: 9 -> 0, of which waited for: 9 -> 0; matrix products, arithmetic and copies ran while one was open for 3% -> 0% of each run, Pallas kernels for 0% -> 0%
where the time goes in v3:
time: 244 us; the launch traced here: 241 us
  Pallas kernels  219 us (90%)
  local copies, waits for them, and re-layouts  16.4 us (7%)
  other arithmetic  4.95 us (2%)
    pallas_call x1, Pallas kernels, layer(): pl.pallas_call(functools.partial(layer_kernel, groups, names), out_shape=...  219 us

profile of v3, /device:TPU:0, one launch (start us, length us, event | category | flops | bytes accessed | tf_op | source)
XLA Modules:
  0.0 240.6 jit_solution(10317282942269472999)
XLA Ops:
  0.7 0.7 stack.39
  1.3 0.7 stack.40
  2.0 0.7 stack.41
  2.7 0.7 stack.49
  3.4 0.7 stack.42
  4.1 0.7 stack.43
  4.8 0.7 stack.44
  5.5 0.7 concatenate.6
  6.2 0.7 concatenate.7
  6.9 0.6 stack.46.refs_8_
  7.5 0.6 stack.51.refs_9_
  8.2 1.3 reshape.87.refs_10_
  9.5 218.6 %shard_map.314 = (bf16[640,768]{1,0:T(8,128)(2,1)}, bf16[640,768]{1,0:T(8,128)(2,1)}, bf16[18,8,16,768]{3,2,1,0:T(8,128)(2,1)}, f32[3,768]{1,0:T(4,128)}) custom-call(bf16[640,768]{1,0:T(8,128)(2,1)} %refs_0_.1, bf16[3,64,768]{2,1,0:T(8,128)(2,1)} %bitcast.36, bf16[3,64,768]{2,1,0:T(8,128)(2,1)} %bitcast.37, bf16[3,64,768]{2,1,0:T(8,128)(2,1)} %bitcast.38, ...), custom_call_target="tpu_custom_call" | custom-call | tf_op jit(solution)/shard_map/pallas_call | solution.py:866
  228.0 1.3 slice_reduce_fusion
  229.3 0.7 reshape.89
  230.1 0.7 fusion.2
  230.7 2.3 fusion
  233.0 0.1 fusion.1
  233.1 1.1 convert_bitcast_fusion.2
  234.2 1.1 convert_bitcast_fusion
  235.4 0.0 copy-start.1
  235.4 2.7 %bitcast_convert_fusion = (f32[768,768]{1,0:T(8,128)}, f32[768,768]{1,0:T(8,128)}) fusion(bf16[6,8,16,768]{3,2,1,0:T(8,128)(2,1)S(1)} %get-tuple-element.25, bf16[6,8,16,768]{3,2,1,0:T(8,128)(2,1)S(1)} %get-tuple-element.26), kind=kLoop, calls=%fused_computation | loop fusion | flops 1179648 | bytes 7077888 | tf_op jit(solution)/shard_map/convert_element_type | solution.py:947
  238.1 0.0 copy-start
  238.1 0.0 copy-done.1
  238.1 0.9 copy.38
  239.0 0.6 copy-done
  239.6 0.9 copy.39
  (5 shorter events, 0.0 us)
Async XLA Ops:
  235.4 2.7 %copy-start.1 = (bf16[640,768]{1,0:T(8,128)(2,1)S(1)}, bf16[640,768]{1,0:T(8,128)(2,1)}, u32[]{:S(2)}) copy-start(bf16[640,768]{1,0:T(8,128)(2,1)} %get-tuple-element.63) | copy-start | bytes 2949124
  238.1 1.6 copy-start

commit v4 on v3

--- a/solution.py
+++ b/solution.py
@@ -26,6 +26,7 @@
 OWNERS = 8
 PAIRS = 3
 PIECES = 18
+LAGS = (6, 4, 2, 0)
 
 
 def dg(left, right, dims=NN):
@@ -121,38 +122,51 @@
         copy.wait_send()
         self.sent = [other for other in self.sent if other is not copy]
 
+    @staticmethod
+    def where(u):
+        if isinstance(u, int):
+            return 2 * (u // 6) + u % 2, u % 6 // 2
+        return 2 * lax.div(u, 6) + lax.rem(u, 2), lax.div(lax.rem(u, 6), 2)
+
     def y_copy(self, u):
         r = self.r
+        b, j = self.where(u)
         side = {"tensor": (self.place + 2) % 4}
-        return remote(r.grads_other.at[u], r.from_side.at[u], r.y_out.at[u], r.y_in.at[u], side)
+        both = pl.ds(0, 2)
+        return remote(r.grads_other.at[b, both, j], r.from_side.at[b, both, j], r.y_out.at[u], r.y_in.at[u], side)
 
     def x_copy(self, u):
         r = self.r
-        away = r.grads_own.at[u, pl.ds((1 - self.x) * 4, 4)]
-        return remote(away, r.from_x.at[u], r.x_out.at[u], r.x_in.at[u], self.dp_at(1 - self.x, self.z))
+        b, j = self.where(u)
+        away = r.grads_own.at[b, 1 - self.x, j]
+        return remote(away, r.from_x.at[b, j], r.x_out.at[u], r.x_in.at[u], self.dp_at(1 - self.x, self.z))
 
     def z_copy(self, u, step):
         r = self.r
+        b, j = self.where(u)
         there = (self.z + step) % 4
-        away = r.grads_own.at[u, self.x * 4 + there]
+        away = r.grads_own.at[b, self.x, j, there]
         out, into = r.z_out.at[u, step - 1], r.z_in.at[u, step - 1]
-        return remote(away, r.from_z.at[u, step - 1], out, into, self.dp_at(self.x, there))
+        return remote(away, r.from_z.at[b, j, step - 1], out, into, self.dp_at(self.x, there))
 
     def f_copy(self, u, step):
         r = self.r
+        b, j = self.where(u)
         peer = {"dp": ((self.far + step) % self.more) * OWNERS + self.z * 2 + self.x}
-        own = r.grads_own.at[u, self.x * 4 + self.z]
+        own = r.grads_own.at[b, self.x, j, self.z]
         return remote(own, r.from_far.at[u, step - 1], r.f_out.at[u, step - 1], r.f_in.at[u, step - 1], peer)
 
     def g_copy(self, u, step, origin):
         r = self.r
-        piece = r.total.at[u, self.x * 4 + origin]
+        b, j = self.where(u)
+        piece = r.total.at[b, self.x, j, origin]
         out, into = r.g_out.at[u, step - 1], r.g_in.at[u, step - 1]
         return remote(piece, piece, out, into, self.dp_at(self.x, (self.z + step) % 4))
 
     def h_copy(self, u, half):
         r = self.r
-        piece = r.total.at[u, pl.ds(half * 4, 4)]
+        b, j = self.where(u)
+        piece = r.total.at[b, half, j]
         return remote(piece, piece, r.h_out.at[u], r.h_in.at[u], self.dp_at(1 - self.x, self.z))
 
     def y_start(self, u):
@@ -160,33 +174,37 @@
 
     def x_start(self, u):
         r = self.r
+        b, j = self.where(u)
         self.y_copy(u).wait_recv()
-        r.grads_own[u] = (r.grads_own[u].astype(F32) + r.from_side[u].astype(F32)).astype(BF16)
+        for half in range(2):
+            summed = r.grads_own[b, half, j].astype(F32) + r.from_side[b, half, j].astype(F32)
+            r.grads_own[b, half, j] = summed.astype(BF16)
         self.x_copy(u).start()
 
     def z_start(self, u):
         r = self.r
+        b, j = self.where(u)
         self.x_copy(u).wait_recv()
-        kept = pl.ds(self.x * 4, 4)
-        r.grads_own[u, kept] = (r.grads_own[u, kept].astype(F32) + r.from_x[u].astype(F32)).astype(BF16)
+        summed = r.grads_own[b, self.x, j].astype(F32) + r.from_x[b, j].astype(F32)
+        r.grads_own[b, self.x, j] = summed.astype(BF16)
         for step in (1, 2, 3):
             self.z_copy(u, step).start()
 
     def g_start(self, u):
         r = self.r
-        own = self.x * 4 + self.z
-        value = r.grads_own[u, own].astype(F32)
+        b, j = self.where(u)
+        value = r.grads_own[b, self.x, j, self.z].astype(F32)
         for step in (1, 2, 3):
             self.z_copy(u, step).wait_recv()
-            value = value + r.from_z[u, step - 1].astype(F32)
+            value = value + r.from_z[b, j, step - 1].astype(F32)
         if self.more > 1:
-            r.grads_own[u, own] = value.astype(BF16)
+            r.grads_own[b, self.x, j, self.z] = value.astype(BF16)
             for step in range(1, self.more):
                 self.f_copy(u, step).start()
             for step in range(1, self.more):
                 self.f_copy(u, step).wait_recv()
                 value = value + r.from_far[u, step - 1].astype(F32)
-        r.total[u, own] = value.astype(BF16)
+        r.total[b, self.x, j, self.z] = value.astype(BF16)
         for step in (1, 2, 3):
             self.g_copy(u, step, self.z).start()
 
@@ -195,11 +213,16 @@
             self.g_copy(u, step, (self.z - step + 4) % 4).wait_recv()
         self.h_copy(u, self.x).start()
 
-    def advance(self, n):
+    def advance(self, n, least=0):
         stages = (self.h_start, self.g_start, self.z_start, self.x_start)
-        for behind, stage in zip((3, 2, 1, 0), stages):
-            if not isinstance(n, int) or 0 <= n - behind < PIECES:
+        for behind, stage in zip(LAGS, stages):
+            if isinstance(n, int):
+                if 0 <= n - behind < PIECES:
+                    stage(n - behind)
+            elif least >= behind:
                 stage(n - behind)
+            else:
+                pl.when(n >= behind)(functools.partial(stage, n - behind))
 
     def finish(self):
         def settle(u, _):
@@ -263,9 +286,20 @@
         ("down", r.w_outer, r.down_own),
         ("cotangent", r.cotangent, r.grad_tokens),
     ]
+    sources += [("shift", r.b_query, r.narrow.at[0]), ("shift", r.b_value, r.narrow.at[1])]
+    sources += [("shift", r.b_inner, r.biases.at[0])]
+    gains = (r.b_output, r.first_gain, r.first_shift, r.b_outer, r.second_gain, r.second_shift)
+    sources += [("gain", ref, r.vectors.at[i]) for i, ref in enumerate(gains)]
+    sources += [("segment", r.segment_ids.at[pl.ds(i * LEN, LEN)], r.segments.at[i]) for i in range(5)]
     for n, (name, source, target) in enumerate(sources):
-        loads[name] = pltpu.make_async_copy(source, target, r.l_sem.at[n])
-        loads[name].start()
+        copy = pltpu.make_async_copy(source, target, r.l_sem.at[n])
+        copy.start()
+        loads.setdefault(name, []).append(copy)
+
+    def loaded(*wanted):
+        for name in wanted:
+            for copy in loads[name]:
+                copy.wait()
 
     pl.semaphore_wait(barrier, 3 + groups - 1)
     rounds = Rounds(r, groups)
@@ -283,13 +317,13 @@
 
     def by_rows(source, target, n):
         def view(ref, half):
-            return ref.at[at_rows(half * 4 * block + n * 2 * block, 2 * block)]
+            return ref.at[at_rows((half * 4 + n) * block, block)]
 
         return source, target, view
 
     fetches = [by_heads(w, i) for i, w in enumerate((r.w_query, r.w_key, r.w_value, r.w_output))]
-    fetches += [by_rows(r.w_inner, r.in_other, n) for n in range(2)]
-    fetches += [by_rows(r.w_outer, r.down_other, n) for n in range(2)]
+    fetches += [by_rows(r.w_inner, r.in_other, n) for n in range(4)]
+    fetches += [by_rows(r.w_outer, r.down_other, n) for n in range(4)]
 
     def fetch_copy(n):
         source, target, view = fetches[n]
@@ -315,10 +349,14 @@
     token_copy = rounds.start(remote(r.tokens, r.x_rows.at[own_at], r.s_out.at[0], r.s_in.at[0], core_peer))
     token_wait = remote(r.tokens, r.x_rows.at[at_rows(theirs, own_rows)], r.s_out.at[0], r.s_in.at[0], core_peer)
     fetch(0, 1, 2)
-    vector_copy = rounds.start(remote(r.biases, r.biases_other, r.s_out.at[1], r.s_in.at[1], side_peer))
+    loaded("shift")
+    vector_copies = [
+        rounds.start(remote(r.biases, r.biases_other, r.s_out.at[1], r.s_in.at[1], side_peer)),
+        rounds.start(remote(r.narrow, r.narrow_other, r.s_out.at[5], r.s_in.at[5], side_peer)),
+    ]
 
     def project(shard, which, start, count, size):
-        shifts = (r.biases, r.biases_other)[shard]
+        shifts = (r.narrow, r.narrow_other)[shard]
         for i in which:
             target = (r.q, r.k, r.v)[i]
             weights = r.w_att[i, :, shard].reshape(width, wide)
@@ -327,9 +365,9 @@
                 block = at_rows(start + n * size, size)
                 value = dg(r.x_rows[block, :], weights, NT)
                 if i == 0:
-                    value = value + shifts[0:1, 0:width]
+                    value = value + shifts[0:1, :]
                 if i == 2:
-                    value = value + shifts[1:2, 0:width]
+                    value = value + shifts[1:2, :]
                 value = value.astype(BF16)
                 for j in range(PAIRS):
                     lane = (2 * j + shard) * HD
@@ -338,9 +376,8 @@
 
             lax.fori_loop(0, count // size, body, 0)
 
-    loads["tokens"].wait()
-    for name in ("q", "k", "v"):
-        loads[name].wait()
+    loaded("tokens")
+    loaded("q", "k", "v")
     project(0, (0, 1, 2), mine, own_rows, chunk)
 
     token_wait.wait_recv()
@@ -351,9 +388,11 @@
     far_copy = rounds.start(
         remote(r.x_rows.at[near_at], r.x_rows.at[far_at], r.s_out.at[2], r.s_in.at[2], side_peer)
     )
-    fetch(3, 4, 5, 6, 7)
+    fetch(*range(3, 12))
     project(0, (0, 1, 2), theirs, own_rows, chunk)
     hand_on(0)
+
+    loaded("segment")
 
     def mask_block(at, row, places, length, count):
         column = jnp.transpose(jnp.broadcast_to(row.astype(F32), (128, LEN)))[:, 0:1]
@@ -383,45 +422,47 @@
     def front_whole(shard, first_pair, last_pair):
         cols = slice(shard * HD, (shard + 1) * HD)
 
-        def body(n, _):
-            j, i = n // 2, n % 2
+        def body(j, _):
             lanes = pair_lanes(j)
-            block = at_rows(side * HALF + i * LEN, LEN)
-            at = pl.ds(pl.multiple_of(i * LEN, LEN), LEN)
-            out, row = attend_front(
-                r.q[block, lanes][:, cols], r.k[block, lanes][:, cols], r.v[block, lanes][:, cols], r.bias[:, at]
-            )
-            front_store(shard, block, lanes, out)
-            r.lse[pl.ds(2 * j + shard, 1), at] = row
+            for i in range(2):
+                block = at_rows(side * HALF + i * LEN, LEN)
+                at = pl.ds(i * LEN, LEN)
+                out, row = attend_front(
+                    r.q[block, lanes][:, cols], r.k[block, lanes][:, cols], r.v[block, lanes][:, cols], r.bias[:, at]
+                )
+                front_store(shard, block, lanes, out)
+                r.lse[pl.ds(2 * j + shard, 1), at] = row
             return 0
 
-        lax.fori_loop(2 * first_pair, 2 * last_pair, body, 0)
-
-    def front_half(shard):
-        cols = slice(shard * HD, (shard + 1) * HD)
-
+        lax.fori_loop(first_pair, last_pair, body, 0)
+
+    def front_half():
         def body(j, _):
             lanes = pair_lanes(j)
             block = pl.ds(c_start, HALF)
             at = pl.ds(2 * LEN, HALF)
-            out, row = attend_front(
-                r.q[block, lanes][:, cols], r.kc[:, lanes][:, cols], r.vc[:, lanes][:, cols], r.bias[:, at]
-            )
-            front_store(shard, block, lanes, out)
-            r.lse[pl.ds(2 * j + shard, 1), at] = row
+            q, k, v = r.q[block, lanes], r.kc[:, lanes], r.vc[:, lanes]
+            outs = []
+            for shard in range(2):
+                cols = slice(shard * HD, (shard + 1) * HD)
+                out, row = attend_front(q[:, cols], k[:, cols], v[:, cols], r.bias[:, at])
+                outs.append(out)
+                r.lse[pl.ds(2 * j + shard, 1), at] = row
+            r.ctx[block, lanes] = jnp.concatenate(outs, axis=1)
             return 0
 
         lax.fori_loop(0, PAIRS, body, 0)
 
-    front_whole(0, 0, 1)
+    front_whole(0, 0, 2)
     hand_on(2)
-    front_whole(0, 1, 3)
+    front_whole(0, 2, 3)
     far_copy.wait_recv()
     far_pass = rounds.start(
         remote(r.x_rows.at[far_at], r.x_rows.at[far_at], r.s_out.at[3], r.s_in.at[3], core_peer)
     )
     far_wait = remote(r.x_rows.at[far_there], r.x_rows.at[far_there], r.s_out.at[3], r.s_in.at[3], core_peer)
-    vector_copy.wait_recv()
+    for copy in vector_copies:
+        copy.wait_recv()
     fetched(0)
     project(1, (0,), 0, rows, chunk)
     fetched(1)
@@ -435,12 +476,13 @@
     for own, near_far in ((r.k, r.kc), (r.v, r.vc)):
         near_far[pl.ds(0, HALF), :] = own[pl.ds(c_start, HALF), :]
         near_far[pl.ds(HALF, HALF), :] = own[pl.ds(rows, HALF), :]
-    front_whole(1, 0, 3)
-    front_half(0)
-    front_half(1)
+    front_whole(1, 0, 2)
     hand_on(4)
-
-    loads["o"].wait()
+    front_whole(1, 2, 3)
+    hand_on(5)
+    front_half()
+
+    loaded("o")
     fetched(3)
 
     def pairs_of(i):
@@ -457,7 +499,7 @@
 
     def trade_rows(compute, keep):
         def away_body(block, local):
-            r.partial[local, :] = compute(block).astype(BF16)
+            r.partial[local, :] = compute(block, local, True).astype(BF16)
 
         each(theirs, own_rows, chunk, away_body)
         n = len(trades)
@@ -466,7 +508,7 @@
         )
 
         def own_body(block, local):
-            keep(local, compute(block))
+            keep(local, compute(block, local, False))
 
         each(mine, own_rows, chunk, own_body)
         trades[n].wait_recv()
@@ -480,7 +522,8 @@
     def keep_acc(local, value):
         r.acc[local, :] = value
 
-    trade_rows(lambda block: dg(r.ctx[block, :], pairs_of(3)), keep_acc)
+    trade_rows(lambda block, local, away: dg(r.ctx[block, :], pairs_of(3)), keep_acc)
+    loaded("gain")
     b_output, first_gain, first_shift = (r.vectors[i : i + 1, :] for i in range(3))
     b_outer, second_gain, second_shift = (r.vectors[i : i + 1, :] for i in range(3, 6))
 
@@ -493,40 +536,58 @@
 
     each(mine, own_rows, strip, first_norm)
     first_copy, first_wait = gather_rows(r.first, 0)
-    hand_on(5)
-
-    def expand(shard, start):
+    hand_on(6)
+
+    def expand(shard, start, part=None):
         weights = (r.in_own, r.in_other)[shard]
         shifts = (r.biases, r.biases_other)[shard]
         hidden, slope = ((r.hidden_own, r.slope_own), (r.hidden_other, r.slope_other))[shard]
 
         def body(block, _):
-            value, gradient = gelu_and_slope(dg(r.first[block, :], weights[...]) + shifts[2:3, :])
+            value, gradient = gelu_and_slope(dg(r.first[block, :], weights[...]) + shifts[0:1, :])
             hidden[block, :] = value.astype(BF16)
             slope[block, :] = gradient.astype(BF16)
 
-        each(start, own_rows, chunk, body)
-
-    loads["in"].wait()
+        if part is None:
+            each(start, own_rows, chunk, body)
+        else:
+            each(start + part * chunk, chunk, chunk, body)
+
+    loaded("in")
     expand(0, mine)
+    hand_on(7)
     first_wait.wait_recv()
     expand(0, theirs)
-    hand_on(6)
-    fetched(4, 5)
-    expand(1, theirs)
-    expand(1, mine)
-    loads["down"].wait()
-    hand_on(7)
-    fetched(6, 7)
+    hand_on(8)
+    loaded("down")
+
+    def own_part(target):
+        def body(block, local):
+            target[local, :] = dg(r.hidden_own[block, :], r.down_own[...])
+
+        return body
+
+    each(theirs, own_rows, chunk, own_part(r.spare))
+    each(mine, own_rows, chunk, own_part(r.second))
+    hand_on(9)
+    fetched(4, 5, 6, 7)
+    expand(1, theirs, 0)
+    hand_on(10)
+    expand(1, theirs, 1)
+    expand(1, mine, 0)
+    hand_on(11)
+    expand(1, mine, 1)
+    fetched(8, 9, 10, 11)
+
+    def other_part(block, local, away):
+        kept = r.spare if away else r.second
+        return kept[local, :] + dg(r.hidden_other[block, :], r.down_other[...])
 
     def keep_second(local, value):
         r.second[local, :] = value
 
-    trade_rows(
-        lambda block: dg(r.hidden_own[block, :], r.down_own[...]) + dg(r.hidden_other[block, :], r.down_other[...]),
-        keep_second,
-    )
-    loads["cotangent"].wait()
+    trade_rows(other_part, keep_second)
+    loaded("cotangent")
     zero = jnp.zeros((1, wide), F32)
 
     def second_norm(n, carry):
@@ -564,22 +625,35 @@
     sum_other = contract(1, mine, jnp.zeros((1, units), F32))
     feed_wait.wait_recv()
 
-    def weight_blocks(target, first_piece, left, right, send):
+    def weight_blocks(target, band, left, right, first):
         columns = left.shape[1] // 3
 
+        def body(n, _):
+            value = dg(left[:, pl.ds(pl.multiple_of(n * columns, 128), columns)], right[...], TN).astype(BF16)
+            for i in range(4):
+                at = 4 * n + i
+                b, h, j = band + lax.div(at, 6), lax.div(lax.rem(at, 6), 3), lax.rem(at, 3)
+                target[b, h, j] = value[i * HD : (i + 1) * HD].reshape(4, HD // 4, value.shape[1])
+            if first is not None:
+
+                @pl.when(n == 0)
+                def _():
+                    rounds.y_start(first)
+
+            return 0
+
+        lax.fori_loop(0, 3, body, 0)
+
+    def send(first, last):
         def body(u, _):
-            value = dg(left[:, pl.ds(pl.multiple_of(u * columns, 128), columns)], right[...], TN).astype(BF16)
-            at = first_piece + 2 * u
-            target[pl.ds(at, 2)] = value.reshape(2, OWNERS, columns // (2 * OWNERS), value.shape[1])
-            if send:
-                rounds.y_start(at)
-                rounds.y_start(at + 1)
+            rounds.y_start(u)
             return 0
 
-        lax.fori_loop(0, 3, body, 0)
-
-    weight_blocks(r.grads_other, 0, r.hidden_other, r.feed, True)
-    weight_blocks(r.grads_own, 0, r.hidden_own, r.feed, False)
+        lax.fori_loop(first, last, body, 0)
+
+    weight_blocks(r.grads_other, 0, r.hidden_other, r.feed, 0)
+    send(1, 6)
+    weight_blocks(r.grads_own, 0, r.hidden_own, r.feed, None)
     sum_own = contract(0, theirs, sum_own)
     sum_other = contract(1, theirs, sum_other)
     rounds.advance(0)
@@ -588,10 +662,11 @@
         r.second[local, :] = r.second[local, :] + value
 
     trade_rows(
-        lambda block: dg(r.slope_own[block, :], r.in_own[...], NT) + dg(r.slope_other[block, :], r.in_other[...], NT),
+        lambda block, local, away: dg(r.slope_own[block, :], r.in_own[...], NT) + dg(r.slope_other[block, :], r.in_other[...], NT),
         keep_first,
     )
     rounds.settle(feed_copy)
+    rounds.advance(1)
 
     def first_back(n, carry):
         block, local = at_rows(mine + n * strip, strip), at_rows(n * strip, strip)
@@ -606,10 +681,11 @@
 
     sum_first_gain, sum_first_shift, sum_b_output = lax.fori_loop(0, own_rows // strip, first_back, (zero, zero, zero))
     branch_copy, branch_wait = gather_rows(r.feed, 2)
-    weight_blocks(r.grads_other, 6, r.first, r.slope_other, True)
-    rounds.advance(1)
-    weight_blocks(r.grads_own, 6, r.first, r.slope_own, False)
     rounds.advance(2)
+    weight_blocks(r.grads_other, 2, r.first, r.slope_other, None)
+    send(6, 12)
+    weight_blocks(r.grads_own, 2, r.first, r.slope_own, None)
+    rounds.advance(3)
     branch_wait.wait_recv()
 
     dq = r.hidden_own.at[:, pl.ds(0, both)]
@@ -638,13 +714,13 @@
         return 0
 
     lax.fori_loop(0, PAIRS, back_half, 0)
-    rounds.advance(3)
+    rounds.advance(4)
 
     grad_out = dg(r.ctx[...], r.feed[...], TN).astype(BF16)
     for j in range(PAIRS):
         for shard, target in ((0, r.grads_own), (1, r.grads_other)):
             lane = (2 * j + shard) * HD
-            target[12 + 2 * j + 1, 4:] = grad_out[lane : lane + HD].reshape(4, HD // 4, wide)
+            target[5, 1, j] = grad_out[lane : lane + HD].reshape(4, HD // 4, wide)
 
     def back_whole(j):
         def body(i, _):
@@ -674,19 +750,22 @@
         for shard, target in ((0, r.grads_own), (1, r.grads_other)):
             cut = slice(shard * HD, (shard + 1) * HD)
             pieces = [v[cut].reshape(4, HD // 4, wide) for v in (first, rest[: 2 * HD], rest[2 * HD :])]
-            target[at, 0:4] = pieces[0]
-            target[at, 4:8] = pieces[1]
-            target[at + 1, 0:4] = pieces[2]
+            target[4, 0, j] = pieces[0]
+            target[4, 1, j] = pieces[1]
+            target[5, 0, j] = pieces[2]
         rounds.y_start(at)
         rounds.y_start(at + 1)
 
     def back_pair(j, _):
         back_whole(j)
+        rounds.advance(5 + 2 * j, 5)
         weight_pair(j)
-        rounds.advance(4 + j)
+        rounds.advance(6 + 2 * j, 6)
         return 0
 
     lax.fori_loop(0, PAIRS, back_pair, 0)
+
+    rounds.advance(11)
 
     def bias_sum(*grads):
         total = sum(column_sum(part) for part in grads)
@@ -709,7 +788,7 @@
         out, into = r.i_out.at[step - 1], r.i_in.at[step - 1]
         tiny_copies.append(rounds.start(remote(r.tiny.at[peer], r.tiny_side.at[step - 1], out, into, {"tensor": peer})))
 
-    def input_rows(block):
+    def input_rows(block, local, away):
         value = dg(dq[block, :], pairs_of(0))
         value = value + dg(dk[block, :], pairs_of(1))
         return value + dg(dv[block, :], pairs_of(2))
@@ -720,15 +799,34 @@
     far_trade = rounds.start(
         remote(r.far_part.at[give], r.far_half, r.s_out.at[4], r.s_in.at[4], core_peer)
     )
+    rounds.advance(12)
     far_trade.wait_recv()
     r.far_send[...] = (r.far_part[keep, :].astype(F32) + r.far_half[...].astype(F32)).astype(BF16)
     owner = {"tensor": (1 - side) * 2 + side}
     rounds.start(remote(r.far_send, r.far_in.at[core], r.o_out, r.o_in.at[core], owner))
 
     trade_rows(input_rows, keep_first)
-
-    for n in (7, 8, 9, 10):
-        rounds.advance(n)
+    rounds.advance(13)
+
+    total = r.tiny[place]
+    for step in (1, 2, 3):
+        tiny_copies[step - 1].wait_recv()
+        total = total + r.tiny_side[step - 1]
+    r.tiny_all[0] = total
+
+    def tell(step, _):
+        peer = {"dp": (group + step) % groups}
+        remote(r.tiny_all.at[0], r.tiny_all.at[step], r.d_out.at[step], r.d_in.at[step], peer).start()
+        return 0
+
+    lax.fori_loop(1, groups, tell, 0)
+
+    def pump(n, _):
+        rounds.advance(n, 14)
+        return 0
+
+    lax.fori_loop(14, PIECES, pump, 0)
+    rounds.advance(PIECES)
 
     @pl.when(core == 1 - side)
     def _():
@@ -743,18 +841,9 @@
 
     each(mine, own_rows, strip, finish)
 
-    total = r.tiny[place]
-    for step in (1, 2, 3):
-        tiny_copies[step - 1].wait_recv()
-        total = total + r.tiny_side[step - 1]
-    r.tiny_all[0] = total
-
-    def tell(step, _):
-        peer = {"dp": (group + step) % groups}
-        remote(r.tiny_all.at[0], r.tiny_all.at[step], r.d_out.at[step], r.d_in.at[step], peer).start()
-        return 0
-
-    lax.fori_loop(1, groups, tell, 0)
+    for n in range(PIECES + 1, PIECES + LAGS[0]):
+        rounds.advance(n)
+
     def hear(step, total):
         peer = {"dp": (group + step) % groups}
         copy = remote(r.tiny_all.at[0], r.tiny_all.at[step], r.d_out.at[step], r.d_in.at[step], peer)
@@ -763,13 +852,6 @@
 
     r.small[...] = lax.fori_loop(1, groups, hear, r.tiny_all[0])
 
-    def pump(n, _):
-        rounds.advance(n)
-        return 0
-
-    lax.fori_loop(11, PIECES, pump, 0)
-    for n in range(PIECES, PIECES + 3):
-        rounds.advance(n)
     rounds.finish()
 
 
@@ -781,10 +863,11 @@
     rows, both = 2 * own_rows, 2 * heads[0] * heads[1]
     more = groups // OWNERS
     share = wide // 6 // OWNERS
+    bands = (6, 2, 3, 4, share, wide)
     outs = {
         "output": ((own_rows, wide), BF16),
         "grad_tokens": ((own_rows, wide), BF16),
-        "total": ((PIECES, OWNERS, share, wide), BF16),
+        "total": (bands, BF16),
         "small": ((3, wide), F32),
     }
     room = {
@@ -794,7 +877,12 @@
         "in_other": ((wide, units), BF16),
         "down_own": ((units, wide), BF16),
         "down_other": ((units, wide), BF16),
+        "vectors": ((8, wide), F32),
+        "biases": ((8, wide), F32),
         "biases_other": ((8, wide), F32),
+        "narrow": ((8, both // 2), F32),
+        "narrow_other": ((8, both // 2), F32),
+        "segments": ((8, LEN), jnp.int32),
         "bias": ((LEN, rows), F32),
         "q": ((rows, both), BF16),
         "k": ((rows + HALF, both), BF16),
@@ -813,30 +901,31 @@
         "slope_own": ((rows, units), BF16),
         "slope_other": ((rows, units), BF16),
         "second": ((own_rows, wide), F32),
+        "spare": ((own_rows, wide), F32),
         "feed": ((rows, wide), BF16),
         "away": ((2, HALF, both), BF16),
         "far_part": ((HALF, wide), BF16),
         "far_half": ((HALF // 2, wide), BF16),
         "far_send": ((HALF // 2, wide), BF16),
         "far_in": ((2, HALF // 2, wide), BF16),
-        "grads_own": ((PIECES, OWNERS, share, wide), BF16),
-        "grads_other": ((PIECES, OWNERS, share, wide), BF16),
-        "from_side": ((PIECES, OWNERS, share, wide), BF16),
-        "from_x": ((PIECES, 4, share, wide), BF16),
-        "from_z": ((PIECES, 3, share, wide), BF16),
+        "grads_own": (bands, BF16),
+        "grads_other": (bands, BF16),
+        "from_side": (bands, BF16),
+        "from_x": ((6, 3, 4, share, wide), BF16),
+        "from_z": ((6, 3, 3, share, wide), BF16),
         "from_far": ((PIECES, more - 1, share, wide) if more > 1 else (1, 1, 16, 128), BF16),
         "tiny": ((PARTS, 3, wide), F32),
         "tiny_side": ((3, 3, wide), F32),
         "tiny_all": ((groups, 3, wide), F32),
     }
     sems = {
-        "l_sem": (8,),
-        "s_out": (5,),
-        "s_in": (5,),
-        "w_out_sem": (8,),
-        "w_in_sem": (8,),
-        "p_out_sem": (8,),
-        "p_in_sem": (8,),
+        "l_sem": (22,),
+        "s_out": (6,),
+        "s_in": (6,),
+        "w_out_sem": (12,),
+        "w_in_sem": (12,),
+        "p_out_sem": (12,),
+        "p_in_sem": (12,),
         "t_out": (4,),
         "t_in": (4,),
         "a_out": (3,),
@@ -862,7 +951,7 @@
     }
     names = list(named) + list(outs) + list(room) + list(sems)
     in_vmem = pl.BlockSpec(memory_space=pltpu.VMEM)
-    spaces = {"lengths": pltpu.SMEM, "vectors": pltpu.VMEM, "biases": pltpu.VMEM, "segments": pltpu.VMEM}
+    spaces = {"lengths": pltpu.SMEM}
     results = pl.pallas_call(
         functools.partial(layer_kernel, groups, names),
         out_shape=[jax.ShapeDtypeStruct(*spec) for spec in outs.values()],
@@ -901,12 +990,6 @@
     wide, width = w_query.shape
     units = w_inner.shape[1]
     by_head = (width // HD, HD, wide)
-    spare = jnp.zeros((wide - width,), F32)
-    rest = jnp.zeros((wide,), F32)
-    vectors = jnp.stack([b_output, first_gain, first_shift, b_outer, second_gain, second_shift, rest, rest])
-    biases = jnp.stack(
-        [jnp.concatenate([b_query, spare]), jnp.concatenate([b_value, spare]), b_inner, rest, rest, rest, rest, rest]
-    )
     done = layer(
         groups,
         {
@@ -918,33 +1001,40 @@
             "w_inner": w_inner,
             "w_outer": w_outer,
             "cotangent": cotangent,
-            "vectors": vectors,
-            "biases": biases,
-            "segments": segment_ids.reshape(-1, LEN),
+            "b_query": b_query,
+            "b_value": b_value,
+            "b_inner": b_inner,
+            "b_output": b_output,
+            "first_gain": first_gain,
+            "first_shift": first_shift,
+            "b_outer": b_outer,
+            "second_gain": second_gain,
+            "second_shift": second_shift,
+            "segment_ids": segment_ids,
             "lengths": lengths,
         },
     )
     sums = done["total"]
-    attention = sums[12:].reshape(PAIRS, 4, HD, wide)
-    query, key, value, out = (attention[:, i].reshape(width, wide).astype(F32) for i in range(4))
-    total = done["small"].reshape(-1)
-    shares = total[: 6 * width].reshape(6, width)
-    rest = total[6 * width :]
+    query, key = (sums[4, i].reshape(width, wide).astype(F32) for i in range(2))
+    value, out = (sums[5, i].reshape(width, wide).astype(F32) for i in range(2))
+    small = done["small"]
+    shares = [small[0, i * width : (i + 1) * width] for i in range(4)]
+    shares += [small[1, i * width : (i + 1) * width] for i in range(4)]
     return (
         done["output"],
         done["grad_tokens"],
         query.T,
-        rest[:width],
+        shares[6],
         key.T,
         value.T,
-        rest[width : 2 * width],
+        shares[7],
         out,
         shares[0],
         shares[1],
         shares[2],
-        sums[6:12].reshape(wide, units).astype(F32),
-        rest[2 * width :],
-        sums[:6].reshape(units, wide).astype(F32),
+        sums[2:4].reshape(wide, units).astype(F32),
+        small[2],
+        sums[0:2].reshape(units, wide).astype(F32),
         shares[3],
         shares[4],
         shares[5],

time: 244 us -> 212 us (0.87); the launches traced: 241 us -> 212 us
  Pallas kernels: 219 us -> 198 us
  local copies, waits for them, and re-layouts: 16.4 us -> 8.42 us
    pallas_call x1, Pallas kernels: 219 us -> 198 us  [layer(): pl.pallas_call(functools.partial(layer_kernel, groups, names), out_shape=...]
    another operation x14 -> x0, local copies, waits for them, and re-layouts: 6.13 us -> none  [the longest x8 4.78 us: shards(): jnp.stack([b_output, first_gain, first_shift, b_outer, second_gain, secon...]
where the time goes in v4:
time: 212 us
  Pallas kernels  198 us (93%)
  local copies, waits for them, and re-layouts  8.42 us (4%)
  other arithmetic  4.95 us (2%)
    pallas_call x1, Pallas kernels, layer(): pl.pallas_call(functools.partial(layer_kernel, groups, names), out_shape=...  198 us

profile of v4, /device:TPU:0, one launch (start us, length us, event | category | flops | bytes accessed | tf_op | source)
XLA Modules:
  0.0 211.7 jit_solution(16885912808078214348)
XLA Ops:
  0.7 197.6 %shard_map.314 = (bf16[640,768]{1,0:T(8,128)(2,1)}, bf16[640,768]{1,0:T(8,128)(2,1)}, bf16[6,2,3,4,16,768]{5,4,3,2,1,0:T(8,128)(2,1)}, f32[3,768]{1,0:T(4,128)}) custom-call(bf16[640,768]{1,0:T(8,128)(2,1)} %refs_0_.1, bf16[3,64,768]{2,1,0:T(8,128)(2,1)} %bitcast.42, bf16[3,64,768]{2,1,0:T(8,128)(2,1)} %bitcast.43, bf16[3,64,768]{2,1,0:T(8,128)(2,1)} %bitcast.44, ...), custom_call_target="tpu_custom_call" | custom-call | tf_op jit(solution)/shard_map/pallas_call | solution.py:955
  198.3 1.3 slice_reduce_fusion
  199.6 1.5 fusion.2
  201.1 1.3 fusion.1
  202.4 1.8 fusion
  204.2 1.1 convert_bitcast_fusion.2
  205.4 1.1 convert_bitcast_fusion
  206.5 0.0 copy-start.1
  206.5 2.7 %bitcast_convert_fusion = (f32[768,768]{1,0:T(8,128)}, f32[768,768]{1,0:T(8,128)}) fusion(bf16[2,2,3,4,16,768]{5,4,3,2,1,0:T(8,128)(2,1)S(1)} %get-tuple-element.25, bf16[2,2,3,4,16,768]{5,4,3,2,1,0:T(8,128)(2,1)S(1)} %get-tuple-element.26), kind=kLoop, calls=%fused_computation | loop fusion | flops 1179648 | bytes 7077888 | tf_op jit(solution)/shard_map/convert_element_type | solution.py:1037
  209.2 0.0 copy-start
  209.2 0.0 copy-done.1
  209.2 0.9 copy.38
  210.1 0.6 copy-done
  210.7 0.9 copy.39
Async XLA Ops:
  206.5 2.7 %copy-start.1 = (bf16[640,768]{1,0:T(8,128)(2,1)S(1)}, bf16[640,768]{1,0:T(8,128)(2,1)}, u32[]{:S(2)}) copy-start(bf16[640,768]{1,0:T(8,128)(2,1)} %get-tuple-element.62) | copy-start | bytes 2949124
  209.2 1.6 copy-start

commit v5 on v4

--- a/solution.py
+++ b/solution.py
@@ -828,6 +828,9 @@
     lax.fori_loop(14, PIECES, pump, 0)
     rounds.advance(PIECES)
 
+    for n in range(PIECES + 1, PIECES + LAGS[0] - 2):
+        rounds.advance(n)
+
     @pl.when(core == 1 - side)
     def _():
         start = (1 - side) * (own_rows - HALF)
@@ -841,7 +844,7 @@
 
     each(mine, own_rows, strip, finish)
 
-    for n in range(PIECES + 1, PIECES + LAGS[0]):
+    for n in range(PIECES + LAGS[0] - 2, PIECES + LAGS[0]):
         rounds.advance(n)
 
     def hear(step, total):
@@ -850,7 +853,8 @@
         copy.wait()
         return total + r.tiny_all[step]
 
-    r.small[...] = lax.fori_loop(1, groups, hear, r.tiny_all[0])
+    r.small[0:3, :] = lax.fori_loop(1, groups, hear, r.tiny_all[0])
+    r.small[3:8, :] = jnp.zeros((5, wide), F32)
 
     rounds.finish()
 
@@ -864,91 +868,91 @@
     more = groups // OWNERS
     share = wide // 6 // OWNERS
     bands = (6, 2, 3, 4, share, wide)
-    outs = {
-        "output": ((own_rows, wide), BF16),
-        "grad_tokens": ((own_rows, wide), BF16),
-        "total": (bands, BF16),
-        "small": ((3, wide), F32),
-    }
-    room = {
-        "x_rows": ((rows + HALF, wide), BF16),
-        "w_att": ((4, PAIRS, 2, HD, wide), BF16),
-        "in_own": ((wide, units), BF16),
-        "in_other": ((wide, units), BF16),
-        "down_own": ((units, wide), BF16),
-        "down_other": ((units, wide), BF16),
-        "vectors": ((8, wide), F32),
-        "biases": ((8, wide), F32),
-        "biases_other": ((8, wide), F32),
-        "narrow": ((8, both // 2), F32),
-        "narrow_other": ((8, both // 2), F32),
-        "segments": ((8, LEN), jnp.int32),
-        "bias": ((LEN, rows), F32),
-        "q": ((rows, both), BF16),
-        "k": ((rows + HALF, both), BF16),
-        "v": ((rows + HALF, both), BF16),
-        "kc": ((LEN, both), BF16),
-        "vc": ((LEN, both), BF16),
-        "ctx": ((rows, both), BF16),
-        "lse": ((8, rows), F32),
-        "partial": ((own_rows, wide), BF16),
-        "partial_in": ((own_rows, wide), BF16),
-        "acc": ((own_rows, wide), F32),
-        "inverse": ((own_rows, 1), F32),
-        "first": ((rows, wide), BF16),
-        "hidden_own": ((rows, units), BF16),
-        "hidden_other": ((rows, units), BF16),
-        "slope_own": ((rows, units), BF16),
-        "slope_other": ((rows, units), BF16),
-        "second": ((own_rows, wide), F32),
-        "spare": ((own_rows, wide), F32),
-        "feed": ((rows, wide), BF16),
-        "away": ((2, HALF, both), BF16),
-        "far_part": ((HALF, wide), BF16),
-        "far_half": ((HALF // 2, wide), BF16),
-        "far_send": ((HALF // 2, wide), BF16),
-        "far_in": ((2, HALF // 2, wide), BF16),
-        "grads_own": (bands, BF16),
-        "grads_other": (bands, BF16),
-        "from_side": (bands, BF16),
-        "from_x": ((6, 3, 4, share, wide), BF16),
-        "from_z": ((6, 3, 3, share, wide), BF16),
-        "from_far": ((PIECES, more - 1, share, wide) if more > 1 else (1, 1, 16, 128), BF16),
-        "tiny": ((PARTS, 3, wide), F32),
-        "tiny_side": ((3, 3, wide), F32),
-        "tiny_all": ((groups, 3, wide), F32),
-    }
-    sems = {
-        "l_sem": (22,),
-        "s_out": (6,),
-        "s_in": (6,),
-        "w_out_sem": (12,),
-        "w_in_sem": (12,),
-        "p_out_sem": (12,),
-        "p_in_sem": (12,),
-        "t_out": (4,),
-        "t_in": (4,),
-        "a_out": (3,),
-        "a_in": (3,),
-        "y_out": (PIECES,),
-        "y_in": (PIECES,),
-        "x_out": (PIECES,),
-        "x_in": (PIECES,),
-        "z_out": (PIECES, 3),
-        "z_in": (PIECES, 3),
-        "g_out": (PIECES, 3),
-        "g_in": (PIECES, 3),
-        "h_out": (PIECES,),
-        "h_in": (PIECES,),
-        "f_out": (PIECES, max(more - 1, 1)),
-        "f_in": (PIECES, max(more - 1, 1)),
-        "i_out": (3,),
-        "i_in": (3,),
-        "d_out": (groups,),
-        "d_in": (groups,),
-        "o_out": (),
-        "o_in": (2,),
-    }
+    outs = dict(
+        output=((own_rows, wide), BF16),
+        grad_tokens=((own_rows, wide), BF16),
+        total=(bands, BF16),
+        small=((8, wide), F32),
+    )
+    room = dict(
+        x_rows=((rows + HALF, wide), BF16),
+        w_att=((4, PAIRS, 2, HD, wide), BF16),
+        in_own=((wide, units), BF16),
+        in_other=((wide, units), BF16),
+        down_own=((units, wide), BF16),
+        down_other=((units, wide), BF16),
+        vectors=((8, wide), F32),
+        biases=((8, wide), F32),
+        biases_other=((8, wide), F32),
+        narrow=((8, both // 2), F32),
+        narrow_other=((8, both // 2), F32),
+        segments=((8, LEN), jnp.int32),
+        bias=((LEN, rows), F32),
+        q=((rows, both), BF16),
+        k=((rows + HALF, both), BF16),
+        v=((rows + HALF, both), BF16),
+        kc=((LEN, both), BF16),
+        vc=((LEN, both), BF16),
+        ctx=((rows, both), BF16),
+        lse=((8, rows), F32),
+        partial=((own_rows, wide), BF16),
+        partial_in=((own_rows, wide), BF16),
+        acc=((own_rows, wide), F32),
+        inverse=((own_rows, 1), F32),
+        first=((rows, wide), BF16),
+        hidden_own=((rows, units), BF16),
+        hidden_other=((rows, units), BF16),
+        slope_own=((rows, units), BF16),
+        slope_other=((rows, units), BF16),
+        second=((own_rows, wide), F32),
+        spare=((own_rows, wide), F32),
+        feed=((rows, wide), BF16),
+        away=((2, HALF, both), BF16),
+        far_part=((HALF, wide), BF16),
+        far_half=((HALF // 2, wide), BF16),
+        far_send=((HALF // 2, wide), BF16),
+        far_in=((2, HALF // 2, wide), BF16),
+        grads_own=(bands, BF16),
+        grads_other=(bands, BF16),
+        from_side=(bands, BF16),
+        from_x=((6, 3, 4, share, wide), BF16),
+        from_z=((6, 3, 3, share, wide), BF16),
+        from_far=((PIECES, more - 1, share, wide) if more > 1 else (1, 1, 16, 128), BF16),
+        tiny=((PARTS, 3, wide), F32),
+        tiny_side=((3, 3, wide), F32),
+        tiny_all=((groups, 3, wide), F32),
+    )
+    sems = dict(
+        l_sem=(22,),
+        s_out=(6,),
+        s_in=(6,),
+        w_out_sem=(12,),
+        w_in_sem=(12,),
+        p_out_sem=(12,),
+        p_in_sem=(12,),
+        t_out=(4,),
+        t_in=(4,),
+        a_out=(3,),
+        a_in=(3,),
+        y_out=(PIECES,),
+        y_in=(PIECES,),
+        x_out=(PIECES,),
+        x_in=(PIECES,),
+        z_out=(PIECES, 3),
+        z_in=(PIECES, 3),
+        g_out=(PIECES, 3),
+        g_in=(PIECES, 3),
+        h_out=(PIECES,),
+        h_in=(PIECES,),
+        f_out=(PIECES, max(more - 1, 1)),
+        f_in=(PIECES, max(more - 1, 1)),
+        i_out=(3,),
+        i_in=(3,),
+        d_out=(groups,),
+        d_in=(groups,),
+        o_out=(),
+        o_in=(2,),
+    )
     names = list(named) + list(outs) + list(room) + list(sems)
     in_vmem = pl.BlockSpec(memory_space=pltpu.VMEM)
     spaces = {"lengths": pltpu.SMEM}
@@ -963,6 +967,67 @@
         ),
     )(*named.values())
     return dict(zip(outs, results))
+
+
+def last_kernel(total, output, grad_tokens, small, *refs):
+    results, (low, full, rows, sums, narrow, load_sem, store_sem) = refs[:17], refs[17:]
+    loads = [pltpu.make_async_copy(small, sums, load_sem.at[14])]
+    loads += [pltpu.make_async_copy(source, rows.at[i], load_sem.at[12 + i]) for i, source in enumerate((output, grad_tokens))]
+    loads += [pltpu.make_async_copy(total.at[i], low.at[i], load_sem.at[i]) for i in range(12)]
+    for copy in loads:
+        copy.start()
+    stores = []
+
+    def store(source, target):
+        stores.append(pltpu.make_async_copy(source, target, store_sem.at[len(stores)]))
+        stores[-1].start()
+
+    loads[0].wait()
+    width = narrow.shape[1]
+    for i in range(8):
+        lane = i % 4 * width
+        narrow[i : i + 1, :] = sums[i // 4 : i // 4 + 1, lane : lane + width]
+        store(narrow.at[i], results[8 + i])
+    store(sums.at[2], results[16])
+    for i in range(2):
+        loads[1 + i].wait()
+        store(rows.at[i], results[i])
+    count = low.shape[1]
+    for i in range(12):
+        loads[3 + i].wait()
+        full[i] = low[i].astype(F32)
+        target = results[2 + i // 4].at[pl.ds(i % 4 * count, count)] if i < 8 else results[4 + i - 8]
+        store(full.at[i], target)
+    for copy in stores:
+        copy.wait()
+
+
+def last(done):
+    own_rows, wide = done["output"].shape
+    total = done["total"].reshape(12, -1, wide)
+    count = total.shape[1]
+    rows = jax.ShapeDtypeStruct((own_rows, wide), BF16)
+    large = jax.ShapeDtypeStruct((4 * count, wide), F32)
+    slim = jax.ShapeDtypeStruct((count, wide), F32)
+    outs = [rows] * 2 + [large] * 2 + [slim] * 4
+    outs += [jax.ShapeDtypeStruct((wide // PARTS,), F32)] * 8 + [jax.ShapeDtypeStruct((wide,), F32)]
+    anywhere = pl.BlockSpec(memory_space=pl.ANY)
+    return pl.pallas_call(
+        last_kernel,
+        out_shape=outs,
+        in_specs=[anywhere] * 4,
+        out_specs=[anywhere] * len(outs),
+        scratch_shapes=[
+            pltpu.VMEM(total.shape, BF16),
+            pltpu.VMEM(total.shape, F32),
+            pltpu.VMEM((2, own_rows, wide), BF16),
+            pltpu.VMEM((8, wide), F32),
+            pltpu.VMEM((8, wide // PARTS), F32),
+            pltpu.SemaphoreType.DMA((15,)),
+            pltpu.SemaphoreType.DMA((23,)),
+        ],
+        compiler_params=pltpu.CompilerParams(vmem_limit_bytes=67043328),
+    )(total, done["output"], done["grad_tokens"], done["small"])
 
 
 def shards(
@@ -992,37 +1057,32 @@
     by_head = (width // HD, HD, wide)
     done = layer(
         groups,
-        {
-            "tokens": tokens,
-            "w_query": w_query.T.reshape(by_head),
-            "w_key": w_key.T.reshape(by_head),
-            "w_value": w_value.T.reshape(by_head),
-            "w_output": w_output.reshape(by_head),
-            "w_inner": w_inner,
-            "w_outer": w_outer,
-            "cotangent": cotangent,
-            "b_query": b_query,
-            "b_value": b_value,
-            "b_inner": b_inner,
-            "b_output": b_output,
-            "first_gain": first_gain,
-            "first_shift": first_shift,
-            "b_outer": b_outer,
-            "second_gain": second_gain,
-            "second_shift": second_shift,
-            "segment_ids": segment_ids,
-            "lengths": lengths,
-        },
-    )
-    sums = done["total"]
-    query, key = (sums[4, i].reshape(width, wide).astype(F32) for i in range(2))
-    value, out = (sums[5, i].reshape(width, wide).astype(F32) for i in range(2))
-    small = done["small"]
-    shares = [small[0, i * width : (i + 1) * width] for i in range(4)]
-    shares += [small[1, i * width : (i + 1) * width] for i in range(4)]
+        dict(
+            tokens=tokens,
+            w_query=w_query.T.reshape(by_head),
+            w_key=w_key.T.reshape(by_head),
+            w_value=w_value.T.reshape(by_head),
+            w_output=w_output.reshape(by_head),
+            w_inner=w_inner,
+            w_outer=w_outer,
+            cotangent=cotangent,
+            b_query=b_query,
+            b_value=b_value,
+            b_inner=b_inner,
+            b_output=b_output,
+            first_gain=first_gain,
+            first_shift=first_shift,
+            b_outer=b_outer,
+            second_gain=second_gain,
+            second_shift=second_shift,
+            segment_ids=segment_ids,
+            lengths=lengths,
+        ),
+    )
+    output, grad_tokens, outer, inner, query, key, value, out, *shares, inner_shift = last(done)
     return (
-        done["output"],
-        done["grad_tokens"],
+        output,
+        grad_tokens,
         query.T,
         shares[6],
         key.T,
@@ -1032,9 +1092,9 @@
         shares[0],
         shares[1],
         shares[2],
-        sums[2:4].reshape(wide, units).astype(F32),
-        small[2],
-        sums[0:2].reshape(units, wide).astype(F32),
+        inner,
+        inner_shift,
+        outer,
         shares[3],
         shares[4],
         shares[5],

time: 212 us -> 204 us (0.962)
  local copies, waits for them, and re-layouts: 8.42 us -> 0 us
  Pallas kernels: 198 us -> 203 us
  other arithmetic: 4.95 us -> 0 us
    slice x4 -> x0, local copies, waits for them, and re-layouts: 5.92 us -> none  [the longest x1 1.78 us: shards(): sums[0:2].reshape(units, wide).astype(F32)]
    pallas_call x0 -> x1, Pallas kernels: none -> 5.05 us  [last(): pl.pallas_call(last_kernel, out_shape=outs, in_specs=[anywhere] * 4, out_...]
    convert_element_type x1 -> x0, other arithmetic: 2.69 us -> none  [shards(): sums[0:2].reshape(units, wide).astype(F32)]
    unnamed x6 -> x0, local copies, waits for them, and re-layouts: 2.5 us -> none
    transpose x2 -> x0, other arithmetic: 2.25 us -> none  [shards(): return (done['output'], done['grad_tokens'], query.T, shares[6], key.T, v...]
where the time goes in v5:
time: 204 us
  Pallas kernels  203 us (100%)
    pallas_call x1, Pallas kernels, layer(): pl.pallas_call(functools.partial(layer_kernel, groups, names), out_shape=...  198 us
    pallas_call x1, Pallas kernels, last(): pl.pallas_call(last_kernel, out_shape=outs, in_specs=[anywhere] * 4, out_...  5.05 us

profile of v5, /device:TPU:0, one launch (start us, length us, event | category | flops | bytes accessed | tf_op | source)
XLA Modules:
  0.0 203.5 jit_solution(490416524833735807)
XLA Ops:
  0.7 197.6 %shard_map.314 = (bf16[640,768]{1,0:T(8,128)(2,1)}, bf16[640,768]{1,0:T(8,128)(2,1)}, bf16[6,2,3,4,16,768]{5,4,3,2,1,0:T(8,128)(2,1)}, f32[8,768]{1,0:T(8,128)}) custom-call(bf16[640,768]{1,0:T(8,128)(2,1)} %refs_0_.1, bf16[3,64,768]{2,1,0:T(8,128)(2,1)} %bitcast.15, bf16[3,64,768]{2,1,0:T(8,128)(2,1)} %bitcast.16, bf16[3,64,768]{2,1,0:T(8,128)(2,1)} %bitcast.17, ...), custom_call_target="tpu_custom_call" | custom-call | tf_op jit(solution)/shard_map/pallas_call | solution.py:959
  198.3 5.0 %shard_map.315 = (bf16[640,768]{1,0:T(8,128)(2,1)}, bf16[640,768]{1,0:T(8,128)(2,1)}, f32[768,768]{1,0:T(8,128)}, f32[768,768]{1,0:T(8,128)}, f32[192,768]{1,0:T...) custom-call(bf16[12,192,768]{2,1,0:T(8,128)(2,1)} %bitcast.14, ...), custom_call_target="tpu_custom_call" | custom-call | tf_op jit(solution)/shard_map/pallas_call | solution.py:1015

commit v6 on v5

--- a/solution.py
+++ b/solution.py
@@ -557,8 +557,10 @@
     expand(0, mine)
     hand_on(7)
     first_wait.wait_recv()
-    expand(0, theirs)
+    expand(0, theirs, 0)
     hand_on(8)
+    expand(0, theirs, 1)
+    hand_on(9)
     loaded("down")
 
     def own_part(target):
@@ -568,15 +570,12 @@
         return body
 
     each(theirs, own_rows, chunk, own_part(r.spare))
+    hand_on(10)
     each(mine, own_rows, chunk, own_part(r.second))
-    hand_on(9)
+    hand_on(11)
     fetched(4, 5, 6, 7)
-    expand(1, theirs, 0)
-    hand_on(10)
-    expand(1, theirs, 1)
-    expand(1, mine, 0)
-    hand_on(11)
-    expand(1, mine, 1)
+    expand(1, theirs)
+    expand(1, mine)
     fetched(8, 9, 10, 11)
 
     def other_part(block, local, away):

time: 204 us -> 204 us (level)
  no operation moved by 1% of the time
where the time goes in v6:
time: 204 us
  Pallas kernels  203 us (100%)
    pallas_call x1, Pallas kernels, layer(): pl.pallas_call(functools.partial(layer_kernel, groups, names), out_shape=...  198 us
    pallas_call x1, Pallas kernels, last(): pl.pallas_call(last_kernel, out_shape=outs, in_specs=[anywhere] * 4, out_...  5.05 us

profile of v6, /device:TPU:0, one launch (start us, length us, event | category | flops | bytes accessed | tf_op | source)
XLA Modules:
  0.0 203.5 jit_solution(1388304367001576534)
XLA Ops:
  0.7 197.6 %shard_map.314 = (bf16[640,768]{1,0:T(8,128)(2,1)}, bf16[640,768]{1,0:T(8,128)(2,1)}, bf16[6,2,3,4,16,768]{5,4,3,2,1,0:T(8,128)(2,1)}, f32[8,768]{1,0:T(8,128)}) custom-call(bf16[640,768]{1,0:T(8,128)(2,1)} %refs_0_.1, bf16[3,64,768]{2,1,0:T(8,128)(2,1)} %bitcast.15, bf16[3,64,768]{2,1,0:T(8,128)(2,1)} %bitcast.16, bf16[3,64,768]{2,1,0:T(8,128)(2,1)} %bitcast.17, ...), custom_call_target="tpu_custom_call" | custom-call | tf_op jit(solution)/shard_map/pallas_call | solution.py:958
  198.3 5.0 %shard_map.315 = (bf16[640,768]{1,0:T(8,128)(2,1)}, bf16[640,768]{1,0:T(8,128)(2,1)}, f32[768,768]{1,0:T(8,128)}, f32[768,768]{1,0:T(8,128)}, f32[192,768]{1,0:T...) custom-call(bf16[12,192,768]{2,1,0:T(8,128)(2,1)} %bitcast.14, ...), custom_call_target="tpu_custom_call" | custom-call | tf_op jit(solution)/shard_map/pallas_call | solution.py:1014

commit v7 on v6

--- a/solution.py
+++ b/solution.py
@@ -765,6 +765,7 @@
     lax.fori_loop(0, PAIRS, back_pair, 0)
 
     rounds.advance(11)
+    rounds.advance(12)
 
     def bias_sum(*grads):
         total = sum(column_sum(part) for part in grads)
@@ -798,14 +799,15 @@
     far_trade = rounds.start(
         remote(r.far_part.at[give], r.far_half, r.s_out.at[4], r.s_in.at[4], core_peer)
     )
-    rounds.advance(12)
+    rounds.advance(13)
     far_trade.wait_recv()
     r.far_send[...] = (r.far_part[keep, :].astype(F32) + r.far_half[...].astype(F32)).astype(BF16)
     owner = {"tensor": (1 - side) * 2 + side}
     rounds.start(remote(r.far_send, r.far_in.at[core], r.o_out, r.o_in.at[core], owner))
 
+    rounds.advance(14)
     trade_rows(input_rows, keep_first)
-    rounds.advance(13)
+    rounds.advance(15)
 
     total = r.tiny[place]
     for step in (1, 2, 3):
@@ -821,10 +823,10 @@
     lax.fori_loop(1, groups, tell, 0)
 
     def pump(n, _):
-        rounds.advance(n, 14)
+        rounds.advance(n, 16)
         return 0
 
-    lax.fori_loop(14, PIECES, pump, 0)
+    lax.fori_loop(16, PIECES, pump, 0)
     rounds.advance(PIECES)
 
     for n in range(PIECES + 1, PIECES + LAGS[0] - 2):

time: 204 us -> 193 us (0.946)
  Pallas kernels: 203 us -> 192 us
    pallas_call x1, Pallas kernels: 198 us -> 187 us  [layer(): pl.pallas_call(functools.partial(layer_kernel, groups, names), out_shape=...]
where the time goes in v7:
time: 193 us
  Pallas kernels  192 us (99%)
    pallas_call x1, Pallas kernels, layer(): pl.pallas_call(functools.partial(layer_kernel, groups, names), out_shape=...  187 us
    pallas_call x1, Pallas kernels, last(): pl.pallas_call(last_kernel, out_shape=outs, in_specs=[anywhere] * 4, out_...  5.05 us

profile of v7, /device:TPU:0, one launch (start us, length us, event | category | flops | bytes accessed | tf_op | source)
XLA Modules:
  0.0 193.3 jit_solution(16246860995111944108)
XLA Ops:
  0.7 187.4 %shard_map.314 = (bf16[640,768]{1,0:T(8,128)(2,1)}, bf16[640,768]{1,0:T(8,128)(2,1)}, bf16[6,2,3,4,16,768]{5,4,3,2,1,0:T(8,128)(2,1)}, f32[8,768]{1,0:T(8,128)}) custom-call(bf16[640,768]{1,0:T(8,128)(2,1)} %refs_0_.1, bf16[3,64,768]{2,1,0:T(8,128)(2,1)} %bitcast.15, bf16[3,64,768]{2,1,0:T(8,128)(2,1)} %bitcast.16, bf16[3,64,768]{2,1,0:T(8,128)(2,1)} %bitcast.17, ...), custom_call_target="tpu_custom_call" | custom-call | tf_op jit(solution)/shard_map/pallas_call | solution.py:960
  188.1 5.0 %shard_map.315 = (bf16[640,768]{1,0:T(8,128)(2,1)}, bf16[640,768]{1,0:T(8,128)(2,1)}, f32[768,768]{1,0:T(8,128)}, f32[768,768]{1,0:T(8,128)}, f32[192,768]{1,0:T...) custom-call(bf16[12,192,768]{2,1,0:T(8,128)(2,1)} %bitcast.14, ...), custom_call_target="tpu_custom_call" | custom-call | tf_op jit(solution)/shard_map/pallas_call | solution.py:1016
